TPU v7x, 32 devices: a whole 2x2x4 slice. The times are simulated.
32 devices in a mesh: wide: 8 (over z, y), narrow: 4 (over x, core).
Axes of the slice: x: 2, y: 2, z: 4, core: 2. Of those that a mesh axis runs over, the one named last changes fastest.
Arguments:
- x_prefix: bfloat16 [2048, 2048], P(('wide', 'narrow')), may hold values from -6 to 6
- x_action: bfloat16 [2048, 1024], P(('wide', 'narrow')), may hold values from -6 to 6
- cot_prefix: bfloat16 [2048, 2048], P(('wide', 'narrow')), may hold values from -6 to 6
- cot_action: bfloat16 [2048, 1024], P(('wide', 'narrow')), may hold values from -6 to 6
- prefix_block: int32 [8, 256], P('wide'), may hold values from 0 to 3, never falling along the last dimension, each value on 1 to 128 neighbouring positions
- action_block: int32 [8, 256], P('wide'), may hold values from 0 to 1, never falling along the last dimension, each value on 1 to 255 neighbouring positions
- valid_len: int32 [8], P('wide'), may hold values from 128 to 256
- mix_weight: float32 [8], P('wide'), may hold values from 0.25 to 4
- wq_prefix: bfloat16 [2048, 2048], P('wide', 'narrow'), may hold values from -0.125 to 0.125
- wk_prefix: bfloat16 [2048, 256], P(('wide', 'narrow')), may hold values from -0.125 to 0.125
- wv_prefix: bfloat16 [2048, 256], P(('wide', 'narrow')), may hold values from -0.125 to 0.125
- wo_prefix: bfloat16 [2048, 2048], P('narrow', 'wide'), may hold values from -2 to 2
- wg_prefix: bfloat16 [2048, 16384], P('wide', 'narrow'), may hold values from -0.125 to 0.125
- wu_prefix: bfloat16 [2048, 16384], P('wide', 'narrow'), may hold values from -0.125 to 0.125
- wd_prefix: bfloat16 [16384, 2048], P('narrow', 'wide'), may hold values from -0.046875 to 0.046875
- norm1_prefix: bfloat16 [2048], P(('wide', 'narrow')), may hold values from 0.099609375 to 1.8984375
- norm2_prefix: bfloat16 [2048], P(('wide', 'narrow')), may hold values from 0.099609375 to 1.8984375
- wq_action: bfloat16 [1024, 2048], P('wide', 'narrow'), may hold values from -0.1875 to 0.1875
- wk_action: bfloat16 [1024, 256], P(('wide', 'narrow')), may hold values from -0.1875 to 0.1875
- wv_action: bfloat16 [1024, 256], P(('wide', 'narrow')), may hold values from -0.1875 to 0.1875
- wo_action: bfloat16 [2048, 1024], P('narrow', 'wide'), may hold values from -2 to 2
- wg_action: bfloat16 [1024, 4096], P('wide', 'narrow'), may hold values from -0.1875 to 0.1875
- wu_action: bfloat16 [1024, 4096], P('wide', 'narrow'), may hold values from -0.1875 to 0.1875
- wd_action: bfloat16 [4096, 1024], P('narrow', 'wide'), may hold values from -0.09375 to 0.09375
- norm1_action: bfloat16 [1024], P(('wide', 'narrow')), may hold values from 0.099609375 to 1.8984375
- norm2_action: bfloat16 [1024], P(('wide', 'narrow')), may hold values from 0.099609375 to 1.8984375
Outputs:
- out_prefix: bfloat16 [2048, 2048], P(('wide', 'narrow'))
- out_action: bfloat16 [2048, 1024], P(('wide', 'narrow'))
- grad_x_prefix: float32 [2048, 2048], P(('wide', 'narrow'))
- grad_x_action: float32 [2048, 1024], P(('wide', 'narrow'))
- grad_wq_prefix: float32 [2048, 2048], P('wide', 'narrow')
- grad_wk_prefix: float32 [2048, 256], P(('wide', 'narrow'))
- grad_wv_prefix: float32 [2048, 256], P(('wide', 'narrow'))
- grad_wo_prefix: float32 [2048, 2048], P('narrow', 'wide')
- grad_wg_prefix: float32 [2048, 16384], P('wide', 'narrow')
- grad_wu_prefix: float32 [2048, 16384], P('wide', 'narrow')
- grad_wd_prefix: float32 [16384, 2048], P('narrow', 'wide')
- grad_norm1_prefix: float32 [2048], P(('wide', 'narrow'))
- grad_norm2_prefix: float32 [2048], P(('wide', 'narrow'))
- grad_wq_action: float32 [1024, 2048], P('wide', 'narrow')
- grad_wk_action: float32 [1024, 256], P(('wide', 'narrow'))
- grad_wv_action: float32 [1024, 256], P(('wide', 'narrow'))
- grad_wo_action: float32 [2048, 1024], P('narrow', 'wide')
- grad_wg_action: float32 [1024, 4096], P('wide', 'narrow')
- grad_wu_action: float32 [1024, 4096], P('wide', 'narrow')
- grad_wd_action: float32 [4096, 1024], P('narrow', 'wide')
- grad_norm1_action: float32 [1024], P(('wide', 'narrow'))
- grad_norm2_action: float32 [1024], P(('wide', 'narrow'))
Inputs may be any that keep to these rules, and one draw needn't show every extreme that they name: `prefix_block`: within an item the prefix block ids never fall along the tokens, and each of the 4 ids labels at least one token. `action_block`: within an item the action block ids never fall along the tokens, and both ids label at least one token. Prefix keys of an item at positions from valid_len on are padding.
All inputs are finite; a program needn't handle non-finite values.
Results may differ from a plain program's by a relative error of at most 0.018.
Values may be sent and summed in bfloat16 or wider, within the bound.
No kernel may reach another device: no remote copies, remote signals or barrier semaphores. Data moves between devices by JAX's collectives and lax.ppermute only.
A program may use at most 320 MiB of HBM per device.

v0:
```python
import jax
import jax.numpy as jnp
from jax import lax
from jax.sharding import PartitionSpec as P

PREFIX_BLOCKS = 4


epsilon = 1e-06
scaling = 0.0625
masked_score = -1e30


def rms_norm(features, weight):
    return (
        features
        * lax.rsqrt(jnp.mean(features * features, axis=-1, keepdims=True) + epsilon)
        * weight
    )


def product(former, latter):
    return jnp.dot(former, latter, preferred_element_type=jnp.float32)


def rows_contract(former, latter):
    return lax.dot_general(
        former, latter, (((0,), (0,)), ((), ())), preferred_element_type=jnp.float32
    )


def cols_contract(former, latter):
    return lax.dot_general(
        former, latter, (((1,), (1,)), ((), ())), preferred_element_type=jnp.float32
    )


def geglu(gate_rows, uppers):
    return jax.nn.gelu(gate_rows, approximate=True) * uppers


def norm_back(features, weight, upstream):
    unused, pullback = jax.vjp(rms_norm, features, weight)
    return pullback(upstream)


def projection(gathered, stream, which):
    return gathered[5 * stream + which]


def masked_scores(queries, key_rows, allowed):
    scores = jnp.einsum("qhd,kd->hqk", queries, key_rows, preferred_element_type=jnp.float32)
    return jnp.where(allowed[None], scores, masked_score)


def local(
    x_prefix,
    x_action,
    cot_prefix,
    cot_action,
    prefix_block,
    action_block,
    valid_len,
    mix_weight,
    wq_prefix,
    wk_prefix,
    wv_prefix,
    wo_prefix,
    wg_prefix,
    wu_prefix,
    wd_prefix,
    norm1_prefix,
    norm2_prefix,
    wq_action,
    wk_action,
    wv_action,
    wo_action,
    wg_action,
    wu_action,
    wd_action,
    norm1_action,
    norm2_action,
):
    compact = (
        lax.all_gather(wk_prefix, ("wide", "narrow"), axis=0, tiled=True),
        lax.all_gather(wv_prefix, ("wide", "narrow"), axis=0, tiled=True),
        lax.all_gather(norm1_prefix, ("wide", "narrow"), axis=0, tiled=True),
        lax.all_gather(norm2_prefix, ("wide", "narrow"), axis=0, tiled=True),
        lax.all_gather(wk_action, ("wide", "narrow"), axis=0, tiled=True),
        lax.all_gather(wv_action, ("wide", "narrow"), axis=0, tiled=True),
        lax.all_gather(norm1_action, ("wide", "narrow"), axis=0, tiled=True),
        lax.all_gather(norm2_action, ("wide", "narrow"), axis=0, tiled=True),
    )
    head_dim = compact[0].shape[1]
    keyval_weight = [
        jnp.concatenate([compact[0], compact[1]], axis=1),
        jnp.concatenate([compact[4], compact[5]], axis=1),
    ]
    first_gain = [compact[2].astype(jnp.float32), compact[6].astype(jnp.float32)]
    second_gain = [compact[3].astype(jnp.float32), compact[7].astype(jnp.float32)]
    gathered = (
        lax.all_gather(wq_prefix, "wide", axis=0, tiled=True),
        lax.all_gather(wo_prefix, "wide", axis=1, tiled=True),
        lax.all_gather(wg_prefix, "wide", axis=0, tiled=True),
        lax.all_gather(wu_prefix, "wide", axis=0, tiled=True),
        lax.all_gather(wd_prefix, "wide", axis=1, tiled=True),
        lax.all_gather(wq_action, "wide", axis=0, tiled=True),
        lax.all_gather(wo_action, "wide", axis=1, tiled=True),
        lax.all_gather(wg_action, "wide", axis=0, tiled=True),
        lax.all_gather(wu_action, "wide", axis=0, tiled=True),
        lax.all_gather(wd_action, "wide", axis=1, tiled=True),
    )
    inputs = [x_prefix.astype(jnp.float32), x_action.astype(jnp.float32)]
    normed = [
        rms_norm(inputs[stream], first_gain[stream]).astype(jnp.bfloat16) for stream in range(2)
    ]
    keyval = [
        product(normed[stream], keyval_weight[stream]).astype(jnp.bfloat16) for stream in range(2)
    ]
    all_normed = (
        lax.all_gather(normed[0], "narrow", axis=0, tiled=True),
        lax.all_gather(normed[1], "narrow", axis=0, tiled=True),
    )
    all_keyval = (
        lax.all_gather(keyval[0], "narrow", axis=0, tiled=True),
        lax.all_gather(keyval[1], "narrow", axis=0, tiled=True),
    )
    prefix_len = all_normed[0].shape[0]
    total_rows = prefix_len + all_normed[1].shape[0]
    joined = jnp.concatenate([all_keyval[0], all_keyval[1]], axis=0)
    key_rows = joined[:, :head_dim]
    values = joined[:, head_dim:]
    queries = jnp.concatenate(
        [
            (product(all_normed[stream], projection(gathered, stream, 0)) * scaling).astype(
                jnp.bfloat16
            )
            for stream in range(2)
        ],
        axis=0,
    ).reshape(total_rows, -1, head_dim)
    blocks = jnp.concatenate([prefix_block[0], action_block[0] + PREFIX_BLOCKS])
    usable = jnp.concatenate(
        [
            jnp.arange(prefix_len, dtype=jnp.int32) < valid_len[0],
            jnp.ones((total_rows - prefix_len,), dtype=jnp.bool_),
        ]
    )
    allowed = (blocks[None, :] <= blocks[:, None]) & usable[None, :]
    scores = masked_scores(queries, key_rows, allowed)
    highest = jnp.max(scores, axis=-1, keepdims=True)
    exponent = jnp.exp(scores - highest)
    denominator = jnp.sum(exponent, axis=-1, keepdims=True)
    log_total = highest + jnp.log(denominator)
    attention = (exponent / denominator).astype(jnp.bfloat16)
    mixed_all = jnp.einsum("hqk,kd->qhd", attention, values, preferred_element_type=jnp.float32)
    mixed_all = mixed_all.astype(jnp.bfloat16).reshape(total_rows, -1)
    mixed_rows = [mixed_all[:prefix_len], mixed_all[prefix_len:]]
    attn_terms = [
        product(mixed_rows[stream], projection(gathered, stream, 1)) for stream in range(2)
    ]
    attended = (
        lax.psum_scatter(attn_terms[0], "narrow", scatter_dimension=0, tiled=True),
        lax.psum_scatter(attn_terms[1], "narrow", scatter_dimension=0, tiled=True),
    )
    middle = [inputs[stream] + attended[stream] for stream in range(2)]
    normed2 = [
        rms_norm(middle[stream], second_gain[stream]).astype(jnp.bfloat16) for stream in range(2)
    ]
    all_normed2 = (
        lax.all_gather(normed2[0], "narrow", axis=0, tiled=True),
        lax.all_gather(normed2[1], "narrow", axis=0, tiled=True),
    )
    gate_rows = [
        product(all_normed2[stream], projection(gathered, stream, 2)) for stream in range(2)
    ]
    uppers = [product(all_normed2[stream], projection(gathered, stream, 3)) for stream in range(2)]
    hidden = [geglu(gate_rows[stream], uppers[stream]).astype(jnp.bfloat16) for stream in range(2)]
    mlp_terms = [product(hidden[stream], projection(gathered, stream, 4)) for stream in range(2)]
    mlp_out = (
        lax.psum_scatter(
            mlp_terms[0].astype(jnp.bfloat16), "narrow", scatter_dimension=0, tiled=True
        ).astype(jnp.float32),
        lax.psum_scatter(
            mlp_terms[1].astype(jnp.bfloat16), "narrow", scatter_dimension=0, tiled=True
        ).astype(jnp.float32),
    )
    outputs = [(middle[stream] + mlp_out[stream]).astype(jnp.bfloat16) for stream in range(2)]
    item_weight = mix_weight[0]
    dout = [
        cot_prefix.astype(jnp.float32) * item_weight,
        cot_action.astype(jnp.float32) * item_weight,
    ]
    grad_mlp = (
        lax.all_gather(dout[0].astype(jnp.bfloat16), "narrow", axis=0, tiled=True),
        lax.all_gather(dout[1].astype(jnp.bfloat16), "narrow", axis=0, tiled=True),
    )
    grad_down = [rows_contract(hidden[stream], grad_mlp[stream]) for stream in range(2)]
    grad_gate = []
    grad_up = []
    for stream in range(2):
        dhidden = cols_contract(grad_mlp[stream], projection(gathered, stream, 4))
        unused, pullback = jax.vjp(geglu, gate_rows[stream], uppers[stream])
        gate_part, up_part = pullback(dhidden)
        grad_gate.append(gate_part.astype(jnp.bfloat16))
        grad_up.append(up_part.astype(jnp.bfloat16))
    grad_gate_w = [rows_contract(all_normed2[stream], grad_gate[stream]) for stream in range(2)]
    grad_up_w = [rows_contract(all_normed2[stream], grad_up[stream]) for stream in range(2)]
    dnormed2_terms = [
        cols_contract(grad_gate[stream], projection(gathered, stream, 2))
        + cols_contract(grad_up[stream], projection(gathered, stream, 3))
        for stream in range(2)
    ]
    dnormed2 = (
        lax.psum_scatter(dnormed2_terms[0], "narrow", scatter_dimension=0, tiled=True),
        lax.psum_scatter(dnormed2_terms[1], "narrow", scatter_dimension=0, tiled=True),
    )
    dmiddle = []
    grad_second = []
    for stream in range(2):
        from_norm, gain_part = norm_back(middle[stream], second_gain[stream], dnormed2[stream])
        dmiddle.append(dout[stream] + from_norm)
        grad_second.append(gain_part)
    grad_att = (
        lax.all_gather(dmiddle[0].astype(jnp.bfloat16), "narrow", axis=0, tiled=True),
        lax.all_gather(dmiddle[1].astype(jnp.bfloat16), "narrow", axis=0, tiled=True),
    )
    grad_out_w = [rows_contract(mixed_rows[stream], grad_att[stream]) for stream in range(2)]
    dmixed = jnp.concatenate(
        [cols_contract(grad_att[stream], projection(gathered, stream, 1)) for stream in range(2)],
        axis=0,
    )
    dmixed = dmixed.astype(jnp.bfloat16).reshape(total_rows, -1, head_dim)
    recomputed = jnp.exp(masked_scores(queries, key_rows, allowed) - log_total)
    dprobs = jnp.einsum("qhd,kd->hqk", dmixed, values, preferred_element_type=jnp.float32)
    row_inner = jnp.sum(recomputed * dprobs, axis=-1, keepdims=True)
    dscores = (recomputed * (dprobs - row_inner)).astype(jnp.bfloat16)
    dquery = jnp.einsum("hqk,kd->qhd", dscores, key_rows, preferred_element_type=jnp.float32)
    dquery = (dquery.astype(jnp.bfloat16) * scaling).reshape(total_rows, -1)
    grad_key = jnp.einsum("hqk,qhd->kd", dscores, queries, preferred_element_type=jnp.float32)
    dvalue = jnp.einsum(
        "hqk,qhd->kd", recomputed.astype(jnp.bfloat16), dmixed, preferred_element_type=jnp.float32
    )
    grad_keyval = jnp.concatenate([grad_key, dvalue], axis=1)
    dquery_rows = [dquery[:prefix_len], dquery[prefix_len:]]
    grad_query_w = [rows_contract(all_normed[stream], dquery_rows[stream]) for stream in range(2)]
    dnormed_terms = [
        cols_contract(dquery_rows[stream], projection(gathered, stream, 0)) for stream in range(2)
    ]
    summed = (
        lax.psum_scatter(
            dnormed_terms[0].astype(jnp.bfloat16), "narrow", scatter_dimension=0, tiled=True
        ).astype(jnp.float32),
        lax.psum_scatter(
            dnormed_terms[1].astype(jnp.bfloat16), "narrow", scatter_dimension=0, tiled=True
        ).astype(jnp.float32),
        lax.psum_scatter(
            grad_keyval[:prefix_len].astype(jnp.bfloat16), "narrow", scatter_dimension=0, tiled=True
        ).astype(jnp.float32),
        lax.psum_scatter(
            grad_keyval[prefix_len:].astype(jnp.bfloat16), "narrow", scatter_dimension=0, tiled=True
        ).astype(jnp.float32),
    )
    grad_inputs = []
    grad_first = []
    grad_keyval_w = []
    for stream in range(2):
        own_keyval = summed[2 + stream].astype(jnp.bfloat16)
        grad_keyval_w.append(rows_contract(normed[stream], own_keyval))
        dnormed = summed[stream] + cols_contract(own_keyval, keyval_weight[stream])
        from_norm, gain_part = norm_back(inputs[stream], first_gain[stream], dnormed)
        grad_inputs.append(dmiddle[stream] + from_norm)
        grad_first.append(gain_part)
    wide_grads = (
        lax.psum_scatter(
            grad_query_w[0].astype(jnp.bfloat16), "wide", scatter_dimension=0, tiled=True
        ).astype(jnp.float32),
        lax.psum_scatter(
            grad_out_w[0].astype(jnp.bfloat16), "wide", scatter_dimension=1, tiled=True
        ).astype(jnp.float32),
        lax.psum_scatter(
            grad_gate_w[0].astype(jnp.bfloat16), "wide", scatter_dimension=0, tiled=True
        ).astype(jnp.float32),
        lax.psum_scatter(
            grad_up_w[0].astype(jnp.bfloat16), "wide", scatter_dimension=0, tiled=True
        ).astype(jnp.float32),
        lax.psum_scatter(
            grad_down[0].astype(jnp.bfloat16), "wide", scatter_dimension=1, tiled=True
        ).astype(jnp.float32),
        lax.psum_scatter(
            grad_query_w[1].astype(jnp.bfloat16), "wide", scatter_dimension=0, tiled=True
        ).astype(jnp.float32),
        lax.psum_scatter(
            grad_out_w[1].astype(jnp.bfloat16), "wide", scatter_dimension=1, tiled=True
        ).astype(jnp.float32),
        lax.psum_scatter(
            grad_gate_w[1].astype(jnp.bfloat16), "wide", scatter_dimension=0, tiled=True
        ).astype(jnp.float32),
        lax.psum_scatter(
            grad_up_w[1].astype(jnp.bfloat16), "wide", scatter_dimension=0, tiled=True
        ).astype(jnp.float32),
        lax.psum_scatter(
            grad_down[1].astype(jnp.bfloat16), "wide", scatter_dimension=1, tiled=True
        ).astype(jnp.float32),
    )
    small_grads = (
        lax.psum_scatter(
            grad_keyval_w[0][:, :head_dim], ("wide", "narrow"), scatter_dimension=0, tiled=True
        ),
        lax.psum_scatter(
            grad_keyval_w[0][:, head_dim:], ("wide", "narrow"), scatter_dimension=0, tiled=True
        ),
        lax.psum_scatter(grad_first[0], ("wide", "narrow"), scatter_dimension=0, tiled=True),
        lax.psum_scatter(grad_second[0], ("wide", "narrow"), scatter_dimension=0, tiled=True),
        lax.psum_scatter(
            grad_keyval_w[1][:, :head_dim], ("wide", "narrow"), scatter_dimension=0, tiled=True
        ),
        lax.psum_scatter(
            grad_keyval_w[1][:, head_dim:], ("wide", "narrow"), scatter_dimension=0, tiled=True
        ),
        lax.psum_scatter(grad_first[1], ("wide", "narrow"), scatter_dimension=0, tiled=True),
        lax.psum_scatter(grad_second[1], ("wide", "narrow"), scatter_dimension=0, tiled=True),
    )
    return (
        outputs[0],
        outputs[1],
        grad_inputs[0],
        grad_inputs[1],
        wide_grads[0],
        small_grads[0],
        small_grads[1],
        wide_grads[1],
        wide_grads[2],
        wide_grads[3],
        wide_grads[4],
        small_grads[2],
        small_grads[3],
        wide_grads[5],
        small_grads[4],
        small_grads[5],
        wide_grads[6],
        wide_grads[7],
        wide_grads[8],
        wide_grads[9],
        small_grads[6],
        small_grads[7],
    )


def solution(mesh):
    return jax.shard_map(
        local,
        mesh=mesh,
        in_specs=(
            P(("wide", "narrow"), None),
            P(("wide", "narrow"), None),
            P(("wide", "narrow"), None),
            P(("wide", "narrow"), None),
            P("wide", None),
            P("wide", None),
            P("wide"),
            P("wide"),
            P("wide", "narrow"),
            P(("wide", "narrow"), None),
            P(("wide", "narrow"), None),
            P("narrow", "wide"),
            P("wide", "narrow"),
            P("wide", "narrow"),
            P("narrow", "wide"),
            P(("wide", "narrow")),
            P(("wide", "narrow")),
            P("wide", "narrow"),
            P(("wide", "narrow"), None),
            P(("wide", "narrow"), None),
            P("narrow", "wide"),
            P("wide", "narrow"),
            P("wide", "narrow"),
            P("narrow", "wide"),
            P(("wide", "narrow")),
            P(("wide", "narrow")),
        ),
        out_specs=(
            P(("wide", "narrow"), None),
            P(("wide", "narrow"), None),
            P(("wide", "narrow"), None),
            P(("wide", "narrow"), None),
            P("wide", "narrow"),
            P(("wide", "narrow"), None),
            P(("wide", "narrow"), None),
            P("narrow", "wide"),
            P("wide", "narrow"),
            P("wide", "narrow"),
            P("narrow", "wide"),
            P(("wide", "narrow")),
            P(("wide", "narrow")),
            P("wide", "narrow"),
            P(("wide", "narrow"), None),
            P(("wide", "narrow"), None),
            P("narrow", "wide"),
            P("wide", "narrow"),
            P("wide", "narrow"),
            P("narrow", "wide"),
            P(("wide", "narrow")),
            P(("wide", "narrow")),
        ),
        check_vma=False,
    )
```

profile of v0, /device:TPU:0, one launch (start us, length us, event | category | flops | bytes accessed | tf_op | source)
XLA Modules:
  0.0 3389.1 jit_solution(16721079745106572148)
XLA Ops:
  12.9 42.5 %all-reduce.10 = (bf16[1024]{0:T(1024)(128)(2,1)S(1)}, bf16[2048]{0:T(1024)(128)(2,1)S(1)}, bf16[2048]{0:T(1024)(128)(2,1)}, bf16[1024]{0:T(1024)(128)(2,1)}) all-reduce(bf16[1024]{0:T(1024)(128)(2,1)S(1)} %dynamic-update-slice.1, bf16[2048]{0:T(1024)(128)(2,1)S(1)} %dynamic-update-slice, ...), channel_id=1, replica_groups=mesh['wide'=8,'narrow'=4] {'wide','narrow'}, use_global_device_ids=true, to_apply=%add.2 | all-reduce | flops 6144 | bytes 24576
  62.5 42.8 %all_gather.89 = bf16[1024,256]{1,0:T(8,128)(2,1)S(1)} all-gather(bf16[32,256]{1,0:T(8,128)(2,1)} %param.44), channel_id=1, replica_groups=mesh['wide'=8,'narrow'=4] {'wide','narrow'}, dimensions={0}, use_global_device_ids=true | all-gather | bytes 540672 | tf_op jit(solution)/shard_map/all_gather | solution.py:89
  105.4 38.1 %all_gather.90 = bf16[1024,256]{1,0:T(8,128)(2,1)S(1)} all-gather(bf16[32,256]{1,0:T(8,128)(2,1)S(1)} %copy-done.53), channel_id=1, replica_groups=mesh['wide'=8,'narrow'=4] {'wide','narrow'}, dimensions={0}, use_global_device_ids=true | all-gather | bytes 540672 | tf_op jit(solution)/shard_map/all_gather | solution.py:90
  145.0 6.0 all_gather.91
  151.0 7.5 all_gather.94
  166.1 5.8 all_gather.87
  171.9 11.3 all-gather.21.cloned.1.call-done
  183.3 51.3 %all-gather.23.cloned.1.call-done = bf16[2048,512]{1,0:T(8,128)(2,1)} async-done(((bf16[256,512]{1,0:T(8,128)(2,1)}), bf16[2048,512]{1,0:T(8,128)(2,1)}) %all-gather.23.cloned.1.call-update) | async-done | bytes 2097168 | tf_op jit(solution)/shard_map/all_gather | solution.py:102
  240.5 45.5 %all-gather.27.cloned.1.call-done = bf16[512,2048]{1,0:T(8,128)(2,1)} async-done(((bf16[512,256]{1,0:T(8,128)(2,1)}), bf16[512,2048]{1,0:T(8,128)(2,1)}) %all-gather.27.cloned.1.call-update) | async-done | bytes 2097168 | tf_op jit(solution)/shard_map/all_gather | solution.py:103
  286.0 3.6 fusion.63
  290.5 28.9 reduce-scatter.33.cloned.1.call-done
  325.2 36.1 %all-gather.37.cloned.1.call-done = bf16[512,1024]{1,0:T(8,128)(2,1)} async-done(((bf16[512,128]{1,0:T(8,128)(2,1)}), bf16[512,1024]{1,0:T(8,128)(2,1)}) %all-gather.37.cloned.1.call-update) | async-done | bytes 1048592 | tf_op jit(solution)/shard_map/all_gather | solution.py:108
  366.0 13.2 all-gather.29.cloned.1.call-done
  379.1 229.8 %all-gather.31.cloned.1.call-done = bf16[2048,4096]{1,0:T(8,128)(2,1)} async-done(((bf16[256,4096]{1,0:T(8,128)(2,1)}), bf16[2048,4096]{1,0:T(8,128)(2,1)}) %all-gather.31.cloned.1.call-update) | async-done | bytes 16777232 | tf_op jit(solution)/shard_map/all_gather | solution.py:104
  609.0 12.7 fusion.64
  621.7 215.5 %all-gather.33.cloned.1.call-done = bf16[2048,4096]{1,0:T(8,128)(2,1)} async-done(((bf16[256,4096]{1,0:T(8,128)(2,1)}), bf16[2048,4096]{1,0:T(8,128)(2,1)}) %all-gather.33.cloned.1.call-update) | async-done | bytes 16777232 | tf_op jit(solution)/shard_map/all_gather | solution.py:105
  837.2 12.6 fusion.65
  849.8 4.4 all-gather.45.cloned.1.call-done
  854.2 230.0 %all-gather.35.cloned.1.call-done = bf16[4096,2048]{1,0:T(8,128)(2,1)} async-done(((bf16[4096,256]{1,0:T(8,128)(2,1)}), bf16[4096,2048]{1,0:T(8,128)(2,1)}) %all-gather.35.cloned.1.call-update) | async-done | bytes 16777232 | tf_op jit(solution)/shard_map/all_gather | solution.py:106
  1084.2 15.1 multiply_convert_fusion
  1099.3 12.4 fusion.69
  1111.7 12.8 convolution_add_fusion
  1125.5 7.8 all_gather.110
  1135.2 7.3 all_gather.104
  1142.5 18.7 all-gather.39.cloned.1.call-done
  1161.1 3.3 fusion.67
  1164.4 46.5 %all-gather.41.cloned.1.call-done = bf16[1024,1024]{1,0:T(8,128)(2,1)} async-done(((bf16[128,1024]{1,0:T(8,128)(2,1)}), bf16[1024,1024]{1,0:T(8,128)(2,1)}) %all-gather.41.cloned.1.call-update) | async-done | bytes 2097168 | tf_op jit(solution)/shard_map/all_gather | solution.py:110
  1210.9 3.3 fusion.68
  1214.2 48.2 %all-gather.43.cloned.1.call-done = bf16[1024,1024]{1,0:T(8,128)(2,1)} async-done(((bf16[1024,128]{1,0:T(8,128)(2,1)}), bf16[1024,1024]{1,0:T(8,128)(2,1)}) %all-gather.43.cloned.1.call-update) | async-done | bytes 2097168 | tf_op jit(solution)/shard_map/all_gather | solution.py:111
  1262.4 4.7 multiply_convert_fusion.2
  1271.0 24.0 reduce-scatter.41.cloned.1.call-done
  1301.3 21.8 reduce-scatter.43.cloned.1.call-done
  1327.3 6.8 all_gather.111
  1337.3 4.7 all-gather.47.cloned.1.call-done
  1341.9 2.7 convolution_convert_fusion.17
  1365.5 3.4 convolution_convert_fusion.15
  1373.6 9.3 convolution_convert_fusion.6
  1383.0 3.4 convolution_convert_fusion.4
  1388.6 9.8 convolution_convert_fusion.2
  1398.5 9.8 convolution_convert_fusion.1
  1409.9 9.7 convolution_convert_fusion
  1428.9 35.3 %reduce-scatter.79.cloned.1.call-done = bf16[128,1024]{1,0:T(8,128)(2,1)} async-done(((bf16[1024,1024]{1,0:T(8,128)(2,1)}), bf16[128,1024]{1,0:T(8,128)(2,1)}) %reduce-scatter.79.cloned.1.call-update) | async-done | bytes 262160
  1466.2 68.5 %reduce-scatter.69.cloned.1.call-done = bf16[128,1024]{1,0:T(8,128)(2,1)} async-done(((bf16[1024,1024]{1,0:T(8,128)(2,1)}), bf16[128,1024]{1,0:T(8,128)(2,1)}) %reduce-scatter.69.cloned.1.call-update) | async-done | bytes 262160 | tf_op jit(solution)/shard_map/reduce_scatter | solution.py:296
  1536.5 68.8 %reduce-scatter.71.cloned.1.call-done = bf16[128,1024]{1,0:T(8,128)(2,1)} async-done(((bf16[1024,1024]{1,0:T(8,128)(2,1)}), bf16[128,1024]{1,0:T(8,128)(2,1)}) %reduce-scatter.71.cloned.1.call-update) | async-done | bytes 262160 | tf_op jit(solution)/shard_map/reduce_scatter | solution.py:299
  1607.1 63.9 %reduce-scatter.77.cloned.1.call-done = bf16[128,512]{1,0:T(8,128)(2,1)} async-done(((bf16[1024,512]{1,0:T(8,128)(2,1)}), bf16[128,512]{1,0:T(8,128)(2,1)}) %reduce-scatter.77.cloned.1.call-update) | async-done | bytes 131088
  1674.3 20.5 reduce-scatter.47.cloned.1.call-done
  1694.8 3.0 fusion.42
  1698.9 20.6 reduce-scatter.39.cloned.1.call-done
  1721.6 25.6 reduce-scatter.45.cloned.1.call-done
  1749.9 40.0 %all-reduce.9 = (f32[2048]{0:T(1024)S(1)}, f32[2048]{0:T(1024)S(1)}, f32[1024]{0:T(1024)S(1)}, f32[1024]{0:T(1024)S(1)}) all-reduce(f32[2048]{0:T(1024)S(1)} %get-tuple-element.24, f32[2048]{0:T(1024)S(1)} %copy-done.49, f32[1024]{0:T(1024)S(1)} %copy-done.52, ...), channel_id=19, replica_groups=mesh['wide'=8,'narrow'=4] {'wide','narrow'}, use_global_device_ids=true, to_apply=%region_29.30.clone | all-reduce | flops 6144 | bytes 49152
  1792.2 21.8 reduce-scatter.63.cloned.1.call-done
  1815.7 25.0 reduce-scatter.35.cloned.1.call-done
  1843.1 69.6 %reduce-scatter.49.cloned.1.call-done = bf16[256,512]{1,0:T(8,128)(2,1)} async-done(((bf16[2048,512]{1,0:T(8,128)(2,1)}), bf16[256,512]{1,0:T(8,128)(2,1)}) %reduce-scatter.49.cloned.1.call-update) | async-done | bytes 262160 | tf_op jit(solution)/shard_map/reduce_scatter | solution.py:275
  1914.5 69.3 %reduce-scatter.55.cloned.1.call-done = bf16[512,256]{1,0:T(8,128)(2,1)} async-done(((bf16[512,2048]{1,0:T(8,128)(2,1)}), bf16[512,256]{1,0:T(8,128)(2,1)}) %reduce-scatter.55.cloned.1.call-update) | async-done | bytes 262160 | tf_op jit(solution)/shard_map/reduce_scatter | solution.py:278
  1985.6 283.8 %reduce-scatter.57.cloned.1.call-done = bf16[256,4096]{1,0:T(8,128)(2,1)} async-done(((bf16[2048,4096]{1,0:T(8,128)(2,1)}), bf16[256,4096]{1,0:T(8,128)(2,1)}) %reduce-scatter.57.cloned.1.call-update) | async-done | bytes 2097168 | tf_op jit(solution)/shard_map/reduce_scatter | solution.py:281
  2269.3 4.1 convert_element_type.242
  2273.4 281.9 %reduce-scatter.59.cloned.1.call-done = bf16[256,4096]{1,0:T(8,128)(2,1)} async-done(((bf16[2048,4096]{1,0:T(8,128)(2,1)}), bf16[256,4096]{1,0:T(8,128)(2,1)}) %reduce-scatter.59.cloned.1.call-update) | async-done | bytes 2097168 | tf_op jit(solution)/shard_map/reduce_scatter | solution.py:284
  2555.4 4.1 convert_element_type.244
  2559.5 281.3 %reduce-scatter.61.cloned.1.call-done = bf16[4096,256]{1,0:T(8,128)(2,1)} async-done(((bf16[4096,2048]{1,0:T(8,128)(2,1)}), bf16[4096,256]{1,0:T(8,128)(2,1)}) %reduce-scatter.61.cloned.1.call-update) | async-done | bytes 2097168 | tf_op jit(solution)/shard_map/reduce_scatter | solution.py:287
  2840.8 3.9 convert_element_type.246
  2844.7 132.7 %reduce-scatter.65.cloned.1.call-done = f32[32,256]{1,0:T(8,128)} async-done(((f32[1024,256]{1,0:T(8,128)}), f32[32,256]{1,0:T(8,128)}) %reduce-scatter.65.cloned.1.call-update) | async-done | bytes 32784 | tf_op jit(solution)/shard_map/reduce_scatter | solution.py:315
  2977.4 133.5 %reduce-scatter.67.cloned.1.call-done = f32[32,256]{1,0:T(8,128)} async-done(((f32[1024,256]{1,0:T(8,128)}), f32[32,256]{1,0:T(8,128)}) %reduce-scatter.67.cloned.1.call-update) | async-done | bytes 32784 | tf_op jit(solution)/shard_map/reduce_scatter | solution.py:318
  3110.9 135.4 %reduce-scatter.51.cloned.1.call-done = f32[64,256]{1,0:T(8,128)} async-done(((f32[2048,256]{1,0:T(8,128)}), f32[64,256]{1,0:T(8,128)}) %reduce-scatter.51.cloned.1.call-update) | async-done | bytes 65552 | tf_op jit(solution)/shard_map/reduce_scatter | solution.py:307
  3246.3 135.5 %reduce-scatter.53.cloned.1.call-done = f32[64,256]{1,0:T(8,128)} async-done(((f32[2048,256]{1,0:T(8,128)}), f32[64,256]{1,0:T(8,128)}) %reduce-scatter.53.cloned.1.call-update) | async-done | bytes 65552 | tf_op jit(solution)/shard_map/reduce_scatter | solution.py:310
  (330 shorter events, 120.4 us)
Async XLA Ops:
  7.2 136.4 %copy-start.16 = (bf16[64,1024]{1,0:T(8,128)(2,1)S(1)}, bf16[64,1024]{1,0:T(8,128)(2,1)}, u32[]{:S(2)}) copy-start(bf16[64,1024]{1,0:T(8,128)(2,1)} %param.27) | copy-start | bytes 393220
  7.2 98.2 %copy-start.53 = (bf16[32,256]{1,0:T(8,128)(2,1)S(1)}, bf16[32,256]{1,0:T(8,128)(2,1)}, u32[]{:S(2)}) copy-start(bf16[32,256]{1,0:T(8,128)(2,1)} %param.45) | copy-start | bytes 49156
  7.2 151.6 %all-gather.25.cloned.1.call-start = ((), (), s32[]{:S(2)}) async-start(), calls=%async_computation.28 | async-start | bytes 1179648 | tf_op jit(solution)/shard_map/all_gather | solution.py:107
  7.9 153.7 %all-gather.17.cloned.1.call-start = ((), (), s32[]{:S(2)}) async-start(), calls=%async_computation.24 | async-start | bytes 1081344 | tf_op jit(solution)/shard_map/all_gather | solution.py:85
  8.7 155.6 %all-gather.19.cloned.1.call-start = ((), (), s32[]{:S(2)}) async-start(), calls=%async_computation.25 | async-start | bytes 1081344 | tf_op jit(solution)/shard_map/all_gather | solution.py:86
  9.4 173.8 %all-gather.21.cloned.1.call-start = ((), (), s32[]{:S(2)}) async-start(), calls=%async_computation.26 | async-start | bytes 1310720 | tf_op jit(solution)/shard_map/all_gather | solution.py:121
  58.4 176.2 %all-gather.23.cloned.1.call-start = ((), (), s32[]{:S(2)}) async-start(), calls=%async_computation.27 | async-start | bytes 2359296 | tf_op jit(solution)/shard_map/all_gather | solution.py:102
  59.0 227.1 %all-gather.27.cloned.1.call-start = ((), (), s32[]{:S(2)}) async-start(), calls=%async_computation.29 | async-start | bytes 2359296 | tf_op jit(solution)/shard_map/all_gather | solution.py:103
  59.5 259.9 %reduce-scatter.33.cloned.1.call-start = ((), (), s32[]{:S(2)}) async-start(), calls=%async_computation.30 | async-start | bytes 2621440 | tf_op jit(solution)/shard_map/reduce_scatter | solution.py:163
  61.0 84.0 %copy-start.46 = (f32[1024]{0:T(1024)}, f32[1024]{0:T(1024)S(1)}, u32[]{:S(2)}) copy-start(f32[1024]{0:T(1024)S(1)} %convert_element_type.200) | copy-start | bytes 12292
  62.5 82.5 %copy-start.59 = (f32[64]{0:T(128)}, f32[64]{0:T(128)S(1)}, u32[]{:S(2)}) copy-start(f32[64]{0:T(128)S(1)} %fusion.51) | copy-start | bytes 772
  105.4 45.6 %copy-start.65 = (s32[1,256]{1,0:T(1,128)S(1)}, s32[1,256]{1,0:T(1,128)}, u32[]{:S(2)}) copy-start(s32[1,256]{1,0:T(1,128)} %param.30) | copy-start | bytes 3076
  158.8 80.9 %copy-start.8 = (pred[512,512]{0,1:T(8,128)(4,1)}, pred[512,512]{0,1:T(8,128)(4,1)S(1)}, u32[]{:S(2)}) copy-start(pred[512,512]{0,1:T(8,128)(4,1)S(1)} %compare_and_fusion) | copy-start | bytes 786436
  165.6 71.6 %copy-start = (bf16[2048,512]{1,0:T(8,128)(2,1)}, bf16[2048,512]{1,0:T(8,128)(2,1)S(1)}, u32[]{:S(2)}) copy-start(bf16[2048,512]{1,0:T(8,128)(2,1)S(1)} %constant_dynamic-update-slice_fusion) | copy-start | bytes 6291460
  171.9 65.3 %copy-start.44 = (bf16[256,512]{1,0:T(8,128)(2,1)S(1)}, bf16[256,512]{1,0:T(8,128)(2,1)}, u32[]{:S(2)}) copy-start(bf16[256,512]{1,0:T(8,128)(2,1)} %fusion.17) | copy-start | bytes 786436
  171.9 62.6 %copy-start.35 = (bf16[512,512]{1,0:T(8,128)(2,1)}, bf16[512,512]{1,0:T(8,128)(2,1)S(1)}, u32[]{:S(2)}) copy-start(bf16[512,512]{1,0:T(8,128)(2,1)S(1)} %constant_dynamic-update-slice_fusion.4) | copy-start | bytes 1572868
  240.5 49.2 %copy-start.23 = (bf16[256,2,256]{0,2,1:T(8,128)(2,1)}, bf16[256,2,256]{0,2,1:T(8,128)(2,1)S(1)}, u32[]{:S(2)}) copy-start(bf16[256,2,256]{0,2,1:T(8,128)(2,1)S(1)} %get-tuple-element.59) | copy-start | bytes 786436
  240.5 120.8 %copy-start.20 = (bf16[256,2,256]{0,2,1:T(8,128)(2,1)}, bf16[256,2,256]{0,2,1:T(8,128)(2,1)S(1)}, u32[]{:S(2)}) copy-start(bf16[256,2,256]{0,2,1:T(8,128)(2,1)S(1)} %get-tuple-element.58) | copy-start | bytes 786436
  289.7 29.8 copy-start.4
  289.7 71.6 %all-gather.37.cloned.1.call-start = ((), (), s32[]{:S(2)}) async-start(), calls=%async_computation.36 | async-start | bytes 1179648 | tf_op jit(solution)/shard_map/all_gather | solution.py:108
  290.5 88.7 %all-gather.29.cloned.1.call-start = ((), (), s32[]{:S(2)}) async-start(), calls=%async_computation.31 | async-start | bytes 1310720 | tf_op jit(solution)/shard_map/all_gather | solution.py:171
  321.6 287.4 %all-gather.31.cloned.1.call-start = ((), (), s32[]{:S(2)}) async-start(), calls=%async_computation.32 | async-start | bytes 18874368 | tf_op jit(solution)/shard_map/all_gather | solution.py:104
  322.2 515.0 %all-gather.33.cloned.1.call-start = ((), (), s32[]{:S(2)}) async-start(), calls=%async_computation.33 | async-start | bytes 18874368 | tf_op jit(solution)/shard_map/all_gather | solution.py:105
  322.9 531.3 %all-gather.45.cloned.1.call-start = ((), (), s32[]{:S(2)}) async-start(), calls=%async_computation.42 | async-start | bytes 1310720 | tf_op jit(solution)/shard_map/all_gather | solution.py:195
  324.4 759.8 %all-gather.35.cloned.1.call-start = ((), (), s32[]{:S(2)}) async-start(), calls=%async_computation.34 | async-start | bytes 18874368 | tf_op jit(solution)/shard_map/all_gather | solution.py:106
  325.1 808.1 %reduce-scatter.37.cloned.1.call-start = ((), (), s32[]{:S(2)}) async-start(), calls=%async_computation.37 | async-start | bytes 1310720 | tf_op jit(solution)/shard_map/reduce_scatter | solution.py:164
  364.0 797.2 %all-gather.39.cloned.1.call-start = ((), (), s32[]{:S(2)}) async-start(), calls=%async_computation.38 | async-start | bytes 2359296 | tf_op jit(solution)/shard_map/all_gather | solution.py:109
  364.6 846.4 %all-gather.41.cloned.1.call-start = ((), (), s32[]{:S(2)}) async-start(), calls=%async_computation.39 | async-start | bytes 2359296 | tf_op jit(solution)/shard_map/all_gather | solution.py:110
  365.1 897.3 %all-gather.43.cloned.1.call-start = ((), (), s32[]{:S(2)}) async-start(), calls=%async_computation.40 | async-start | bytes 2359296 | tf_op jit(solution)/shard_map/all_gather | solution.py:111
  365.7 929.3 %reduce-scatter.41.cloned.1.call-start = ((), (), s32[]{:S(2)}) async-start(), calls=%async_computation.43 | async-start | bytes 2621440 | tf_op jit(solution)/shard_map/reduce_scatter | solution.py:215
  1124.5 198.6 %reduce-scatter.43.cloned.1.call-start = ((), (), s32[]{:S(2)}) async-start(), calls=%async_computation.45 | async-start | bytes 1310720 | tf_op jit(solution)/shard_map/reduce_scatter | solution.py:216
  1125.2 9.2 copy-start.45
  1270.9 71.0 %all-gather.47.cloned.1.call-start = ((), (), s32[]{:S(2)}) async-start(), calls=%async_computation.44 | async-start | bytes 1310720 | tf_op jit(solution)/shard_map/all_gather | solution.py:225
  1300.0 119.7 %reduce-scatter.75.cloned.1.call-start = ((), (), s32[]{:S(2)}) async-start(), calls=%async_computation.61 | async-start | bytes 327680
  1349.4 74.7 %reduce-scatter.73.cloned.1.call-start = ((), (), s32[]{:S(2)}) async-start(), calls=%async_computation.60 | async-start | bytes 327680
  1350.3 113.9 %reduce-scatter.79.cloned.1.call-start = ((), (), s32[]{:S(2)}) async-start(), calls=%async_computation.63 | async-start | bytes 2359296
  1354.9 179.8 %reduce-scatter.69.cloned.1.call-start = ((), (), s32[]{:S(2)}) async-start(), calls=%async_computation.58 | async-start | bytes 2359296 | tf_op jit(solution)/shard_map/reduce_scatter | solution.py:296
  1358.0 247.3 %reduce-scatter.71.cloned.1.call-start = ((), (), s32[]{:S(2)}) async-start(), calls=%async_computation.59 | async-start | bytes 2359296 | tf_op jit(solution)/shard_map/reduce_scatter | solution.py:299
  1360.4 310.6 %reduce-scatter.77.cloned.1.call-start = ((), (), s32[]{:S(2)}) async-start(), calls=%async_computation.62 | async-start | bytes 1179648
  1362.3 332.5 %reduce-scatter.47.cloned.1.call-start = ((), (), s32[]{:S(2)}) async-start(), calls=%async_computation.47 | async-start | bytes 655360 | tf_op jit(solution)/shard_map/reduce_scatter | solution.py:254
  1365.5 354.0 %reduce-scatter.39.cloned.1.call-start = ((), (), s32[]{:S(2)}) async-start(), calls=%async_computation.41 | async-start | bytes 655360 | tf_op jit(solution)/shard_map/reduce_scatter | solution.py:184
  1369.0 378.2 %reduce-scatter.45.cloned.1.call-start = ((), (), s32[]{:S(2)}) async-start(), calls=%async_computation.46 | async-start | bytes 1310720 | tf_op jit(solution)/shard_map/reduce_scatter | solution.py:251
  1370.8 443.3 %reduce-scatter.63.cloned.1.call-start = ((), (), s32[]{:S(2)}) async-start(), calls=%async_computation.55 | async-start | bytes 1179648 | tf_op jit(solution)/shard_map/reduce_scatter | solution.py:290
  1373.6 467.1 %reduce-scatter.35.cloned.1.call-start = ((), (), s32[]{:S(2)}) async-start(), calls=%async_computation.35 | async-start | bytes 1310720 | tf_op jit(solution)/shard_map/reduce_scatter | solution.py:181
  1383.0 529.7 %reduce-scatter.49.cloned.1.call-start = ((), (), s32[]{:S(2)}) async-start(), calls=%async_computation.48 | async-start | bytes 2359296 | tf_op jit(solution)/shard_map/reduce_scatter | solution.py:275
  1386.4 597.4 %reduce-scatter.55.cloned.1.call-start = ((), (), s32[]{:S(2)}) async-start(), calls=%async_computation.51 | async-start | bytes 2359296 | tf_op jit(solution)/shard_map/reduce_scatter | solution.py:278
  1388.6 880.8 %reduce-scatter.57.cloned.1.call-start = ((), (), s32[]{:S(2)}) async-start(), calls=%async_computation.52 | async-start | bytes 18874368 | tf_op jit(solution)/shard_map/reduce_scatter | solution.py:281
  1398.5 1156.9 %reduce-scatter.59.cloned.1.call-start = ((), (), s32[]{:S(2)}) async-start(), calls=%async_computation.53 | async-start | bytes 18874368 | tf_op jit(solution)/shard_map/reduce_scatter | solution.py:284
  1408.3 1432.4 %reduce-scatter.61.cloned.1.call-start = ((), (), s32[]{:S(2)}) async-start(), calls=%async_computation.54 | async-start | bytes 18874368 | tf_op jit(solution)/shard_map/reduce_scatter | solution.py:287
  1419.6 1557.8 %reduce-scatter.65.cloned.1.call-start = ((), (), s32[]{:S(2)}) async-start(), calls=%async_computation.56 | async-start | bytes 1081344 | tf_op jit(solution)/shard_map/reduce_scatter | solution.py:315
  1423.3 1687.7 %reduce-scatter.67.cloned.1.call-start = ((), (), s32[]{:S(2)}) async-start(), calls=%async_computation.57 | async-start | bytes 1081344 | tf_op jit(solution)/shard_map/reduce_scatter | solution.py:318
  1424.0 1822.3 %reduce-scatter.51.cloned.1.call-start = ((), (), s32[]{:S(2)}) async-start(), calls=%async_computation.49 | async-start | bytes 2162688 | tf_op jit(solution)/shard_map/reduce_scatter | solution.py:307
  1428.2 1953.7 %reduce-scatter.53.cloned.1.call-start = ((), (), s32[]{:S(2)}) async-start(), calls=%async_computation.50 | async-start | bytes 2162688 | tf_op jit(solution)/shard_map/reduce_scatter | solution.py:310
  1466.2 253.4 %copy-start.7 = (f32[64,1024]{1,0:T(8,128)S(1)}, f32[64,1024]{1,0:T(8,128)}, u32[]{:S(2)}) copy-start(f32[64,1024]{1,0:T(8,128)} %copy-done.6) | copy-start | bytes 786436
  1466.2 253.4 %copy-start.22 = (f32[64,1024]{1,0:T(8,128)S(1)}, f32[64,1024]{1,0:T(8,128)}, u32[]{:S(2)}) copy-start(f32[64,1024]{1,0:T(8,128)} %reduce-scatter.43.cloned.1.call-done) | copy-start | bytes 786436
  1607.1 140.1 %copy-start.1 = (bf16[2048,512]{1,0:T(8,128)(2,1)S(1)}, bf16[2048,512]{1,0:T(8,128)(2,1)}, u32[]{:S(2)}) copy-start(bf16[2048,512]{1,0:T(8,128)(2,1)} %copy-done) | copy-start | bytes 6291460
  1721.6 28.3 copy-start.49
  1721.6 28.3 copy-start.51
  1721.6 28.3 copy-start.52
  1721.6 94.1 %copy-start.67 = (f32[64]{0:T(128)S(1)}, f32[64]{0:T(128)}, u32[]{:S(2)}) copy-start(f32[64]{0:T(128)} %copy-done.66) | copy-start | bytes 772
  1721.6 119.1 %copy-start.13 = (f32[64,2048]{1,0:T(8,128)S(1)}, f32[64,2048]{1,0:T(8,128)}, u32[]{:S(2)}) copy-start(f32[64,2048]{1,0:T(8,128)} %reduce-scatter.41.cloned.1.call-done) | copy-start | bytes 1572868
  1721.6 119.1 %copy-start.55 = (f32[64]{0:T(128)S(1)}, f32[64]{0:T(128)}, u32[]{:S(2)}) copy-start(f32[64]{0:T(128)} %copy-done.54) | copy-start | bytes 772
  1721.6 119.1 %copy-start.58 = (f32[64]{0:T(128)S(1)}, f32[64]{0:T(128)}, u32[]{:S(2)}) copy-start(f32[64]{0:T(128)} %copy-done.57) | copy-start | bytes 772
  1721.6 119.1 %copy-start.62 = (f32[64]{0:T(128)S(1)}, f32[64]{0:T(128)}, u32[]{:S(2)}) copy-start(f32[64]{0:T(128)} %copy-done.61) | copy-start | bytes 772
  (47 other events, 89.7 us)
Sparse Core Ops, SparseCore 0:
  10.2 42.8 all-gather.24
  56.0 52.8 all-gather.16
  111.7 52.4 all-gather.18
  166.2 16.9 all-gather.20
  185.2 49.2 all-gather.22
  236.5 49.5 all-gather.26
  289.8 29.5 reduce-scatter.32
  321.7 39.5 all-gather.36
  363.5 15.5 all-gather.28
  381.3 227.6 all-gather.30
  611.3 225.7 all-gather.32
  839.2 14.8 all-gather.44
  856.4 227.7 all-gather.34
  1086.7 23.0 reduce-scatter.36
  1111.8 49.2 all-gather.38
  1163.1 47.7 all-gather.40
  1212.8 49.5 all-gather.42
  1265.4 29.5 reduce-scatter.40
  1298.3 24.8 reduce-scatter.42
  1325.2 16.7 all-gather.46
  1349.5 20.0 reduce-scatter.74
  1372.8 20.0 reduce-scatter.72
  1396.4 67.8 reduce-scatter.78
  1467.6 67.0 reduce-scatter.68
  1538.2 67.0 reduce-scatter.70
  1608.5 62.4 reduce-scatter.76
  1674.0 20.6 reduce-scatter.46
  1697.8 21.6 reduce-scatter.38
  1722.2 24.8 reduce-scatter.44
  1750.4 63.5 reduce-scatter.62
  1816.8 23.9 reduce-scatter.34
  1844.8 67.7 reduce-scatter.48
  1916.6 67.1 reduce-scatter.54
  1987.6 281.6 reduce-scatter.56
  2273.6 281.7 reduce-scatter.58
  2559.0 281.7 reduce-scatter.60
  2843.5 133.8 reduce-scatter.64
  2980.2 130.6 reduce-scatter.66
  3113.7 132.5 reduce-scatter.50
  3249.2 132.6 reduce-scatter.52
where the time goes:
time: 3400 us; the launch traced here: 3390 us
  waiting for transfers between devices  2910 us (86%)
  blocking collectives  205 us (6%)
  matrix products  171 us (5%)
  other arithmetic  48.3 us (1%)
    reduce_scatter x1, waiting for transfers between devices, local(): lax.psum_scatter(grad_gate_w[0].astype(jnp.bfloat16), 'wide', scatter_dim...  284 us
    reduce_scatter x1, waiting for transfers between devices, local(): lax.psum_scatter(grad_up_w[0].astype(jnp.bfloat16), 'wide', scatter_dimen...  282 us
    reduce_scatter x1, waiting for transfers between devices, local(): lax.psum_scatter(grad_down[0].astype(jnp.bfloat16), 'wide', scatter_dimen...  281 us
    all_gather x1, waiting for transfers between devices, local(): lax.all_gather(wd_prefix, 'wide', axis=1, tiled=True)  230 us
    all_gather x1, waiting for transfers between devices, local(): lax.all_gather(wg_prefix, 'wide', axis=0, tiled=True)  230 us
    all_gather x1, waiting for transfers between devices, local(): lax.all_gather(wu_prefix, 'wide', axis=0, tiled=True)  215 us
    reduce_scatter x1, waiting for transfers between devices, local(): lax.psum_scatter(grad_keyval_w[0][:, head_dim:], ('wide', 'narrow'), scat...  136 us
    reduce_scatter x1, waiting for transfers between devices, local(): lax.psum_scatter(grad_keyval_w[0][:, :head_dim], ('wide', 'narrow'), scat...  135 us
  transfers between devices with their start and end apart: 40, of which 35 were waited for; matrix products, arithmetic and copies ran while one was open for 7% of the time, Pallas kernels for 0%

commit v1 on v0

v1 whole, which is shorter than its diff:
```python
import functools

import jax
import jax.numpy as jnp
from jax import lax
from jax.experimental import pallas as pl
from jax.experimental.pallas import tpu as pltpu
from jax.sharding import PartitionSpec as P

PREFIX_BLOCKS = 4
BOTH = ("wide", "narrow")

epsilon = 1e-06
scaling = 0.0625
masked_score = -1e30
low = jnp.bfloat16
wider = jnp.float32


def rms_norm(features, weight):
    return (
        features
        * lax.rsqrt(jnp.mean(features * features, axis=-1, keepdims=True) + epsilon)
        * weight
    )


def product(former, latter):
    return jnp.dot(former, latter, preferred_element_type=wider)


def rows_contract(former, latter):
    return lax.dot_general(
        former, latter, (((0,), (0,)), ((), ())), preferred_element_type=wider
    )


def cols_contract(former, latter):
    return lax.dot_general(
        former, latter, (((1,), (1,)), ((), ())), preferred_element_type=wider
    )


def norm_back(features, weight, upstream):
    unused, pullback = jax.vjp(rms_norm, features, weight)
    return pullback(upstream)


def tie(value, *earlier):
    return lax.optimization_barrier((value, *earlier))[0] if earlier else value


def masked_scores(queries, key_rows, allowed):
    scores = jnp.einsum("qhd,kd->hqk", queries, key_rows, preferred_element_type=wider)
    return jnp.where(allowed[None], scores, masked_score)


def copies_kernel(plan, n_in, place_ref, *refs):
    copied = refs[-1]
    copies = []
    for i, (source, source_at, target, target_at) in enumerate(plan):
        source_ref = refs[source].at[source_at(place_ref)]
        target_ref = refs[n_in + target].at[target_at(place_ref)]
        copies.append(pltpu.make_async_copy(source_ref, target_ref, copied.at[i]))
    for copy in copies:
        copy.start()
    for copy in copies:
        copy.wait()


def copy_blocks(plan, places, arrays, shapes, name):
    any_spec = pl.BlockSpec(memory_space=pl.ANY)
    moved = 2 * sum(shape[0] * shape[1] * 2 for shape in shapes)
    return pl.pallas_call(
        functools.partial(copies_kernel, plan, len(arrays)),
        in_specs=[pl.BlockSpec(memory_space=pltpu.SMEM)] + [any_spec] * len(arrays),
        out_specs=[pl.BlockSpec(memory_space=pltpu.VMEM)] * len(shapes),
        scratch_shapes=[pltpu.SemaphoreType.DMA((len(plan),))],
        compiler_params=pltpu.CompilerParams(vmem_limit_bytes=24 << 20),
        out_shape=[jax.ShapeDtypeStruct(shape, low) for shape in shapes],
        cost_estimate=pl.CostEstimate(flops=0, bytes_accessed=moved, transcendentals=0),
        name=name,
    )(places, *arrays)


def block(index, size):
    return pl.ds(pl.multiple_of(index * size, size), size)


def feed_kernel(count, half, n_kept, n_copied, first, *refs):
    token_refs, refs = refs[:count], refs[count:]
    grad_refs, refs = refs[:count], refs[count:]
    weight_refs, refs = refs[:4], refs[4 + n_kept :]
    kept_refs, row_refs = refs[:n_copied], refs[n_copied : n_copied + 4]
    back_ref, out_ref, copied = refs[n_copied + 4 :]
    step = pl.program_id(0)
    tile = token_refs[0].shape[0]
    width = weight_refs[1].shape[1]
    columns_of = (slice(0, width), slice(width, width + weight_refs[3].shape[1]))
    slope = 0.7978845608028654

    def run(token_ref, grad_ref):
        place = block(first + step, tile)
        copies = [
            pltpu.make_async_copy(
                source.at[:, columns_of[i % 2]], kept_refs[i].at[place], copied.at[i]
            )
            for i, source in enumerate((token_ref, token_ref, grad_ref, grad_ref)[:n_copied])
        ]
        for copy in copies:
            copy.start()
        for i, columns in enumerate(columns_of):
            gate_up_ref, down_ref = weight_refs[2 * i : 2 * i + 2]
            hidden_ref, both_ref = row_refs[2 * i : 2 * i + 2]
            units = down_ref.shape[0]
            both = product(token_ref[:, columns], gate_up_ref[...])
            gate, up = both[:, :units], both[:, units:]
            square = gate * gate
            bend = jnp.tanh(slope * gate * (1.0 + 0.044715 * square))
            active = 0.5 * gate * (1.0 + bend)
            hidden = (active * up).astype(low)
            hidden_ref[...] = hidden
            dhidden = cols_contract(grad_ref[:, columns], down_ref[...])
            steep = 0.5 * (1.0 + bend) + 0.5 * gate * (1.0 - bend * bend) * slope * (
                1.0 + 3 * 0.044715 * square
            )
            both_ref[:, :units] = (dhidden * up * steep).astype(low)
            both_ref[:, units:] = (dhidden * active).astype(low)
            back_ref[:, columns] = cols_contract(both_ref[...], gate_up_ref[...]).astype(low)
            out_ref[:, columns] = product(hidden, down_ref[...]).astype(low)
        for copy in copies:
            copy.wait()

    for piece in range(count):
        pl.when(step // half == piece)(
            functools.partial(run, token_refs[piece], grad_refs[piece])
        )


def feed_forward(tokens, grads, weights, kept, size, total, first, n_copied):
    count = len(tokens)
    columns = tokens[0][0].shape[1]
    tile = min(size, 256)
    half = size // tile
    units = [weights[1].shape[0], weights[3].shape[0]]
    widths = [weights[1].shape[1], weights[3].shape[1]]
    first = first * half
    rows = [units[0], 2 * units[0], units[1], 2 * units[1]]
    any_spec = pl.BlockSpec(memory_space=pl.ANY)

    def piece_spec(piece, place):
        return pl.BlockSpec(
            (tile, columns),
            lambda i: (place * half + jnp.clip(i - piece * half, 0, half - 1), 0),
        )

    out = pl.pallas_call(
        functools.partial(feed_kernel, count, half, len(kept), n_copied, first),
        grid=(count * half,),
        in_specs=[piece_spec(i, place) for i, (unused, place) in enumerate(tokens)]
        + [piece_spec(i, place) for i, (unused, place) in enumerate(grads)]
        + [
            pl.BlockSpec(w.shape, lambda i: (0, 0), pipeline_mode=pl.Buffered(1)) for w in weights
        ]
        + [any_spec] * len(kept),
        out_specs=[any_spec] * n_copied
        + [pl.BlockSpec((tile, w), lambda i: (first + i, 0)) for w in rows]
        + [pl.BlockSpec((tile, columns), lambda i: (i, 0))] * 2,
        scratch_shapes=[pltpu.SemaphoreType.DMA((4,))],
        out_shape=[
            jax.ShapeDtypeStruct((total, w), low) for w in (widths * 2)[:n_copied] + rows
        ]
        + [jax.ShapeDtypeStruct((count * size, columns), low)] * 2,
        input_output_aliases={2 * count + 4 + i: i for i in range(len(kept))},
        compiler_params=pltpu.CompilerParams(vmem_limit_bytes=52 << 20),
        cost_estimate=pl.CostEstimate(
            flops=2 * count * size * 6 * (widths[0] * units[0] + widths[1] * units[1]),
            bytes_accessed=12 * count * size * columns,
            transcendentals=0,
        ),
        name="feed_forward",
    )(*(array for array, unused in tokens), *(array for array, unused in grads), *weights, *kept)
    return out[: n_copied + 4], out[n_copied + 4], out[n_copied + 5]


def make_local(n_wide, n_narrow):
    n_all = n_wide * n_narrow
    wide_masks = [1 << bit for bit in range(n_wide.bit_length() - 1)]
    far = [("wide", mask) for mask in wide_masks[:0:-1]]
    side, across, core = ("wide", 1), ("narrow", 2), ("narrow", 1)
    sizes = {"wide": n_wide, "narrow": n_narrow}

    def join(*values):
        return lax.optimization_barrier(values)

    def hop(value, link, *earlier):
        axis, mask = link
        value = tie(value, *earlier)
        return lax.ppermute(value, axis, [(i, i ^ mask) for i in range(sizes[axis])])

    def rank_of(link):
        return link[1] if link[0] == "narrow" else link[1] * n_narrow

    def gather_blocks(block, links, at, events, *earlier):
        held = []
        for i, link in enumerate(links):
            position = sum(other > rank_of(link) for other in held)
            moved = hop(block, link, *(earlier[i] if i < len(earlier) else ()))
            events.append(moved)
            block = jnp.where(
                (at[link[0]] & link[1]) != 0,
                jnp.stack([moved, block], position),
                jnp.stack([block, moved], position),
            )
            held.append(rank_of(link))
        return block.reshape(-1, *block.shape[len(links) :])

    def scatter_blocks(blocks, links, at, events=None, earlier=()):
        held = sorted((rank_of(link) for link in links), reverse=True)
        blocks = blocks.reshape(*(2 for unused in links), *blocks.shape[1:])
        for stage, link in enumerate(links):
            position = held.index(rank_of(link))
            bit = jnp.minimum(at[link[0]] & link[1], 1)
            mine = lax.dynamic_index_in_dim(blocks, bit, position, keepdims=False)
            theirs = lax.dynamic_index_in_dim(blocks, 1 - bit, position, keepdims=False)
            moved = hop(theirs, link, *at_stage(earlier, stage))
            if events is not None:
                events.append(moved)
            blocks = mine.astype(wider) + moved.astype(wider)
            if stage + 1 < len(links):
                blocks = blocks.astype(low)
            held.remove(rank_of(link))
        return blocks

    def at_stage(earlier, stage):
        return earlier[stage] if stage < len(earlier) else ()

    def gather_rows(rows, links, events, earlier=()):
        for stage, link in enumerate(links):
            moved = hop(rows, link, *at_stage(earlier, stage))
            events.append(moved)
            rows = jnp.concatenate([rows, moved], axis=0)
        return rows

    def scatter_rows(rows, links, events, earlier=()):
        for stage, link in enumerate(links):
            half = rows.shape[0] // 2
            moved = hop(rows[half:], link, *at_stage(earlier, stage))
            events.append(moved)
            rows = rows[:half].astype(wider) + moved.astype(wider)
            if stage + 1 < len(links):
                rows = rows.astype(low)
        return rows

    def gather_all(rows, events, even, earlier=()):
        own = gather_rows(rows, far, events, earlier)
        sides, last = at_stage(earlier, len(far)), at_stage(earlier, len(far) + 1)
        from_x, from_y = hop(own, across, *sides), hop(own, side, *sides)
        events.append(from_y)
        half = own.shape[0] // 2
        if even:
            corner = jnp.concatenate(
                [hop(from_y[:half], across, *last), hop(from_x[half:], side, *last)], axis=0
            )
        else:
            corner = hop(from_y, across, *last)
        return own, from_x, from_y, corner

    def scatter_all(most, other_most, corner, other_corner, events, even, earlier=()):
        chip, first, second = (at_stage(earlier, stage) for stage in range(3))
        corner = corner.astype(wider) + hop(other_corner, core, *chip).astype(wider)
        corner = corner.astype(low)
        size = corner.shape[0]
        half = size // 2 if even else size
        for_y = hop(corner[:half], across, *first)
        events.append(for_y)
        sums = []
        for i in range(3):
            rows = slice(i * size, (i + 1) * size)
            moved = other_most[i] if isinstance(other_most, list) else other_most[rows]
            sums.append((most[rows], moved))
        own, sum_x, sum_y = (mine.astype(wider) + moved.astype(wider) for mine, moved in sums)
        if even:
            for_x = hop(corner[half:], side, *first)
            sum_x = jnp.concatenate([sum_x[:half], sum_x[half:] + for_x.astype(wider)], axis=0)
            sum_y = jnp.concatenate([sum_y[:half] + for_y.astype(wider), sum_y[half:]], axis=0)
        else:
            sum_y = sum_y + for_y.astype(wider)
        moved_x = hop(sum_x.astype(low), across, *second)
        moved_y = hop(sum_y.astype(low), side, *second)
        events.append(moved_y)
        total = own + moved_x.astype(wider) + moved_y.astype(wider)
        return scatter_rows(total.astype(low), far[::-1], events, earlier[3:])

    def local(
        x_prefix,
        x_action,
        cot_prefix,
        cot_action,
        prefix_block,
        action_block,
        valid_len,
        mix_weight,
        wq_prefix,
        wk_prefix,
        wv_prefix,
        wo_prefix,
        wg_prefix,
        wu_prefix,
        wd_prefix,
        norm1_prefix,
        norm2_prefix,
        wq_action,
        wk_action,
        wv_action,
        wo_action,
        wg_action,
        wu_action,
        wd_action,
        norm1_action,
        norm2_action,
    ):
        at = {"wide": lax.axis_index("wide"), "narrow": lax.axis_index("narrow")}
        head_dim = wk_prefix.shape[1]
        own = x_prefix.shape[0]
        width = x_prefix.shape[1]

        def streams(packed):
            return [packed[:, :width], packed[:, width:]]

        depth = [wg_prefix.shape[0], wg_action.shape[0]]
        units = [wg_prefix.shape[1] // n_wide, wg_action.shape[1] // n_wide]

        def fold(rows, lead):
            return jnp.concatenate(
                [rows[i * lead : (i + 1) * lead] for i in range(rows.shape[0] // lead)], axis=1
            )

        def unfold(rows, columns):
            return jnp.concatenate(
                [
                    rows[:, i * columns : (i + 1) * columns]
                    for i in range(rows.shape[1] // columns)
                ],
                axis=0,
            )

        def pack(parts):
            gate_p, up_p, down_p, gate_a, up_a, down_a = parts
            action = jnp.concatenate([gate_a, up_a, fold(down_a, depth[1])], axis=1)
            action = jnp.pad(action, [(0, 0), (0, units[0] - action.shape[1])])
            return jnp.concatenate([gate_p, up_p, fold(down_p, depth[0]), action], axis=0)

        def unpack(packet):
            d, f = depth[0], units[1]
            action = packet[3 * d :]
            return (
                packet[:d],
                packet[d : 2 * d],
                unfold(packet[2 * d : 3 * d], d),
                action[:, :f],
                action[:, f : 2 * f],
                unfold(action[:, 2 * f : 3 * f], depth[1]),
            )

        distances = list(range(1, n_wide))

        aligned = units[1] % 128 == 0 and depth[1] % 16 == 0 and units[1] == depth[1]
        folds = units[0] // depth[0]
        packet_shape = (3 * depth[0] + depth[1], units[0])
        peers = at["wide"] ^ jnp.arange(n_wide, dtype=jnp.int32)

        copying = n_all * own <= 4096

        def packet_plan(outward, blocks_of):
            plan = []
            for k in range(n_wide):
                for array, array_at, packet_at in blocks_of(k):
                    if outward:
                        plan.append((array, array_at, k, lambda ref, at=packet_at: at))
                    else:
                        plan.append((k, lambda ref, at=packet_at: at, array, array_at))
            return plan

        def span(start, size):
            return slice(start, start + size)

        def packet_places(k, gate_at, up_at, down_at, arrays):
            for i, (d, f) in enumerate(zip(depth, units, strict=True)):
                gate, up, down = arrays[3 * i : 3 * i + 3]
                top = 3 * depth[0] if i else 0
                second = (span(top, d), span(f, f)) if i else (span(d, d), span(0, f))
                yield gate, functools.partial(gate_at, k, d, f), (span(top, d), span(0, f))
                yield up, functools.partial(up_at, k, d, f), second
                for part in range(f // d):
                    place = (span(top, d), span(2 * f, d)) if i else (span(2 * d, d), span(part * d, d))
                    yield down, functools.partial(down_at, k, d, f, part), place

        def weight_packet(k):
            peer = at["wide"] ^ k
            f, g = units
            return pack(
                (
                    lax.dynamic_slice_in_dim(wg_prefix, peer * f, f, 1),
                    lax.dynamic_slice_in_dim(wu_prefix, peer * f, f, 1),
                    lax.dynamic_slice_in_dim(wd_prefix, peer * f, f, 0),
                    lax.dynamic_slice_in_dim(wg_action, peer * g, g, 1),
                    lax.dynamic_slice_in_dim(wu_action, peer * g, g, 1),
                    lax.dynamic_slice_in_dim(wd_action, peer * g, g, 0),
                )
            )

        if aligned:
            packets = copy_blocks(
                packet_plan(
                    True,
                    lambda k: packet_places(
                        k,
                        lambda k, d, f, ref: (slice(None), block(ref[k], f)),
                        lambda k, d, f, ref: (slice(None), block(ref[k], f)),
                        lambda k, d, f, part, ref: (
                            pl.ds(pl.multiple_of(ref[k] * f, f) + part * d, d),
                            slice(None),
                        ),
                        range(6),
                    ),
                ),
                peers,
                [wg_prefix, wu_prefix, wd_prefix, wg_action, wu_action, wd_action],
                [packet_shape] * n_wide,
                "pack_weights",
            )
            packets = dict(enumerate(packets))
            weight_packet = packets.get
        else:
            packets = {0: weight_packet(0)}

        def send_packets(few, packet_of, *earlier):
            for k in few:
                packets[k] = hop(packet_of(k), ("wide", k), *earlier)

        def share(first, last):
            return [k for k in distances if first * n_wide <= 8 * k < last * n_wide]

        narrow_links = [across, core]
        x_packed = jnp.concatenate([x_prefix, x_action], axis=1)
        item_packed = gather_rows(x_packed, narrow_links, [])
        item_rows = streams(item_packed)

        gain_parts = [norm1_prefix, norm2_prefix, norm1_action, norm2_action]
        gain_sizes = [part.shape[0] for part in gain_parts]
        gain_stops = [sum(gain_sizes[: i + 1]) for i in range(4)]
        keyval_rows_of = [wk_prefix.shape[0], wk_action.shape[0]]
        gain_start = sum(keyval_rows_of)
        gain_rows = 16

        def pad_gains(row):
            return jnp.pad(
                row[..., None, :],
                [(0, 0)] * (row.ndim - 1) + [(0, gain_rows - 1), (0, 2 * head_dim - row.shape[-1])],
            )

        shared_events, query_events, out_events = [], [], []
        query_depth = [wq_prefix.shape[0], wq_action.shape[0]]
        query_half = wq_prefix.shape[1] // 2
        query_packed = jnp.concatenate([wq_prefix, wq_action], axis=0)
        wide_links = far + [side]
        query_blocks = [
            gather_blocks(query_packed[:, :query_half], wide_links, at, []),
            gather_blocks(
                query_packed[:, query_half:],
                [side] + far,
                at,
                query_events,
                (),
                (packets[max(packets)],),
            ),
        ]
        send_packets(share(4, 5), weight_packet, query_events[0])
        shared = gather_blocks(
            jnp.concatenate(
                [
                    jnp.concatenate([wk_prefix, wv_prefix], axis=1),
                    jnp.concatenate([wk_action, wv_action], axis=1),
                    pad_gains(jnp.concatenate(gain_parts)),
                ],
                axis=0,
            ),
            far + [side, across, core],
            at,
            shared_events,
            *[()] * (len(far) + 2),
            tuple(packets[k] for k in share(4, 5)),
        )
        send_packets(share(5, 6), weight_packet, shared_events[-2])
        send_packets(share(0, 2), weight_packet, shared_events[-2])
        gains_all = shared[:, gain_start, :].astype(wider)
        gains = [
            gains_all[:, stop - size : stop].reshape(-1)
            for stop, size in zip(gain_stops, gain_sizes, strict=True)
        ]
        first_gain = [gains[0], gains[2]]
        second_gain = [gains[1], gains[3]]
        keyval_weight = [
            shared[:, : keyval_rows_of[0]].reshape(-1, 2 * head_dim),
            shared[:, keyval_rows_of[0] : gain_start].reshape(-1, 2 * head_dim),
        ]
        query_weight = [
            [blocks[:, : query_depth[0]].reshape(-1, query_half) for blocks in query_blocks],
            [blocks[:, query_depth[0] :].reshape(-1, query_half) for blocks in query_blocks],
        ]
        out_held = gather_blocks(
            jnp.concatenate([wo_prefix.T, wo_action.T], axis=0),
            far,
            at,
            out_events,
            (query_events[1],),
        )
        out_moved = hop(out_held.reshape(*(2 for unused in far), *out_held.shape[1:]), side)
        item_weight = mix_weight[0]
        dout = jnp.concatenate([cot_prefix, cot_action], axis=1).astype(wider) * item_weight

        all_normed = [
            rms_norm(item_rows[stream].astype(wider), first_gain[stream]).astype(low)
            for stream in range(2)
        ]
        prefix_len = item_packed.shape[0]
        total_rows = 2 * prefix_len
        joined = jnp.concatenate(
            [
                product(all_normed[stream], keyval_weight[stream]).astype(low)
                for stream in range(2)
            ],
            axis=0,
        )
        key_rows = joined[:, :head_dim]
        values = joined[:, head_dim:]
        queries = jnp.concatenate(
            [
                jnp.concatenate(
                    [
                        (product(all_normed[stream], part) * scaling).astype(low)
                        for part in query_weight[stream]
                    ],
                    axis=1,
                )
                for stream in range(2)
            ],
            axis=0,
        ).reshape(total_rows, -1, head_dim)
        offsets = [0]
        for unused, mask in narrow_links:
            offsets = offsets + [offset ^ mask for offset in offsets]
        owners = at["narrow"] ^ jnp.array(offsets, jnp.int32)

        def reorder(ids):
            return jnp.take(ids.reshape(n_narrow, -1), owners, axis=0).reshape(-1)

        blocks = jnp.concatenate(
            [reorder(prefix_block[0]), reorder(action_block[0]) + PREFIX_BLOCKS]
        )
        positions = (owners[:, None] * own + jnp.arange(own, dtype=jnp.int32)[None]).reshape(-1)
        usable = jnp.concatenate(
            [
                positions < valid_len[0],
                jnp.ones((total_rows - prefix_len,), dtype=jnp.bool_),
            ]
        )
        allowed = (blocks[None, :] <= blocks[:, None]) & usable[None, :]
        scores = masked_scores(queries, key_rows, allowed)
        highest = jnp.max(scores, axis=-1, keepdims=True)
        exponent = jnp.exp(scores - highest)
        denominator = jnp.sum(exponent, axis=-1, keepdims=True)
        log_total = highest + jnp.log(denominator)
        attention = (exponent / denominator).astype(low)
        mixed_all = jnp.einsum("hqk,kd->qhd", attention, values, preferred_element_type=wider)
        mixed_all = mixed_all.astype(low).reshape(total_rows, -1)
        mixed_rows = [mixed_all[:prefix_len], mixed_all[prefix_len:]]
        out_moved, mixed_all = join(out_moved, mixed_all)
        mixed_rows = [mixed_all[:prefix_len], mixed_all[prefix_len:]]
        out_held = out_held.reshape(out_moved.shape)
        out_blocks = jnp.where(
            (at["wide"] & 1) != 0,
            jnp.stack([out_moved, out_held], len(far)),
            jnp.stack([out_held, out_moved], len(far)),
        )
        out_blocks = out_blocks.reshape(-1, *out_blocks.shape[len(far) + 1 :])
        out_weight = [
            out_blocks[:, : query_depth[0]].reshape(-1, wo_prefix.shape[0]),
            out_blocks[:, query_depth[0] :].reshape(-1, wo_action.shape[0]),
        ]
        attended_all = (
            jnp.concatenate(
                [
                    cols_contract(mixed_rows[stream], out_weight[stream]).astype(low)
                    for stream in range(2)
                ],
                axis=1,
            )
        )
        attended_events = []
        attended = scatter_rows(
            attended_all,
            [core, across],
            attended_events,
            [(), tuple(packets[k] for k in share(5, 6))],
        )
        send_packets(share(7, 8), weight_packet, attended_events[1])
        send_packets(share(3, 4), weight_packet, attended_events[1])
        inputs = [x_prefix.astype(wider), x_action.astype(wider)]
        middle = [
            rows + part for rows, part in zip(inputs, streams(attended), strict=True)
        ]
        normed2 = jnp.concatenate(
            [rms_norm(middle[stream], second_gain[stream]).astype(low) for stream in range(2)],
            axis=1,
        )
        token_events = []
        near = gather_all(
            normed2,
            token_events,
            True,
            [tuple(packets[k] for k in share(0, 2))]
            + [()] * (len(far) - 1)
            + [
                tuple(packets[k] for k in share(7, 8)),
                tuple(packets[k] for k in share(3, 4)),
            ],
        )
        send_packets(share(6, 7), weight_packet, token_events[-2])
        send_packets(share(2, 3), weight_packet, token_events[-2])
        grad_near = gather_all(
            dout.astype(low),
            [],
            False,
            [(shared_events[-3],)]
            + [(shared_events[-1],)] * (len(far) - 1)
            + [(attended_events[0],), (token_events[-2],)],
        )
        if aligned:
            feed_weights = copy_blocks(
                packet_plan(
                    False,
                    lambda k: packet_places(
                        k,
                        lambda k, d, f, ref: (block(ref[k], d), span(0, f)),
                        lambda k, d, f, ref: (block(ref[k], d), span(f, f)),
                        lambda k, d, f, part, ref: (span(part * d, d), block(ref[k], d)),
                        (0, 0, 1, 2, 2, 3),
                    ),
                ),
                peers,
                [packets[k] for k in range(n_wide)],
                [
                    (depth[0] * n_wide, 2 * units[0]),
                    (units[0], depth[0] * n_wide),
                    (depth[1] * n_wide, 2 * units[1]),
                    (units[1], depth[1] * n_wide),
                ],
                "unpack_weights",
            )
        else:
            gate_up_weight = [jnp.zeros((depth[i] * n_wide, 2 * units[i]), low) for i in range(2)]
            down_weight = [jnp.zeros((units[i], depth[i] * n_wide), low) for i in range(2)]
            for k, packet in packets.items():
                peer = at["wide"] ^ k
                parts = unpack(packet)
                for i in range(2):
                    gate_up_weight[i] = lax.dynamic_update_slice_in_dim(
                        gate_up_weight[i],
                        jnp.concatenate(parts[3 * i : 3 * i + 2], axis=1),
                        peer * depth[i],
                        0,
                    )
                    down_weight[i] = lax.dynamic_update_slice_in_dim(
                        down_weight[i], parts[3 * i + 2], peer * depth[i], 1
                    )
            feed_weights = [gate_up_weight[0], down_weight[0], gate_up_weight[1], down_weight[1]]

        size = near[0].shape[0]
        feed = functools.partial(
            feed_forward,
            weights=feed_weights,
            size=size,
            total=n_all * own,
            n_copied=4 if copying else 0,
        )
        if copying:
            other_most = hop(jnp.concatenate(near[:3], axis=0), core)
            token_far = [(other_most, i) for i in range(3)] + [(hop(near[3], core), 0)]
            grad_near = jnp.concatenate(grad_near, axis=0)
            grad_far = hop(grad_near, core)
            grad_near, grad_far = ([(rows, i) for i in range(4)] for rows in (grad_near, grad_far))
        else:
            token_far = [(hop(rows, core), 0) for rows in near]
            grad_far = [(hop(rows, core), 0) for rows in grad_near]
            grad_near = [(rows, 0) for rows in grad_near]
        token_pieces = [(rows, 0) for rows in near] + [token_far[3], *token_far[:3]]
        grad_pieces = [*grad_near, grad_far[3], *grad_far[:3]]
        kept, back_most, out_most = feed(token_pieces[:3], grad_pieces[:3], kept=[], first=0)
        kept, back_corner, out_corner = feed(
            token_pieces[3:5], grad_pieces[3:5], kept=kept, first=3
        )
        kept, back_far, out_far = feed(token_pieces[5:], grad_pieces[5:], kept=kept, first=5)
        hidden_rows, both_rows = kept[-4::2], kept[-3::2]
        def chip_far(rows, *earlier):
            if copying:
                return hop(rows, core, *earlier)
            return [hop(rows[i * size : (i + 1) * size], core, *earlier) for i in range(3)]

        back_events = []
        dnormed2_packed = scatter_all(
            back_most,
            chip_far(back_far),
            back_corner[:size],
            back_corner[size:],
            back_events,
            True,
        )
        dnormed2 = streams(dnormed2_packed)
        if copying:
            gate_up_grad = [rows_contract(kept[i], both_rows[i]) for i in range(2)]
            down_grad = [rows_contract(hidden_rows[i], kept[2 + i]) for i in range(2)]
        else:
            gate_up_grad = [0.0, 0.0]
            down_grad = [0.0, 0.0]
            for i, ((token, token_at), (grad, grad_at)) in enumerate(
                zip(token_pieces, grad_pieces, strict=True)
            ):
                rows = slice(i * size, (i + 1) * size)
                token = streams(token[token_at * size : (token_at + 1) * size])
                grad = streams(grad[grad_at * size : (grad_at + 1) * size])
                for j in range(2):
                    gate_up_grad[j] = gate_up_grad[j] + rows_contract(token[j], both_rows[j][rows])
                    down_grad[j] = down_grad[j] + rows_contract(hidden_rows[j][rows], grad[j])
        gate_up_grad = [grad.astype(low) for grad in gate_up_grad]
        down_grad = [grad.astype(low) for grad in down_grad]

        def gradient_packet(k):
            peer = at["wide"] ^ k
            parts = []
            for i in range(2):
                both = lax.dynamic_slice_in_dim(gate_up_grad[i], peer * depth[i], depth[i], 0)
                down = lax.dynamic_slice_in_dim(down_grad[i], peer * depth[i], depth[i], 1)
                parts += [both[:, : units[i]], both[:, units[i] :], down]
            return pack(parts)

        if aligned:
            packets = copy_blocks(
                packet_plan(
                    True,
                    lambda k: packet_places(
                        k,
                        lambda k, d, f, ref: (block(ref[k], d), span(0, f)),
                        lambda k, d, f, ref: (block(ref[k], d), span(f, f)),
                        lambda k, d, f, part, ref: (span(part * d, d), block(ref[k], d)),
                        (0, 0, 1, 2, 2, 3),
                    ),
                ),
                peers,
                [gate_up_grad[0], down_grad[0], gate_up_grad[1], down_grad[1]],
                [packet_shape] * n_wide,
                "pack_gradients",
            )
            packets = dict(enumerate(packets))
            gradient_packet = packets.get
        else:
            packets = {0: gradient_packet(0)}
        send_packets(share(4, 5), gradient_packet)
        send_packets(share(2, 3), gradient_packet)
        send_packets(share(6, 7), gradient_packet, back_events[1])
        dmiddle = []
        grad_second = []
        for stream, dout_part in enumerate(streams(dout)):
            from_norm, gain_part = norm_back(middle[stream], second_gain[stream], dnormed2[stream])
            dmiddle.append(dout_part + from_norm)
            grad_second.append(gain_part)
        att_events = []
        grad_att = streams(
            gather_rows(
                jnp.concatenate([part.astype(low) for part in dmiddle], axis=1),
                narrow_links,
                att_events,
            )
        )
        send_packets(share(5, 6), gradient_packet, att_events[0])
        send_packets(share(0, 2), gradient_packet, att_events[0])
        return_events = []

        def return_wide(parts, links, events=None, earlier=()):
            blocks = jnp.concatenate(
                [part.astype(low).reshape(n_wide, -1, part.shape[1]) for part in parts], axis=1
            )
            return scatter_blocks(blocks, links, at, events, earlier)

        out_grads = return_wide(
            [rows_contract(grad_att[stream], mixed_rows[stream]) for stream in range(2)],
            wide_links[::-1],
            return_events,
        )
        send_packets(share(7, 8), gradient_packet, return_events[0])
        send_packets(share(3, 4), gradient_packet, return_events[0])
        grad_out_w = [out_grads[: query_depth[0]].T, out_grads[query_depth[0] :].T]
        dmixed = jnp.concatenate(
            [product(grad_att[stream], out_weight[stream]) for stream in range(2)],
            axis=0,
        )
        dmixed = dmixed.astype(low).reshape(total_rows, -1, head_dim)
        recomputed = jnp.exp(masked_scores(queries, key_rows, allowed) - log_total)
        dprobs = jnp.einsum("qhd,kd->hqk", dmixed, values, preferred_element_type=wider)
        row_inner = jnp.sum(recomputed * dprobs, axis=-1, keepdims=True)
        dscores = (recomputed * (dprobs - row_inner)).astype(low)
        dquery = jnp.einsum("hqk,kd->qhd", dscores, key_rows, preferred_element_type=wider)
        dquery = (dquery.astype(low) * scaling).reshape(total_rows, -1)
        grad_key = jnp.einsum("hqk,qhd->kd", dscores, queries, preferred_element_type=wider)
        dvalue = jnp.einsum(
            "hqk,qhd->kd", recomputed.astype(low), dmixed, preferred_element_type=wider
        )
        grad_keyval = jnp.concatenate([grad_key, dvalue], axis=1).astype(low)
        dquery_rows = [dquery[:prefix_len], dquery[prefix_len:]]
        keyval_rows = [grad_keyval[:prefix_len], grad_keyval[prefix_len:]]
        query_links = [[side] + far[::-1], far[::-1] + [side]]
        query_grads = jnp.concatenate(
            [
                return_wide(
                    [
                        rows_contract(
                            all_normed[stream],
                            dquery_rows[stream][:, part * query_half : (part + 1) * query_half],
                        )
                        for stream in range(2)
                    ],
                    query_links[part],
                    None,
                    [(return_events[0],)],
                )
                for part in range(2)
            ],
            axis=1,
        )
        grad_query_w = [query_grads[: query_depth[0]], query_grads[query_depth[0] :]]
        wide_mlp = []
        for i, (gate_w, down_w) in enumerate(((wg_prefix, wd_prefix), (wg_action, wd_action))):
            wide_mlp += [
                jnp.zeros(gate_w.shape, wider),
                jnp.zeros(gate_w.shape, wider),
                jnp.zeros(down_w.shape, wider),
            ]
        for k, packet in packets.items():
            peer = at["wide"] ^ k
            parts = unpack(packet)
            for i in range(6):
                wide_mlp[i] = lax.dynamic_update_slice_in_dim(
                    wide_mlp[i],
                    parts[i].astype(wider),
                    peer * units[i // 3],
                    0 if i % 3 == 2 else 1,
                )

        dnormed_parts = []
        grad_first = []
        for stream in range(2):
            dnormed = cols_contract(keyval_rows[stream], keyval_weight[stream])
            for part in range(2):
                dnormed = dnormed + cols_contract(
                    dquery_rows[stream][:, part * query_half : (part + 1) * query_half],
                    query_weight[stream][part],
                )
            wide_rows = item_rows[stream].astype(wider)
            unit_rows = wide_rows * lax.rsqrt(
                jnp.mean(wide_rows * wide_rows, axis=-1, keepdims=True) + epsilon
            )
            grad_first.append(jnp.sum(dnormed * unit_rows, axis=0))
            dnormed_parts.append(dnormed.astype(low))
        dnormed = streams(
            scatter_rows(jnp.concatenate(dnormed_parts, axis=1), [core, across], [])
        )
        grad_inputs = [
            dmiddle[stream] + norm_back(inputs[stream], first_gain[stream], dnormed[stream])[0]
            for stream in range(2)
        ]
        gain_grads = jnp.concatenate(
            [
                part.reshape(n_all, -1)
                for part in (grad_first[0], grad_second[0], grad_first[1], grad_second[1])
            ],
            axis=1,
        )
        shared_grads = scatter_blocks(
            jnp.concatenate(
                [
                    rows_contract(all_normed[stream], keyval_rows[stream])
                    .astype(low)
                    .reshape(n_all, -1, 2 * head_dim)
                    for stream in range(2)
                ]
                + [pad_gains(gain_grads.astype(low))],
                axis=1,
            ),
            [core, across, side] + far[::-1],
            at,
        )
        grad_keyval_w = [
            shared_grads[: keyval_rows_of[0]],
            shared_grads[keyval_rows_of[0] : gain_start],
        ]
        gain_grads = shared_grads[gain_start]
        small = [
            gain_grads[stop - size : stop]
            for stop, size in zip(gain_stops, gain_sizes, strict=True)
        ]
        mlp_out = streams(
            scatter_all(
                out_most,
                chip_far(out_far, back_events[-1]),
                out_corner[:size],
                out_corner[size:],
                [],
                False,
                [
                    (back_events[-1],),
                    (att_events[0],),
                    (att_events[1],),
                    (return_events[0],),
                    (return_events[1],),
                ],
            )
        )
        outputs = [(middle[stream] + mlp_out[stream]).astype(low) for stream in range(2)]
        weights = [
            (
                grad_query_w[i],
                grad_keyval_w[i][:, :head_dim],
                grad_keyval_w[i][:, head_dim:],
                grad_out_w[i],
                *wide_mlp[3 * i : 3 * i + 3],
                small[2 * i],
                small[2 * i + 1],
            )
            for i in range(2)
        ]
        return (*outputs, *grad_inputs, *weights[0], *weights[1])

    return local


def solution(mesh):
    rows = P(BOTH, None)
    block = P("wide", "narrow")
    turned = P("narrow", "wide")
    vector = P(BOTH)
    weights = (block, rows, rows, turned, block, block, turned, vector, vector)
    return jax.shard_map(
        make_local(mesh.shape["wide"], mesh.shape["narrow"]),
        mesh=mesh,
        in_specs=(
            rows,
            rows,
            rows,
            rows,
            P("wide", None),
            P("wide", None),
            P("wide"),
            P("wide"),
            *weights,
            *weights,
        ),
        out_specs=(rows, rows, rows, rows, *weights, *weights),
        check_vma=False,
    )
```

time: 3400 us -> 1030 us (0.30)
  waiting for transfers between devices: 2910 us -> 588 us
  blocking collectives: 205 us -> 0 us
  starting transfers between devices: 2.29 us -> 126 us
  matrix products: 171 us -> 56.9 us
  Pallas kernels: 0 us -> 74.4 us
  local copies, waits for them, and re-layouts: 32.1 us -> 81.4 us
  other arithmetic: 48.3 us -> 86.6 us
    reduce_scatter x20 -> x0, waiting for transfers between devices: 1850 us -> none  [the longest x1 284 us: local(): lax.psum_scatter(grad_gate_w[0].astype(jnp.bfloat16), 'wide', scatter_dim...]
    all_gather x16 -> x0, waiting for transfers between devices: 956 us -> none  [the longest x1 230 us: local(): lax.all_gather(wd_prefix, 'wide', axis=1, tiled=True)]
    ppermute x0 -> x79, waiting for transfers between devices: none -> 588 us  [hop(): lax.ppermute(value, axis, [(i, i ^ mask) for i in range(sizes[axis])])]
    ppermute x0 -> x79, starting transfers between devices: none -> 126 us  [hop(): lax.ppermute(value, axis, [(i, i ^ mask) for i in range(sizes[axis])])]
    all_gather x8 -> x0, blocking collectives: 122 us -> none  [the longest x1 42.8 us: local(): lax.all_gather(wk_action, ('wide', 'narrow'), axis=0, tiled=True)]
    unnamed x44 -> x0, waiting for transfers between devices: 108 us -> none
    unnamed x2 -> x0, blocking collectives: 82.6 us -> none
    pallas_call x0 -> x6, Pallas kernels: none -> 74.4 us  [the longest x3 67 us: feed_forward(): pl.pallas_call(functools.partial(feed_kernel, count, half, len(kept), n_c...]
  transfers between devices with their start and end apart: 40 -> 79, of which waited for: 35 -> 40; matrix products, arithmetic and copies ran while one was open for 7% -> 19% of each run, Pallas kernels for 0% -> 5%
where the time goes in v1:
time: 1030 us; the launch traced here: 1020 us
  waiting for transfers between devices  588 us (57%)
  starting transfers between devices  126 us (12%)
  other arithmetic  86.6 us (8%)
  local copies, waits for them, and re-layouts  81.4 us (8%)
  Pallas kernels  74.4 us (7%)
  matrix products  56.9 us (6%)
    ppermute x79, waiting for transfers between devices, hop(): lax.ppermute(value, axis, [(i, i ^ mask) for i in range(sizes[axis])])  588 us
    ppermute x79, starting transfers between devices, hop(): lax.ppermute(value, axis, [(i, i ^ mask) for i in range(sizes[axis])])  126 us
    pallas_call x3, Pallas kernels, feed_forward(): pl.pallas_call(functools.partial(feed_kernel, count, half, len(kept), n_c...  67 us
    unnamed x386, local copies, waits for them, and re-layouts  33.5 us
    dot_general x12, matrix products, rows_contract(): lax.dot_general(former, latter, (((0,), (0,)), ((), ())), preferred_eleme...  28.1 us
  transfers between devices with their start and end apart: 79, of which 40 were waited for; matrix products, arithmetic and copies ran while one was open for 19% of the time, Pallas kernels for 5%

profile of v1, /device:TPU:0, one launch (start us, length us, event | category | flops | bytes accessed | tf_op | source)
XLA Modules:
  0.0 1018.8 jit_solution(4970445382882346691)
XLA Ops:
  3.9 3.0 collective-permute-start
  10.5 2.6 collective-permute-start.7
  30.1 2.8 pack_weights.1
  39.6 2.7 collective-permute-start.1
  50.6 28.8 %collective-permute-done.1 = bf16[2,384,256]{2,1,0:T(8,128)(2,1)S(1)} collective-permute-done((bf16[2,384,256]{2,1,0:T(8,128)(2,1)S(1)}, bf16[2,384,256]{2,1,0:T(8,128)(2,1)S(1)}, u32[]{:S(2)}, u32[]{:S(2)}) %collective-permute-start.1) | collective-permute-done | bytes 393248 | tf_op jit(solution)/shard_map/ppermute | solution.py:199
  79.7 8.4 collective-permute-start.16
  89.3 25.4 %collective-permute-done.2 = bf16[384,512]{1,0:T(8,128)(2,1)S(1)} collective-permute-done((bf16[384,512]{1,0:T(8,128)(2,1)S(1)}, bf16[384,512]{1,0:T(8,128)(2,1)S(1)}, u32[]{:S(2)}, u32[]{:S(2)}) %collective-permute-start.2) | collective-permute-done | bytes 393248 | tf_op jit(solution)/shard_map/ppermute | solution.py:199
  116.0 3.2 collective-permute-start.3
  122.9 13.3 %collective-permute-done.16 = bf16[2,2,384,256]{3,2,1,0:T(8,128)(2,1)S(1)} collective-permute-done((bf16[2,2,384,256]{3,2,1,0:T(8,128)(2,1)S(1)}, bf16[2,2,384,256]{3,2,1,0:T(8,128)(2,1)S(1)}, u32[]{:S(2)}, u32[]{:S(2)}) %collective-permute-start.16) | collective-permute-done | bytes 786464 | tf_op jit(solution)/shard_map/ppermute | solution.py:199
  139.8 9.0 collective-permute-done.3
  170.0 12.7 %collective-permute-done.4 = bf16[2,2,384,512]{3,2,0,1:T(8,128)(2,1)} collective-permute-done((bf16[2,2,384,512]{3,2,0,1:T(8,128)(2,1)}, bf16[2,2,384,512]{3,2,0,1:T(8,128)(2,1)}, u32[]{:S(2)}, u32[]{:S(2)}) %collective-permute-start.4) | collective-permute-done | bytes 1572896 | tf_op jit(solution)/shard_map/ppermute | solution.py:199
  192.0 38.5 %collective-permute-done.18.refs_5_ = bf16[896,512]{1,0:T(8,128)(2,1)S(1)} collective-permute-done((bf16[896,512]{1,0:T(8,128)(2,1)S(1)}, bf16[896,512]{1,0:T(8,128)(2,1)S(1)}, u32[]{:S(2)}, u32[]{:S(2)}) %collective-permute-start.18) | collective-permute-done | bytes 917536 | tf_op jit(solution)/shard_map/ppermute | solution.py:199
  235.4 6.2 collective-permute-done.19
  244.2 10.4 %collective-permute-done.20.refs_1_ = bf16[896,512]{1,0:T(8,128)(2,1)} collective-permute-done((bf16[896,512]{1,0:T(8,128)(2,1)}, bf16[896,512]{1,0:T(8,128)(2,1)}, u32[]{:S(2)}, u32[]{:S(2)}) %collective-permute-start.20) | collective-permute-done | bytes 917536 | tf_op jit(solution)/shard_map/ppermute | solution.py:199
  256.1 15.1 %collective-permute-done.21 = bf16[64,3072]{1,0:T(8,128)(2,1)S(1)} collective-permute-done((bf16[64,3072]{1,0:T(8,128)(2,1)S(1)}, bf16[64,3072]{1,0:T(8,128)(2,1)S(1)}, u32[]{:S(2)}, u32[]{:S(2)}) %collective-permute-start.21) | collective-permute-done | bytes 393248 | tf_op jit(solution)/shard_map/ppermute | solution.py:199
  271.3 15.6 %collective-permute-done.29 = bf16[256,3072]{1,0:T(8,128)(2,1)S(1)} collective-permute-done((bf16[256,3072]{1,0:T(8,128)(2,1)S(1)}, bf16[256,3072]{1,0:T(8,128)(2,1)S(1)}, u32[]{:S(2)}, u32[]{:S(2)}) %collective-permute-start.29) | collective-permute-done | bytes 1572896 | tf_op jit(solution)/shard_map/ppermute | solution.py:199
  286.9 3.8 collective-permute-done.22
  301.3 18.7 %collective-permute-done.23.refs_7_ = bf16[896,512]{1,0:T(8,128)(2,1)S(1)} collective-permute-done((bf16[896,512]{1,0:T(8,128)(2,1)S(1)}, bf16[896,512]{1,0:T(8,128)(2,1)S(1)}, u32[]{:S(2)}, u32[]{:S(2)}) %collective-permute-start.23) | collective-permute-done | bytes 917536 | tf_op jit(solution)/shard_map/ppermute | solution.py:199
  320.6 7.5 collective-permute-done.30
  332.6 27.3 %collective-permute-done.24.refs_1_ = bf16[256,3072]{1,0:T(8,128)(2,1)S(1)} collective-permute-done((bf16[256,3072]{1,0:T(8,128)(2,1)S(1)}, bf16[256,3072]{1,0:T(8,128)(2,1)S(1)}, u32[]{:S(2)}, u32[]{:S(2)}) %collective-permute-start.24) | collective-permute-done | bytes 1572896 | tf_op jit(solution)/shard_map/ppermute | solution.py:199
  361.3 4.8 collective-permute-done.25.refs_2_
  367.5 11.9 %collective-permute-start.32 = (bf16[896,512]{1,0:T(8,128)(2,1)S(1)}, bf16[896,512]{1,0:T(8,128)(2,1)S(1)}, u32[]{:S(2)}, u32[]{:S(2)}) collective-permute-start(bf16[896,512]{1,0:T(8,128)(2,1)S(1)} %copy-done.13), channel_id=1, source_target_pairs={{0,12},{4,8},{8,4},{12,0},{16,28},{20,24},{24,20},{28,16},{1,13},{... | collective-permute-start | bytes 2752520 | tf_op jit(solution)/shard_map/ppermute | solution.py:199
  379.5 20.9 %collective-permute-done.32.refs_3_ = bf16[896,512]{1,0:T(8,128)(2,1)S(1)} collective-permute-done((bf16[896,512]{1,0:T(8,128)(2,1)S(1)}, bf16[896,512]{1,0:T(8,128)(2,1)S(1)}, u32[]{:S(2)}, u32[]{:S(2)}) %collective-permute-start.32) | collective-permute-done | bytes 917536 | tf_op jit(solution)/shard_map/ppermute | solution.py:199
  402.5 2.7 collective-permute-start.31
  405.2 14.5 %collective-permute-done.36 = bf16[128,3072]{1,0:T(8,128)(2,1)S(1)} collective-permute-done((bf16[128,3072]{1,0:T(8,128)(2,1)S(1)}, bf16[128,3072]{1,0:T(8,128)(2,1)S(1)}, u32[]{:S(2)}, u32[]{:S(2)}) %collective-permute-start.36) | collective-permute-done | bytes 786464 | tf_op jit(solution)/shard_map/ppermute | solution.py:199
  423.1 2.9 collective-permute-done.31.refs_2_
  426.0 19.8 %collective-permute-done.33.refs_6_ = bf16[896,512]{1,0:T(8,128)(2,1)S(1)} collective-permute-done((bf16[896,512]{1,0:T(8,128)(2,1)S(1)}, bf16[896,512]{1,0:T(8,128)(2,1)S(1)}, u32[]{:S(2)}, u32[]{:S(2)}) %collective-permute-start.33) | collective-permute-done | bytes 917536 | tf_op jit(solution)/shard_map/ppermute | solution.py:199
  451.5 22.8 %feed_forward.3 = (bf16[2048,2048]{1,0:T(8,128)(2,1)}, bf16[2048,1024]{1,0:T(8,128)(2,1)}, bf16[2048,2048]{1,0:T(8,128)(2,1)}, bf16[2048,1024]{1,0:T(8,128)(2,1)...) custom-call(bf16[256,3072]{1,0:T(8,128)(2,1)} %copy-done.94, ...), custom_call_target="tpu_custom_call" | custom-call | flops 10871635968 | bytes 28311552 | tf_op jit(solution)/shard_map/feed_forward/pallas_call | solution.py:157
  474.4 18.8 %feed_forward.4 = (bf16[2048,2048]{1,0:T(8,128)(2,1)}, bf16[2048,1024]{1,0:T(8,128)(2,1)}, bf16[2048,2048]{1,0:T(8,128)(2,1)}, bf16[2048,1024]{1,0:T(8,128)(2,1)...) custom-call(bf16[256,3072]{1,0:T(8,128)(2,1)} %constant_dynamic-upda, ...), custom_call_target="tpu_custom_call", output_to_operand_aliasing={{0}: (8, {}), {1}: (9, {}), {2}: (10, {}), {3}: (11, {}), {... | custom-call | flops 7247757312 | bytes 18874368 | tf_op jit(solution)/shard_map/feed_forward/pallas_call | solution.py:157
  493.2 25.4 %feed_forward.5 = (bf16[2048,2048]{1,0:T(8,128)(2,1)}, bf16[2048,1024]{1,0:T(8,128)(2,1)}, bf16[2048,2048]{1,0:T(8,128)(2,1)}, bf16[2048,1024]{1,0:T(8,128)(2,1)...) custom-call(bf16[768,3072]{1,0:T(8,128)(2,1)} %collective-permute-do, ...), custom_call_target="tpu_custom_call", output_to_operand_aliasing={{0}: (10, {}), {1}: (11, {}), {2}: (12, {}), {3}: (13, {}),... | custom-call | flops 10871635968 | bytes 28311552 | tf_op jit(solution)/shard_map/feed_forward/pallas_call | solution.py:157
  522.5 2.7 copy.110
  533.9 4.0 convert_add_fusion.3
  538.0 13.4 %collective-permute-done.43 = bf16[128,3072]{1,0:T(8,128)(2,1)S(1)} collective-permute-done((bf16[128,3072]{1,0:T(8,128)(2,1)S(1)}, bf16[128,3072]{1,0:T(8,128)(2,1)S(1)}, u32[]{:S(2)}, u32[]{:S(2)}) %collective-permute-start.43) | collective-permute-done | bytes 786464 | tf_op jit(solution)/shard_map/ppermute | solution.py:199
  556.2 9.6 convolution_convert_fusion.refs_0_
  565.8 4.7 convolution_convert_fusion.3.refs_1_
  570.6 16.9 %collective-permute-done.44 = bf16[256,3072]{1,0:T(8,128)(2,1)} collective-permute-done((bf16[256,3072]{1,0:T(8,128)(2,1)S(1)}, bf16[256,3072]{1,0:T(8,128)(2,1)}, u32[]{:S(2)}, u32[]{:S(2)}) %collective-permute-start.44) | collective-permute-done | bytes 1572896 | tf_op jit(solution)/shard_map/ppermute | solution.py:199
  587.5 2.9 collective-permute-done.42
  590.3 3.4 add_convert_fusion.4
  593.8 16.0 %collective-permute-start.45 = (bf16[128,3072]{1,0:T(8,128)(2,1)S(1)}, bf16[128,3072]{1,0:T(8,128)(2,1)S(1)}, u32[]{:S(2)}, u32[]{:S(2)}) collective-permute-start(bf16[128,3072]{1,0:T(8,128)(2,1)S(1)} %slice.733), channel_id=1, source_target_pairs={{0,8},{4,12},{8,0},{12,4},{16,24},{20,28},{24,16},{28,20},{1,9},{5... | collective-permute-start | bytes 2359304 | tf_op jit(solution)/shard_map/ppermute | solution.py:199
  619.5 29.8 %collective-permute-done.45 = bf16[128,3072]{1,0:T(8,128)(2,1)S(1)} collective-permute-done((bf16[128,3072]{1,0:T(8,128)(2,1)S(1)}, bf16[128,3072]{1,0:T(8,128)(2,1)S(1)}, u32[]{:S(2)}, u32[]{:S(2)}) %collective-permute-start.45) | collective-permute-done | bytes 786464 | tf_op jit(solution)/shard_map/ppermute | solution.py:199
  650.3 31.4 %collective-permute-done.46 = bf16[64,3072]{1,0:T(8,128)(2,1)S(1)} collective-permute-done((bf16[64,3072]{1,0:T(8,128)(2,1)S(1)}, bf16[64,3072]{1,0:T(8,128)(2,1)S(1)}, u32[]{:S(2)}, u32[]{:S(2)}) %collective-permute-start.46) | collective-permute-done | bytes 393248 | tf_op jit(solution)/shard_map/ppermute | solution.py:199
  689.0 5.6 collective-permute-done.48
  698.1 11.3 %collective-permute-done.77 = bf16[896,512]{1,0:T(8,128)(2,1)S(1)} collective-permute-done((bf16[896,512]{1,0:T(8,128)(2,1)S(1)}, bf16[896,512]{1,0:T(8,128)(2,1)S(1)}, u32[]{:S(2)}, u32[]{:S(2)}) %collective-permute-start.77) | collective-permute-done | bytes 917536 | tf_op jit(solution)/shard_map/ppermute | solution.py:199
  712.9 18.2 %collective-permute-start.76 = (bf16[896,512]{1,0:T(8,128)(2,1)S(1)}, bf16[896,512]{1,0:T(8,128)(2,1)}, u32[]{:S(2)}, u32[]{:S(2)}) collective-permute-start(bf16[896,512]{1,0:T(8,128)(2,1)S(1)} %get-tuple-element.188), channel_id=1, source_target_pairs={{0,20},{4,16},{8,28},{12,24},{16,4},{20,0},{24,12},{28,8},{1,21},{... | collective-permute-start | bytes 2752520 | tf_op jit(solution)/shard_map/ppermute | solution.py:199
  752.9 4.3 copy.107
  757.2 2.6 convolution_convert_fusion.8
  762.1 2.8 fusion.17
  770.9 5.3 fusion.6
  794.5 7.8 collective-permute-done.59
  810.8 13.5 %collective-permute-done.60 = bf16[2,2,384,256]{3,2,0,1:T(8,128)(2,1)S(1)} collective-permute-done((bf16[2,2,384,256]{3,2,0,1:T(8,128)(2,1)S(1)}, bf16[2,2,384,256]{3,2,0,1:T(8,128)(2,1)S(1)}, u32[]{:S(2)}, u32[]{:S(2)}) %collective-permute-start.60) | collective-permute-done | bytes 786464 | tf_op jit(solution)/shard_map/ppermute | solution.py:199
  824.6 20.7 %collective-permute-done.63 = bf16[2,2,384,256]{3,2,1,0:T(8,128)(2,1)S(1)} collective-permute-done((bf16[2,2,384,256]{3,2,1,0:T(8,128)(2,1)S(1)}, bf16[2,2,384,256]{3,2,1,0:T(8,128)(2,1)S(1)}, u32[]{:S(2)}, u32[]{:S(2)}) %collective-permute-start.63) | collective-permute-done | bytes 786464 | tf_op jit(solution)/shard_map/ppermute | solution.py:199
  848.9 28.2 %collective-permute-done.74 = bf16[896,512]{1,0:T(8,128)(2,1)S(1)} collective-permute-done((bf16[896,512]{1,0:T(8,128)(2,1)S(1)}, bf16[896,512]{1,0:T(8,128)(2,1)S(1)}, u32[]{:S(2)}, u32[]{:S(2)}) %collective-permute-start.74) | collective-permute-done | bytes 917536 | tf_op jit(solution)/shard_map/ppermute | solution.py:199
  877.1 5.3 collective-permute-start.61
  883.5 16.2 %collective-permute-done.78 = bf16[896,512]{1,0:T(8,128)(2,1)S(1)} collective-permute-done((bf16[896,512]{1,0:T(8,128)(2,1)S(1)}, bf16[896,512]{1,0:T(8,128)(2,1)S(1)}, u32[]{:S(2)}, u32[]{:S(2)}) %collective-permute-start.78) | collective-permute-done | bytes 917536 | tf_op jit(solution)/shard_map/ppermute | solution.py:199
  899.7 4.3 collective-permute-start.64
  906.4 9.5 collective-permute-done.61
  916.0 14.9 %collective-permute-done.64 = bf16[2,384,256]{2,1,0:T(8,128)(2,1)S(1)} collective-permute-done((bf16[2,384,256]{2,1,0:T(8,128)(2,1)S(1)}, bf16[2,384,256]{2,1,0:T(8,128)(2,1)S(1)}, u32[]{:S(2)}, u32[]{:S(2)}) %collective-permute-start.64) | collective-permute-done | bytes 393248 | tf_op jit(solution)/shard_map/ppermute | solution.py:199
  931.1 10.4 %collective-permute-done.71 = bf16[384,512]{0,1:T(8,128)(2,1)S(1)} collective-permute-done((bf16[384,512]{0,1:T(8,128)(2,1)S(1)}, bf16[384,512]{0,1:T(8,128)(2,1)S(1)}, u32[]{:S(2)}, u32[]{:S(2)}) %collective-permute-start.71) | collective-permute-done | bytes 393248 | tf_op jit(solution)/shard_map/ppermute | solution.py:199
  941.5 2.8 collective-permute-start.65
  944.4 3.0 add_convert_fusion.3
  950.8 6.3 collective-permute-done.69
  958.4 23.2 %collective-permute-done.53 = bf16[256,3072]{1,0:T(8,128)(2,1)S(1)} collective-permute-done((bf16[256,3072]{1,0:T(8,128)(2,1)S(1)}, bf16[256,3072]{1,0:T(8,128)(2,1)S(1)}, u32[]{:S(2)}, u32[]{:S(2)}) %collective-permute-start.53) | collective-permute-done | bytes 1572896 | tf_op jit(solution)/shard_map/ppermute | solution.py:199
  986.1 14.4 %collective-permute-done.55 = bf16[128,3072]{1,0:T(8,128)(2,1)S(1)} collective-permute-done((bf16[128,3072]{1,0:T(8,128)(2,1)S(1)}, bf16[128,3072]{1,0:T(8,128)(2,1)S(1)}, u32[]{:S(2)}, u32[]{:S(2)}) %collective-permute-start.55) | collective-permute-done | bytes 786464 | tf_op jit(solution)/shard_map/ppermute | solution.py:199
  1002.1 15.0 %collective-permute-done.57 = bf16[64,3072]{1,0:T(8,128)(2,1)S(1)} collective-permute-done((bf16[64,3072]{1,0:T(8,128)(2,1)S(1)}, bf16[64,3072]{1,0:T(8,128)(2,1)S(1)}, u32[]{:S(2)}, u32[]{:S(2)}) %collective-permute-start.57) | collective-permute-done | bytes 393248 | tf_op jit(solution)/shard_map/ppermute | solution.py:199
  (763 shorter events, 233.2 us)
Async XLA Ops:
  3.9 34.6 %collective-permute-start = (bf16[384,256]{1,0:T(8,128)(2,1)}, bf16[384,256]{1,0:T(8,128)(2,1)}, u32[]{:S(2)}, u32[]{:S(2)}) collective-permute-start(bf16[384,256]{1,0:T(8,128)(2,1)} %get-tuple-element.295), channel_id=1, source_target_pairs={{0,4},{4,0},{8,12},{12,8},{16,20},{20,16},{24,28},{28,24},{1,5},{5... | collective-permute-start | bytes 589832 | tf_op jit(solution)/shard_map/ppermute | solution.py:199
  8.2 41.1 %collective-permute-start.5 = (bf16[64,3072]{1,0:T(8,128)(2,1)}, bf16[64,3072]{1,0:T(8,128)(2,1)}, u32[]{:S(2)}, u32[]{:S(2)}) collective-permute-start(bf16[64,3072]{1,0:T(8,128)(2,1)} %constant_dynamic-update-slice_fusion.2), channel_id=1, source_target_pairs={{0,2},{1,3},{2,0},{3,1},{4,6},{5,7},{6,4},{7,5},{8,10},{9,11},{10,... | collective-permute-start | bytes 1179656 | tf_op jit(solution)/shard_map/ppermute | solution.py:199
  10.5 22.6 %collective-permute-start.7 = (bf16[112,512]{1,0:T(8,128)(2,1)}, bf16[112,512]{1,0:T(8,128)(2,1)}, u32[]{:S(2)}, u32[]{:S(2)}) collective-permute-start(bf16[112,512]{1,0:T(8,128)(2,1)} %fusion.91), channel_id=1, source_target_pairs={{0,16},{4,20},{8,24},{12,28},{16,0},{20,4},{24,8},{28,12},{1,17},{... | collective-permute-start | bytes 344072 | tf_op jit(solution)/shard_map/ppermute | solution.py:199
  13.1 31.6 %collective-permute-start.13 = (bf16[384,256]{1,0:T(8,128)(2,1)}, bf16[384,256]{1,0:T(8,128)(2,1)}, u32[]{:S(2)}, u32[]{:S(2)}) collective-permute-start(bf16[384,256]{1,0:T(8,128)(2,1)} %get-tuple-element.294), channel_id=1, source_target_pairs={{0,16},{4,20},{8,24},{12,28},{16,0},{20,4},{24,8},{28,12},{1,17},{... | collective-permute-start | bytes 589832 | tf_op jit(solution)/shard_map/ppermute | solution.py:199
  39.6 39.8 %collective-permute-start.1 = (bf16[2,384,256]{2,1,0:T(8,128)(2,1)S(1)}, bf16[2,384,256]{2,1,0:T(8,128)(2,1)S(1)}, u32[]{:S(2)}, u32[]{:S(2)}) collective-permute-start(bf16[2,384,256]{2,1,0:T(8,128)(2,1)S(1)} %maximum_select_fusion.15), channel_id=1, source_target_pairs={{0,16},{4,20},{8,24},{12,28},{16,0},{20,4},{24,8},{28,12},{1,17},{... | collective-permute-start | bytes 1179656 | tf_op jit(solution)/shard_map/ppermute | solution.py:199
  42.3 73.8 %collective-permute-start.11 = (bf16[896,512]{1,0:T(8,128)(2,1)S(1)}, bf16[896,512]{1,0:T(8,128)(2,1)S(1)}, u32[]{:S(2)}, u32[]{:S(2)}) collective-permute-start(bf16[896,512]{1,0:T(8,128)(2,1)S(1)} %get-tuple-element.112), channel_id=1, source_target_pairs={{0,16},{4,20},{8,24},{12,28},{16,0},{20,4},{24,8},{28,12},{1,17},{... | collective-permute-start | bytes 2752520 | tf_op jit(solution)/shard_map/ppermute | solution.py:199
  45.9 33.7 %collective-permute-start.14 = (bf16[2,384,256]{2,1,0:T(8,128)(2,1)S(1)}, bf16[2,384,256]{2,1,0:T(8,128)(2,1)S(1)}, u32[]{:S(2)}, u32[]{:S(2)}) collective-permute-start(bf16[2,384,256]{2,1,0:T(8,128)(2,1)S(1)} %maximum_select_fusion.16), channel_id=1, source_target_pairs={{0,8},{4,12},{8,0},{12,4},{16,24},{20,28},{24,16},{28,20},{1,9},{5... | collective-permute-start | bytes 1179656 | tf_op jit(solution)/shard_map/ppermute | solution.py:199
  48.7 39.5 %collective-permute-start.9 = (bf16[2,2,112,512]{3,2,1,0:T(8,128)(2,1)S(1)}, bf16[2,2,112,512]{3,2,1,0:T(8,128)(2,1)S(1)}, u32[]{:S(2)}, u32[]{:S(2)}) collective-permute-start(bf16[2,2,112,512]{3,2,1,0:T(8,128)(2,1)S(1)} %maximum_select_fusion.14), channel_id=1, source_target_pairs={{0,4},{4,0},{8,12},{12,8},{16,20},{20,16},{24,28},{28,24},{1,5},{5... | collective-permute-start | bytes 1376264 | tf_op jit(solution)/shard_map/ppermute | solution.py:199
  50.6 68.6 %collective-permute-start.6 = (bf16[128,3072]{1,0:T(8,128)(2,1)S(1)}, bf16[128,3072]{1,0:T(8,128)(2,1)S(1)}, u32[]{:S(2)}, u32[]{:S(2)}) collective-permute-start(bf16[128,3072]{1,0:T(8,128)(2,1)S(1)} %pad_maximum_fusion.11), channel_id=1, source_target_pairs={{0,1},{1,0},{2,3},{3,2},{4,5},{5,4},{6,7},{7,6},{8,9},{9,8},{10,11... | collective-permute-start | bytes 2359304 | tf_op jit(solution)/shard_map/ppermute | solution.py:199
  79.4 35.3 %collective-permute-start.2 = (bf16[384,512]{1,0:T(8,128)(2,1)S(1)}, bf16[384,512]{1,0:T(8,128)(2,1)S(1)}, u32[]{:S(2)}, u32[]{:S(2)}) collective-permute-start(bf16[384,512]{1,0:T(8,128)(2,1)S(1)} %get-tuple-element.110), channel_id=1, source_target_pairs={{0,16},{4,20},{8,24},{12,28},{16,0},{20,4},{24,8},{28,12},{1,17},{... | collective-permute-start | bytes 1179656 | tf_op jit(solution)/shard_map/ppermute | solution.py:199
  79.7 56.5 %collective-permute-start.16 = (bf16[2,2,384,256]{3,2,1,0:T(8,128)(2,1)S(1)}, bf16[2,2,384,256]{3,2,1,0:T(8,128)(2,1)S(1)}, u32[]{:S(2)}, u32[]{:S(2)}) collective-permute-start(bf16[2,2,384,256]{3,2,1,0:T(8,128)(2,1)S(1)} %maximum_select_fusion.12), channel_id=1, source_target_pairs={{0,8},{4,12},{8,0},{12,4},{16,24},{20,28},{24,16},{28,20},{1,9},{5... | collective-permute-start | bytes 2359304 | tf_op jit(solution)/shard_map/ppermute | solution.py:199
  88.2 27.4 %collective-permute-start.10 = (bf16[2,2,2,112,512]{4,3,2,1,0:T(8,128)(2,1)S(1)}, bf16[2,2,2,112,512]{4,3,2,1,0:T(8,128)(2,1)S(1)}, u32[]{:S(2)}, u32[]{:S(2)}) collective-permute-start(bf16[2,2,2,112,512]{4,3,2,1,0:T(8,128)(2,1)S(1)} %maximum_select_fusion.8), channel_id=1, source_target_pairs={{0,2},{1,3},{2,0},{3,1},{4,6},{5,7},{6,4},{7,5},{8,10},{9,11},{10,... | collective-permute-start | bytes 2752520 | tf_op jit(solution)/shard_map/ppermute | solution.py:199
  114.7 22.7 %collective-permute-start.15 = (bf16[2,2,384,256]{3,2,0,1:T(8,128)(2,1)S(1)}, bf16[2,2,384,256]{3,2,0,1:T(8,128)(2,1)S(1)}, u32[]{:S(2)}, u32[]{:S(2)}) collective-permute-start(bf16[2,2,384,256]{3,2,0,1:T(8,128)(2,1)S(1)} %maximum_select_fusion.10), channel_id=1, source_target_pairs={{0,4},{4,0},{8,12},{12,8},{16,20},{20,16},{24,28},{28,24},{1,5},{5... | collective-permute-start | bytes 2359304 | tf_op jit(solution)/shard_map/ppermute | solution.py:199
  115.6 71.9 %collective-permute-start.26 = (bf16[64,3072]{1,0:T(8,128)(2,1)}, bf16[64,3072]{1,0:T(8,128)(2,1)}, u32[]{:S(2)}, u32[]{:S(2)}) collective-permute-start(bf16[64,3072]{1,0:T(8,128)(2,1)} %get-tuple-element.124), channel_id=1, source_target_pairs={{0,16},{4,20},{8,24},{12,28},{16,0},{20,4},{24,8},{28,12},{1,17},{... | collective-permute-start | bytes 1179656 | tf_op jit(solution)/shard_map/ppermute | solution.py:199
  116.0 32.8 %collective-permute-start.3 = (bf16[2,384,512]{2,1,0:T(8,128)(2,1)S(1)}, bf16[2,384,512]{2,1,0:T(8,128)(2,1)S(1)}, u32[]{:S(2)}, u32[]{:S(2)}) collective-permute-start(bf16[2,384,512]{2,1,0:T(8,128)(2,1)S(1)} %maximum_select_fusion.9), channel_id=1, source_target_pairs={{0,8},{4,12},{8,0},{12,4},{16,24},{20,28},{24,16},{28,20},{1,9},{5... | collective-permute-start | bytes 2359304 | tf_op jit(solution)/shard_map/ppermute | solution.py:199
  119.2 32.9 %collective-permute-start.12 = (bf16[2,2,2,2,112,512]{5,4,2,1,0,3:T(8,128)(2,1)S(1)}, bf16[2,2,2,2,112,512]{5,4,2,1,0,3:T(8,128)(2,1)S(1)}, u32[]{:S(2)}, u32[]{:S(2)}) collective-permute-start(bf16[2,2,2,2,112,512]{5,4,2,1,0,3:T(8,128)(2,1)S(1)} %maximum_select_fusion.2), channel_id=1, source_target_pairs={{0,1},{1,0},{2,3},{3,2},{4,5},{5,4},{6,7},{7,6},{8,9},{9,8},{10,11... | collective-permute-start | bytes 5505032 | tf_op jit(solution)/shard_map/ppermute | solution.py:199
  150.2 32.5 %collective-permute-start.4 = (bf16[2,2,384,512]{3,2,0,1:T(8,128)(2,1)}, bf16[2,2,384,512]{3,2,0,1:T(8,128)(2,1)}, u32[]{:S(2)}, u32[]{:S(2)}) collective-permute-start(bf16[2,2,384,512]{3,2,0,1:T(8,128)(2,1)} %maximum_select_fusion.4), channel_id=1, source_target_pairs={{0,4},{4,0},{8,12},{12,8},{16,20},{20,16},{24,28},{28,24},{1,5},{5... | collective-permute-start | bytes 4718600 | tf_op jit(solution)/shard_map/ppermute | solution.py:199
  187.5 42.9 %collective-permute-start.18 = (bf16[896,512]{1,0:T(8,128)(2,1)S(1)}, bf16[896,512]{1,0:T(8,128)(2,1)S(1)}, u32[]{:S(2)}, u32[]{:S(2)}) collective-permute-start(bf16[896,512]{1,0:T(8,128)(2,1)S(1)} %copy-done.17), channel_id=1, source_target_pairs={{0,20},{4,16},{8,28},{12,24},{16,4},{20,0},{24,12},{28,8},{1,21},{... | collective-permute-start | bytes 2752520 | tf_op jit(solution)/shard_map/ppermute | solution.py:199
  189.6 42.7 %collective-permute-start.27 = (bf16[128,3072]{1,0:T(8,128)(2,1)}, bf16[128,3072]{1,0:T(8,128)(2,1)}, u32[]{:S(2)}, u32[]{:S(2)}) collective-permute-start(bf16[128,3072]{1,0:T(8,128)(2,1)} %pad_maximum_fusion.13), channel_id=1, source_target_pairs={{0,8},{4,12},{8,0},{12,4},{16,24},{20,28},{24,16},{28,20},{1,9},{5... | collective-permute-start | bytes 2359304 | tf_op jit(solution)/shard_map/ppermute | solution.py:199
  231.0 23.6 %collective-permute-start.20 = (bf16[896,512]{1,0:T(8,128)(2,1)}, bf16[896,512]{1,0:T(8,128)(2,1)}, u32[]{:S(2)}, u32[]{:S(2)}) collective-permute-start(bf16[896,512]{1,0:T(8,128)(2,1)} %get-tuple-element.120), channel_id=1, source_target_pairs={{0,4},{4,0},{8,12},{12,8},{16,20},{20,16},{24,28},{28,24},{1,5},{5... | collective-permute-start | bytes 2752520 | tf_op jit(solution)/shard_map/ppermute | solution.py:199
  233.8 53.1 %collective-permute-start.29 = (bf16[256,3072]{1,0:T(8,128)(2,1)S(1)}, bf16[256,3072]{1,0:T(8,128)(2,1)S(1)}, u32[]{:S(2)}, u32[]{:S(2)}) collective-permute-start(bf16[256,3072]{1,0:T(8,128)(2,1)S(1)} %pad_maximum_fusion.3), channel_id=1, source_target_pairs={{0,4},{4,0},{8,12},{12,8},{16,20},{20,16},{24,28},{28,24},{1,5},{5... | collective-permute-start | bytes 4718600 | tf_op jit(solution)/shard_map/ppermute | solution.py:199
  254.6 44.1 %collective-permute-start.28 = (bf16[256,3072]{1,0:T(8,128)(2,1)S(1)}, bf16[256,3072]{1,0:T(8,128)(2,1)S(1)}, u32[]{:S(2)}, u32[]{:S(2)}) collective-permute-start(bf16[256,3072]{1,0:T(8,128)(2,1)S(1)} %pad_maximum_fusion.3), channel_id=1, source_target_pairs={{0,2},{1,3},{2,0},{3,1},{4,6},{5,7},{6,4},{7,5},{8,10},{9,11},{10,... | collective-permute-start | bytes 4718600 | tf_op jit(solution)/shard_map/ppermute | solution.py:199
  271.2 19.5 %collective-permute-start.22 = (bf16[128,3072]{1,0:T(8,128)(2,1)S(1)}, bf16[128,3072]{1,0:T(8,128)(2,1)S(1)}, u32[]{:S(2)}, u32[]{:S(2)}) collective-permute-start(bf16[128,3072]{1,0:T(8,128)(2,1)S(1)} %pad_maximum_fusion.12), channel_id=1, source_target_pairs={{0,8},{4,12},{8,0},{12,4},{16,24},{20,28},{24,16},{28,20},{1,9},{5... | collective-permute-start | bytes 2359304 | tf_op jit(solution)/shard_map/ppermute | solution.py:199
  290.7 37.3 %collective-permute-start.30 = (bf16[256,3072]{1,0:T(8,128)(2,1)S(1)}, bf16[256,3072]{1,0:T(8,128)(2,1)S(1)}, u32[]{:S(2)}, u32[]{:S(2)}) collective-permute-start(bf16[256,3072]{1,0:T(8,128)(2,1)S(1)} %collective-permute-done.29), channel_id=1, source_target_pairs={{0,2},{1,3},{2,0},{3,1},{4,6},{5,7},{6,4},{7,5},{8,10},{9,11},{10,... | collective-permute-start | bytes 4718600 | tf_op jit(solution)/shard_map/ppermute | solution.py:199
  296.1 23.9 %collective-permute-start.23 = (bf16[896,512]{1,0:T(8,128)(2,1)S(1)}, bf16[896,512]{1,0:T(8,128)(2,1)S(1)}, u32[]{:S(2)}, u32[]{:S(2)}) collective-permute-start(bf16[896,512]{1,0:T(8,128)(2,1)S(1)} %copy-done.15), channel_id=1, source_target_pairs={{0,28},{4,24},{8,20},{12,16},{16,12},{20,8},{24,4},{28,0},{1,29},{... | collective-permute-start | bytes 2752520 | tf_op jit(solution)/shard_map/ppermute | solution.py:199
  320.0 39.9 %collective-permute-start.24 = (bf16[256,3072]{1,0:T(8,128)(2,1)S(1)}, bf16[256,3072]{1,0:T(8,128)(2,1)S(1)}, u32[]{:S(2)}, u32[]{:S(2)}) collective-permute-start(bf16[256,3072]{1,0:T(8,128)(2,1)S(1)} %pad_maximum_fusion.2.refs_0_), channel_id=1, source_target_pairs={{0,2},{1,3},{2,0},{3,1},{4,6},{5,7},{6,4},{7,5},{8,10},{9,11},{10,... | collective-permute-start | bytes 4718600 | tf_op jit(solution)/shard_map/ppermute | solution.py:199
  329.3 145.0 %collective-permute-start.35 = (bf16[1024,3072]{1,0:T(8,128)(2,1)}, bf16[1024,3072]{1,0:T(8,128)(2,1)}, u32[]{:S(2)}, u32[]{:S(2)}) collective-permute-start(bf16[1024,3072]{1,0:T(8,128)(2,1)} %constant_dynamic-update-slice_fusion.5.refs_3_.refs_4_.refs_5_.refs_2_), channel_id=1, source_target_pairs={{0,1},{1,0},{2,3},{3,2},{4,5},{5,4},{6,7},{7,6},{8,9},{9,8},{10,11... | collective-permute-start | bytes 18874376 | tf_op jit(solution)/shard_map/ppermute | solution.py:199
  329.3 36.8 %collective-permute-start.25 = (bf16[256,3072]{1,0:T(8,128)(2,1)S(1)}, bf16[256,3072]{1,0:T(8,128)(2,1)S(1)}, u32[]{:S(2)}, u32[]{:S(2)}) collective-permute-start(bf16[256,3072]{1,0:T(8,128)(2,1)S(1)} %pad_maximum_fusion.2.refs_0_), channel_id=1, source_target_pairs={{0,4},{4,0},{8,12},{12,8},{16,20},{20,16},{24,28},{28,24},{1,5},{5... | collective-permute-start | bytes 4718600 | tf_op jit(solution)/shard_map/ppermute | solution.py:199
  367.5 125.7 %collective-permute-start.34 = (bf16[768,3072]{1,0:T(8,128)(2,1)}, bf16[768,3072]{1,0:T(8,128)(2,1)}, u32[]{:S(2)}, u32[]{:S(2)}) collective-permute-start(bf16[768,3072]{1,0:T(8,128)(2,1)} %constant_dynamic-update-slice_fusion.11), channel_id=1, source_target_pairs={{0,1},{1,0},{2,3},{3,2},{4,5},{5,4},{6,7},{7,6},{8,9},{9,8},{10,11... | collective-permute-start | bytes 14155784 | tf_op jit(solution)/shard_map/ppermute | solution.py:199
  367.5 32.9 %collective-permute-start.32 = (bf16[896,512]{1,0:T(8,128)(2,1)S(1)}, bf16[896,512]{1,0:T(8,128)(2,1)S(1)}, u32[]{:S(2)}, u32[]{:S(2)}) collective-permute-start(bf16[896,512]{1,0:T(8,128)(2,1)S(1)} %copy-done.13), channel_id=1, source_target_pairs={{0,12},{4,8},{8,4},{12,0},{16,28},{20,24},{24,20},{28,16},{1,13},{... | collective-permute-start | bytes 2752520 | tf_op jit(solution)/shard_map/ppermute | solution.py:199
  401.9 20.2 %collective-permute-start.37 = (bf16[128,3072]{1,0:T(8,128)(2,1)S(1)}, bf16[128,3072]{1,0:T(8,128)(2,1)S(1)}, u32[]{:S(2)}, u32[]{:S(2)}) collective-permute-start(bf16[128,3072]{1,0:T(8,128)(2,1)S(1)} %slice.722), channel_id=1, source_target_pairs={{0,4},{4,0},{8,12},{12,8},{16,20},{20,16},{24,28},{28,24},{1,5},{5... | collective-permute-start | bytes 2359304 | tf_op jit(solution)/shard_map/ppermute | solution.py:199
  402.5 23.5 %collective-permute-start.31 = (bf16[896,512]{1,0:T(8,128)(2,1)S(1)}, bf16[896,512]{1,0:T(8,128)(2,1)S(1)}, u32[]{:S(2)}, u32[]{:S(2)}) collective-permute-start(bf16[896,512]{1,0:T(8,128)(2,1)S(1)} %copy-done.11), channel_id=1, source_target_pairs={{0,8},{4,12},{8,0},{12,4},{16,24},{20,28},{24,16},{28,20},{1,9},{5... | collective-permute-start | bytes 2752520 | tf_op jit(solution)/shard_map/ppermute | solution.py:199
  419.7 26.2 %collective-permute-start.33 = (bf16[896,512]{1,0:T(8,128)(2,1)S(1)}, bf16[896,512]{1,0:T(8,128)(2,1)S(1)}, u32[]{:S(2)}, u32[]{:S(2)}) collective-permute-start(bf16[896,512]{1,0:T(8,128)(2,1)S(1)} %copy-done.9), channel_id=1, source_target_pairs={{0,24},{4,28},{8,16},{12,20},{16,8},{20,12},{24,0},{28,4},{1,25},{... | collective-permute-start | bytes 2752520 | tf_op jit(solution)/shard_map/ppermute | solution.py:199
  423.1 51.2 %collective-permute-start.38 = (bf16[256,3072]{1,0:T(8,128)(2,1)}, bf16[256,3072]{1,0:T(8,128)(2,1)}, u32[]{:S(2)}, u32[]{:S(2)}) collective-permute-start(bf16[256,3072]{1,0:T(8,128)(2,1)} %constant_dynamic-update-slice_fusion.16.refs_0_), channel_id=1, source_target_pairs={{0,1},{1,0},{2,3},{3,2},{4,5},{5,4},{6,7},{7,6},{8,9},{9,8},{10,11... | collective-permute-start | bytes 4718600 | tf_op jit(solution)/shard_map/ppermute | solution.py:199
  531.8 19.6 %collective-permute-start.43 = (bf16[128,3072]{1,0:T(8,128)(2,1)S(1)}, bf16[128,3072]{1,0:T(8,128)(2,1)S(1)}, u32[]{:S(2)}, u32[]{:S(2)}) collective-permute-start(bf16[128,3072]{1,0:T(8,128)(2,1)S(1)} %get-tuple-element.226), channel_id=1, source_target_pairs={{0,2},{1,3},{2,0},{3,1},{4,6},{5,7},{6,4},{7,5},{8,10},{9,11},{10,... | collective-permute-start | bytes 2359304 | tf_op jit(solution)/shard_map/ppermute | solution.py:199
  532.4 21.0 %collective-permute-start.41 = (bf16[128,3072]{1,0:T(8,128)(2,1)S(1)}, bf16[128,3072]{1,0:T(8,128)(2,1)S(1)}, u32[]{:S(2)}, u32[]{:S(2)}) collective-permute-start(bf16[128,3072]{1,0:T(8,128)(2,1)S(1)} %get-tuple-element.225), channel_id=1, source_target_pairs={{0,4},{4,0},{8,12},{12,8},{16,20},{20,16},{24,28},{28,24},{1,5},{5... | collective-permute-start | bytes 2359304 | tf_op jit(solution)/shard_map/ppermute | solution.py:199
  551.7 35.8 %collective-permute-start.44 = (bf16[256,3072]{1,0:T(8,128)(2,1)S(1)}, bf16[256,3072]{1,0:T(8,128)(2,1)}, u32[]{:S(2)}, u32[]{:S(2)}) collective-permute-start(bf16[256,3072]{1,0:T(8,128)(2,1)S(1)} %pad_maximum_fusion.5), channel_id=1, source_target_pairs={{0,4},{4,0},{8,12},{12,8},{16,20},{20,16},{24,28},{28,24},{1,5},{5... | collective-permute-start | bytes 4718600 | tf_op jit(solution)/shard_map/ppermute | solution.py:199
  554.8 35.5 %collective-permute-start.42 = (bf16[256,3072]{1,0:T(8,128)(2,1)}, bf16[256,3072]{1,0:T(8,128)(2,1)S(1)}, u32[]{:S(2)}, u32[]{:S(2)}) collective-permute-start(bf16[256,3072]{1,0:T(8,128)(2,1)} %pad_maximum_fusion.4), channel_id=1, source_target_pairs={{0,2},{1,3},{2,0},{3,1},{4,6},{5,7},{6,4},{7,5},{8,10},{9,11},{10,... | collective-permute-start | bytes 4718600 | tf_op jit(solution)/shard_map/ppermute | solution.py:199
  593.8 55.5 %collective-permute-start.45 = (bf16[128,3072]{1,0:T(8,128)(2,1)S(1)}, bf16[128,3072]{1,0:T(8,128)(2,1)S(1)}, u32[]{:S(2)}, u32[]{:S(2)}) collective-permute-start(bf16[128,3072]{1,0:T(8,128)(2,1)S(1)} %slice.733), channel_id=1, source_target_pairs={{0,8},{4,12},{8,0},{12,4},{16,24},{20,28},{24,16},{28,20},{1,9},{5... | collective-permute-start | bytes 2359304 | tf_op jit(solution)/shard_map/ppermute | solution.py:199
  616.6 79.4 %collective-permute-start.73 = (bf16[896,512]{1,0:T(8,128)(2,1)S(1)}, bf16[896,512]{1,0:T(8,128)(2,1)S(1)}, u32[]{:S(2)}, u32[]{:S(2)}) collective-permute-start(bf16[896,512]{1,0:T(8,128)(2,1)S(1)} %get-tuple-element.183), channel_id=1, source_target_pairs={{0,8},{4,12},{8,0},{12,4},{16,24},{20,28},{24,16},{28,20},{1,9},{5... | collective-permute-start | bytes 2752520 | tf_op jit(solution)/shard_map/ppermute | solution.py:199
  617.4 79.4 %collective-permute-start.75 = (bf16[896,512]{1,0:T(8,128)(2,1)S(1)}, bf16[896,512]{1,0:T(8,128)(2,1)S(1)}, u32[]{:S(2)}, u32[]{:S(2)}) collective-permute-start(bf16[896,512]{1,0:T(8,128)(2,1)S(1)} %get-tuple-element.186), channel_id=1, source_target_pairs={{0,16},{4,20},{8,24},{12,28},{16,0},{20,4},{24,8},{28,12},{1,17},{... | collective-permute-start | bytes 2752520 | tf_op jit(solution)/shard_map/ppermute | solution.py:199
  649.6 32.1 %collective-permute-start.46 = (bf16[64,3072]{1,0:T(8,128)(2,1)S(1)}, bf16[64,3072]{1,0:T(8,128)(2,1)S(1)}, u32[]{:S(2)}, u32[]{:S(2)}) collective-permute-start(bf16[64,3072]{1,0:T(8,128)(2,1)S(1)} %slice.734), channel_id=1, source_target_pairs={{0,16},{4,20},{8,24},{12,28},{16,0},{20,4},{24,8},{28,12},{1,17},{... | collective-permute-start | bytes 1179656 | tf_op jit(solution)/shard_map/ppermute | solution.py:199
  687.0 22.4 %collective-permute-start.77 = (bf16[896,512]{1,0:T(8,128)(2,1)S(1)}, bf16[896,512]{1,0:T(8,128)(2,1)S(1)}, u32[]{:S(2)}, u32[]{:S(2)}) collective-permute-start(bf16[896,512]{1,0:T(8,128)(2,1)S(1)} %get-tuple-element.190), channel_id=1, source_target_pairs={{0,24},{4,28},{8,16},{12,20},{16,8},{20,12},{24,0},{28,4},{1,25},{... | collective-permute-start | bytes 2752520 | tf_op jit(solution)/shard_map/ppermute | solution.py:199
  695.7 35.4 %collective-permute-start.49 = (bf16[128,3072]{1,0:T(8,128)(2,1)}, bf16[128,3072]{1,0:T(8,128)(2,1)}, u32[]{:S(2)}, u32[]{:S(2)}) collective-permute-start(bf16[128,3072]{1,0:T(8,128)(2,1)} %pad_maximum_fusion.14), channel_id=1, source_target_pairs={{0,1},{1,0},{2,3},{3,2},{4,5},{5,4},{6,7},{7,6},{8,9},{9,8},{10,11... | collective-permute-start | bytes 2359304 | tf_op jit(solution)/shard_map/ppermute | solution.py:199
  710.5 233.9 %collective-permute-start.47 = (bf16[768,3072]{1,0:T(8,128)(2,1)}, bf16[768,3072]{1,0:T(8,128)(2,1)}, u32[]{:S(2)}, u32[]{:S(2)}) collective-permute-start(bf16[768,3072]{1,0:T(8,128)(2,1)} %get-tuple-element.162), channel_id=1, source_target_pairs={{0,1},{1,0},{2,3},{3,2},{4,5},{5,4},{6,7},{7,6},{8,9},{9,8},{10,11... | collective-permute-start | bytes 14155784 | tf_op jit(solution)/shard_map/ppermute | solution.py:199
  710.5 80.4 %collective-permute-start.51 = (bf16[256,3072]{1,0:T(8,128)(2,1)}, bf16[256,3072]{1,0:T(8,128)(2,1)}, u32[]{:S(2)}, u32[]{:S(2)}) collective-permute-start(bf16[256,3072]{1,0:T(8,128)(2,1)} %slice.596), channel_id=1, source_target_pairs={{0,1},{1,0},{2,3},{3,2},{4,5},{5,4},{6,7},{7,6},{8,9},{9,8},{10,11... | collective-permute-start | bytes 4718600 | tf_op jit(solution)/shard_map/ppermute | solution.py:199
  712.3 72.5 %collective-permute-start.72 = (bf16[896,512]{1,0:T(8,128)(2,1)}, bf16[896,512]{1,0:T(8,128)(2,1)}, u32[]{:S(2)}, u32[]{:S(2)}) collective-permute-start(bf16[896,512]{1,0:T(8,128)(2,1)} %copy-done.18), channel_id=1, source_target_pairs={{0,4},{4,0},{8,12},{12,8},{16,20},{20,16},{24,28},{28,24},{1,5},{5... | collective-permute-start | bytes 2752520 | tf_op jit(solution)/shard_map/ppermute | solution.py:199
  712.9 74.7 %collective-permute-start.76 = (bf16[896,512]{1,0:T(8,128)(2,1)S(1)}, bf16[896,512]{1,0:T(8,128)(2,1)}, u32[]{:S(2)}, u32[]{:S(2)}) collective-permute-start(bf16[896,512]{1,0:T(8,128)(2,1)S(1)} %get-tuple-element.188), channel_id=1, source_target_pairs={{0,20},{4,16},{8,28},{12,24},{16,4},{20,0},{24,12},{28,8},{1,21},{... | collective-permute-start | bytes 2752520 | tf_op jit(solution)/shard_map/ppermute | solution.py:199
  765.0 39.9 %collective-permute-start.54 = (bf16[2,2,384,512]{2,3,0,1:T(8,128)(2,1)}, bf16[2,2,384,512]{2,3,0,1:T(8,128)(2,1)}, u32[]{:S(2)}, u32[]{:S(2)}) collective-permute-start(bf16[2,2,384,512]{2,3,0,1:T(8,128)(2,1)} %fusion.17), channel_id=1, source_target_pairs={{0,4},{4,0},{8,12},{12,8},{16,20},{20,16},{24,28},{28,24},{1,5},{5... | collective-permute-start | bytes 4718600 | tf_op jit(solution)/shard_map/ppermute | solution.py:199
  787.6 20.7 %collective-permute-start.66 = (bf16[2,2,2,2,112,512]{5,4,0,1,2,3:T(8,128)(2,1)S(1)}, bf16[2,2,2,2,112,512]{5,4,0,1,2,3:T(8,128)(2,1)S(1)}, u32[]{:S(2)}, u32[]{:S(2)}) collective-permute-start(bf16[2,2,2,2,112,512]{5,4,0,1,2,3:T(8,128)(2,1)S(1)} %bitcast.363), channel_id=1, source_target_pairs={{0,1},{1,0},{2,3},{3,2},{4,5},{5,4},{6,7},{7,6},{8,9},{9,8},{10,11... | collective-permute-start | bytes 5505032 | tf_op jit(solution)/shard_map/ppermute | solution.py:199
  794.0 150.4 %collective-permute-start.52 = (bf16[256,3072]{1,0:T(8,128)(2,1)S(1)}, bf16[256,3072]{1,0:T(8,128)(2,1)S(1)}, u32[]{:S(2)}, u32[]{:S(2)}) collective-permute-start(bf16[256,3072]{1,0:T(8,128)(2,1)S(1)} %add_convert_fusion.2), channel_id=1, source_target_pairs={{0,2},{1,3},{2,0},{3,1},{4,6},{5,7},{6,4},{7,5},{8,10},{9,11},{10,... | collective-permute-start | bytes 4718600 | tf_op jit(solution)/shard_map/ppermute | solution.py:199
  804.8 19.5 %collective-permute-start.60 = (bf16[2,2,384,256]{3,2,0,1:T(8,128)(2,1)S(1)}, bf16[2,2,384,256]{3,2,0,1:T(8,128)(2,1)S(1)}, u32[]{:S(2)}, u32[]{:S(2)}) collective-permute-start(bf16[2,2,384,256]{3,2,0,1:T(8,128)(2,1)S(1)} %bitcast.383), channel_id=1, source_target_pairs={{0,4},{4,0},{8,12},{12,8},{16,20},{20,16},{24,28},{28,24},{1,5},{5... | collective-permute-start | bytes 2359304 | tf_op jit(solution)/shard_map/ppermute | solution.py:199
  808.0 40.2 %collective-permute-start.56 = (bf16[2,384,512]{1,2,0:T(8,128)(2,1)S(1)}, bf16[2,384,512]{1,2,0:T(8,128)(2,1)S(1)}, u32[]{:S(2)}, u32[]{:S(2)}) collective-permute-start(bf16[2,384,512]{1,2,0:T(8,128)(2,1)S(1)} %dynamic-slice_bitcast_fusion.1), channel_id=1, source_target_pairs={{0,8},{4,12},{8,0},{12,4},{16,24},{20,28},{24,16},{28,20},{1,9},{5... | collective-permute-start | bytes 2359304 | tf_op jit(solution)/shard_map/ppermute | solution.py:199
  808.3 37.1 %collective-permute-start.63 = (bf16[2,2,384,256]{3,2,1,0:T(8,128)(2,1)S(1)}, bf16[2,2,384,256]{3,2,1,0:T(8,128)(2,1)S(1)}, u32[]{:S(2)}, u32[]{:S(2)}) collective-permute-start(bf16[2,2,384,256]{3,2,1,0:T(8,128)(2,1)S(1)} %fusion.49), channel_id=1, source_target_pairs={{0,8},{4,12},{8,0},{12,4},{16,24},{20,28},{24,16},{28,20},{1,9},{5... | collective-permute-start | bytes 2359304 | tf_op jit(solution)/shard_map/ppermute | solution.py:199
  824.3 52.8 %collective-permute-start.74 = (bf16[896,512]{1,0:T(8,128)(2,1)S(1)}, bf16[896,512]{1,0:T(8,128)(2,1)S(1)}, u32[]{:S(2)}, u32[]{:S(2)}) collective-permute-start(bf16[896,512]{1,0:T(8,128)(2,1)S(1)} %get-tuple-element.185), channel_id=1, source_target_pairs={{0,12},{4,8},{8,4},{12,0},{16,28},{20,24},{24,20},{28,16},{1,13},{... | collective-permute-start | bytes 2752520 | tf_op jit(solution)/shard_map/ppermute | solution.py:199
  845.4 54.3 %collective-permute-start.78 = (bf16[896,512]{1,0:T(8,128)(2,1)S(1)}, bf16[896,512]{1,0:T(8,128)(2,1)S(1)}, u32[]{:S(2)}, u32[]{:S(2)}) collective-permute-start(bf16[896,512]{1,0:T(8,128)(2,1)S(1)} %get-tuple-element.192), channel_id=1, source_target_pairs={{0,28},{4,24},{8,20},{12,16},{16,12},{20,8},{24,4},{28,0},{1,29},{... | collective-permute-start | bytes 2752520 | tf_op jit(solution)/shard_map/ppermute | solution.py:199
  848.2 57.8 %collective-permute-start.67 = (bf16[2,2,2,112,512]{4,3,0,1,2:T(8,128)(2,1)S(1)}, bf16[2,2,2,112,512]{4,3,0,1,2:T(8,128)(2,1)S(1)}, u32[]{:S(2)}, u32[]{:S(2)}) collective-permute-start(bf16[2,2,2,112,512]{4,3,0,1,2:T(8,128)(2,1)S(1)} %dynamic-slice_bitcast_fusion), channel_id=1, source_target_pairs={{0,2},{1,3},{2,0},{3,1},{4,6},{5,7},{6,4},{7,5},{8,10},{9,11},{10,... | collective-permute-start | bytes 2752520 | tf_op jit(solution)/shard_map/ppermute | solution.py:199
  877.1 38.8 %collective-permute-start.61 = (bf16[2,384,256]{2,1,0:T(8,128)(2,1)S(1)}, bf16[2,384,256]{2,1,0:T(8,128)(2,1)S(1)}, u32[]{:S(2)}, u32[]{:S(2)}) collective-permute-start(bf16[2,384,256]{2,1,0:T(8,128)(2,1)S(1)} %dynamic-slice_bitcast_fusion.5), channel_id=1, source_target_pairs={{0,8},{4,12},{8,0},{12,4},{16,24},{20,28},{24,16},{28,20},{1,9},{5... | collective-permute-start | bytes 1179656 | tf_op jit(solution)/shard_map/ppermute | solution.py:199
  899.7 31.2 %collective-permute-start.64 = (bf16[2,384,256]{2,1,0:T(8,128)(2,1)S(1)}, bf16[2,384,256]{2,1,0:T(8,128)(2,1)S(1)}, u32[]{:S(2)}, u32[]{:S(2)}) collective-permute-start(bf16[2,384,256]{2,1,0:T(8,128)(2,1)S(1)} %dynamic-slice_bitcast_fusion.4), channel_id=1, source_target_pairs={{0,16},{4,20},{8,24},{12,28},{16,0},{20,4},{24,8},{28,12},{1,17},{... | collective-permute-start | bytes 1179656 | tf_op jit(solution)/shard_map/ppermute | solution.py:199
  906.0 35.4 %collective-permute-start.71 = (bf16[384,512]{0,1:T(8,128)(2,1)S(1)}, bf16[384,512]{0,1:T(8,128)(2,1)S(1)}, u32[]{:S(2)}, u32[]{:S(2)}) collective-permute-start(bf16[384,512]{0,1:T(8,128)(2,1)S(1)} %dynamic-slice_bitcast_fusion.3), channel_id=1, source_target_pairs={{0,16},{4,20},{8,24},{12,28},{16,0},{20,4},{24,8},{28,12},{1,17},{... | collective-permute-start | bytes 1179656 | tf_op jit(solution)/shard_map/ppermute | solution.py:199
  915.9 33.7 %collective-permute-start.68 = (bf16[2,2,112,512]{3,2,0,1:T(8,128)(2,1)S(1)}, bf16[2,2,112,512]{3,2,0,1:T(8,128)(2,1)S(1)}, u32[]{:S(2)}, u32[]{:S(2)}) collective-permute-start(bf16[2,2,112,512]{3,2,0,1:T(8,128)(2,1)S(1)} %dynamic-slice_bitcast_fusion.2), channel_id=1, source_target_pairs={{0,4},{4,0},{8,12},{12,8},{16,20},{20,16},{24,28},{28,24},{1,5},{5... | collective-permute-start | bytes 1376264 | tf_op jit(solution)/shard_map/ppermute | solution.py:199
  947.4 34.2 %collective-permute-start.53 = (bf16[256,3072]{1,0:T(8,128)(2,1)S(1)}, bf16[256,3072]{1,0:T(8,128)(2,1)S(1)}, u32[]{:S(2)}, u32[]{:S(2)}) collective-permute-start(bf16[256,3072]{1,0:T(8,128)(2,1)S(1)} %get-tuple-element.167), channel_id=1, source_target_pairs={{0,4},{4,0},{8,12},{12,8},{16,20},{20,16},{24,28},{28,24},{1,5},{5... | collective-permute-start | bytes 4718600 | tf_op jit(solution)/shard_map/ppermute | solution.py:199
  947.5 34.1 %collective-permute-start.50 = (bf16[256,3072]{1,0:T(8,128)(2,1)S(1)}, bf16[256,3072]{1,0:T(8,128)(2,1)S(1)}, u32[]{:S(2)}, u32[]{:S(2)}) collective-permute-start(bf16[256,3072]{1,0:T(8,128)(2,1)S(1)} %get-tuple-element.163), channel_id=1, source_target_pairs={{0,2},{1,3},{2,0},{3,1},{4,6},{5,7},{6,4},{7,5},{8,10},{9,11},{10,... | collective-permute-start | bytes 4718600 | tf_op jit(solution)/shard_map/ppermute | solution.py:199
  957.2 27.6 %collective-permute-start.70 = (bf16[112,512]{1,0:T(8,128)(2,1)S(1)}, bf16[112,512]{1,0:T(8,128)(2,1)S(1)}, u32[]{:S(2)}, u32[]{:S(2)}) collective-permute-start(bf16[112,512]{1,0:T(8,128)(2,1)S(1)} %dynamic-slice_bitcast_fusion.9), channel_id=1, source_target_pairs={{0,16},{4,20},{8,24},{12,28},{16,0},{20,4},{24,8},{28,12},{1,17},{... | collective-permute-start | bytes 344072 | tf_op jit(solution)/shard_map/ppermute | solution.py:199
  (199 other events, 2599.1 us)

commit v2 on v1

--- a/solution.py
+++ b/solution.py
@@ -215,7 +215,7 @@
             held.append(rank_of(link))
         return block.reshape(-1, *block.shape[len(links) :])
 
-    def scatter_blocks(blocks, links, at, events=None, earlier=()):
+    def scatter_blocks(blocks, links, at):
         held = sorted((rank_of(link) for link in links), reverse=True)
         blocks = blocks.reshape(*(2 for unused in links), *blocks.shape[1:])
         for stage, link in enumerate(links):
@@ -223,74 +223,70 @@
             bit = jnp.minimum(at[link[0]] & link[1], 1)
             mine = lax.dynamic_index_in_dim(blocks, bit, position, keepdims=False)
             theirs = lax.dynamic_index_in_dim(blocks, 1 - bit, position, keepdims=False)
-            moved = hop(theirs, link, *at_stage(earlier, stage))
-            if events is not None:
-                events.append(moved)
-            blocks = mine.astype(wider) + moved.astype(wider)
+            blocks = mine.astype(wider) + hop(theirs, link).astype(wider)
             if stage + 1 < len(links):
                 blocks = blocks.astype(low)
             held.remove(rank_of(link))
         return blocks
 
-    def at_stage(earlier, stage):
-        return earlier[stage] if stage < len(earlier) else ()
-
-    def gather_rows(rows, links, events, earlier=()):
-        for stage, link in enumerate(links):
-            moved = hop(rows, link, *at_stage(earlier, stage))
-            events.append(moved)
+    def gather_rows(rows, links, events=None, *earlier):
+        for link in links:
+            moved = hop(rows, link, *earlier)
+            earlier = ()
+            if events is not None:
+                events.append(moved)
             rows = jnp.concatenate([rows, moved], axis=0)
         return rows
 
-    def scatter_rows(rows, links, events, earlier=()):
+    def scatter_rows(rows, links, events=None):
         for stage, link in enumerate(links):
             half = rows.shape[0] // 2
-            moved = hop(rows[half:], link, *at_stage(earlier, stage))
-            events.append(moved)
+            moved = hop(rows[half:], link)
+            if events is not None:
+                events.append(moved)
             rows = rows[:half].astype(wider) + moved.astype(wider)
             if stage + 1 < len(links):
                 rows = rows.astype(low)
         return rows
 
-    def gather_all(rows, events, even, earlier=()):
-        own = gather_rows(rows, far, events, earlier)
-        sides, last = at_stage(earlier, len(far)), at_stage(earlier, len(far) + 1)
-        from_x, from_y = hop(own, across, *sides), hop(own, side, *sides)
-        events.append(from_y)
+    def gather_all(rows, events, even, *earlier):
+        own = gather_rows(rows, far, events, *earlier)
+        from_x, from_y = hop(own, across), hop(own, side)
         half = own.shape[0] // 2
         if even:
             corner = jnp.concatenate(
-                [hop(from_y[:half], across, *last), hop(from_x[half:], side, *last)], axis=0
+                [hop(from_y[:half], across), hop(from_x[half:], side)], axis=0
             )
         else:
-            corner = hop(from_y, across, *last)
+            corner = hop(from_y, across)
         return own, from_x, from_y, corner
 
-    def scatter_all(most, other_most, corner, other_corner, events, even, earlier=()):
-        chip, first, second = (at_stage(earlier, stage) for stage in range(3))
-        corner = corner.astype(wider) + hop(other_corner, core, *chip).astype(wider)
+    def scatter_all(most, other_most, corner, other_corner, events, even, *earlier):
+        corner = corner.astype(wider) + hop(other_corner, core, *earlier).astype(wider)
         corner = corner.astype(low)
         size = corner.shape[0]
         half = size // 2 if even else size
-        for_y = hop(corner[:half], across, *first)
+        for_y = hop(corner[:half], across)
         events.append(for_y)
-        sums = []
-        for i in range(3):
-            rows = slice(i * size, (i + 1) * size)
-            moved = other_most[i] if isinstance(other_most, list) else other_most[rows]
-            sums.append((most[rows], moved))
-        own, sum_x, sum_y = (mine.astype(wider) + moved.astype(wider) for mine, moved in sums)
+        if n_all * 64 <= 4096:
+            most = most.astype(wider) + hop(other_most, core, *earlier).astype(wider)
+            own, sum_x, sum_y = (most[i * size : (i + 1) * size] for i in range(3))
+        else:
+            parts = [slice(i * size, (i + 1) * size) for i in range(3)]
+            own, sum_x, sum_y = (
+                most[rows].astype(wider) + hop(other_most[rows], core, *earlier).astype(wider)
+                for rows in parts
+            )
         if even:
-            for_x = hop(corner[half:], side, *first)
+            for_x = hop(corner[half:], side)
             sum_x = jnp.concatenate([sum_x[:half], sum_x[half:] + for_x.astype(wider)], axis=0)
             sum_y = jnp.concatenate([sum_y[:half] + for_y.astype(wider), sum_y[half:]], axis=0)
         else:
             sum_y = sum_y + for_y.astype(wider)
-        moved_x = hop(sum_x.astype(low), across, *second)
-        moved_y = hop(sum_y.astype(low), side, *second)
+        moved_x, moved_y = hop(sum_x.astype(low), across), hop(sum_y.astype(low), side)
         events.append(moved_y)
         total = own + moved_x.astype(wider) + moved_y.astype(wider)
-        return scatter_rows(total.astype(low), far[::-1], events, earlier[3:])
+        return scatter_rows(total.astype(low), far[::-1], events)
 
     def local(
         x_prefix,
@@ -370,8 +366,6 @@
         packet_shape = (3 * depth[0] + depth[1], units[0])
         peers = at["wide"] ^ jnp.arange(n_wide, dtype=jnp.int32)
 
-        copying = n_all * own <= 4096
-
         def packet_plan(outward, blocks_of):
             plan = []
             for k in range(n_wide):
@@ -435,16 +429,9 @@
         else:
             packets = {0: weight_packet(0)}
 
-        def send_packets(few, packet_of, *earlier):
-            for k in few:
-                packets[k] = hop(packet_of(k), ("wide", k), *earlier)
-
-        def share(first, last):
-            return [k for k in distances if first * n_wide <= 8 * k < last * n_wide]
-
         narrow_links = [across, core]
         x_packed = jnp.concatenate([x_prefix, x_action], axis=1)
-        item_packed = gather_rows(x_packed, narrow_links, [])
+        item_packed = gather_rows(x_packed, narrow_links)
         item_rows = streams(item_packed)
 
         gain_parts = [norm1_prefix, norm2_prefix, norm1_action, norm2_action]
@@ -461,6 +448,30 @@
             )
 
         shared_events, query_events, out_events = [], [], []
+        shared = gather_blocks(
+            jnp.concatenate(
+                [
+                    jnp.concatenate([wk_prefix, wv_prefix], axis=1),
+                    jnp.concatenate([wk_action, wv_action], axis=1),
+                    pad_gains(jnp.concatenate(gain_parts)),
+                ],
+                axis=0,
+            ),
+            far + [side, across, core],
+            at,
+            shared_events,
+        )
+        gains_all = shared[:, gain_start, :].astype(wider)
+        gains = [
+            gains_all[:, stop - size : stop].reshape(-1)
+            for stop, size in zip(gain_stops, gain_sizes, strict=True)
+        ]
+        first_gain = [gains[0], gains[2]]
+        second_gain = [gains[1], gains[3]]
+        keyval_weight = [
+            shared[:, : keyval_rows_of[0]].reshape(-1, 2 * head_dim),
+            shared[:, keyval_rows_of[0] : gain_start].reshape(-1, 2 * head_dim),
+        ]
         query_depth = [wq_prefix.shape[0], wq_action.shape[0]]
         query_half = wq_prefix.shape[1] // 2
         query_packed = jnp.concatenate([wq_prefix, wq_action], axis=0)
@@ -476,49 +487,43 @@
                 (packets[max(packets)],),
             ),
         ]
-        send_packets(share(4, 5), weight_packet, query_events[0])
-        shared = gather_blocks(
-            jnp.concatenate(
-                [
-                    jnp.concatenate([wk_prefix, wv_prefix], axis=1),
-                    jnp.concatenate([wk_action, wv_action], axis=1),
-                    pad_gains(jnp.concatenate(gain_parts)),
-                ],
-                axis=0,
-            ),
-            far + [side, across, core],
-            at,
-            shared_events,
-            *[()] * (len(far) + 2),
-            tuple(packets[k] for k in share(4, 5)),
-        )
-        send_packets(share(5, 6), weight_packet, shared_events[-2])
-        send_packets(share(0, 2), weight_packet, shared_events[-2])
-        gains_all = shared[:, gain_start, :].astype(wider)
-        gains = [
-            gains_all[:, stop - size : stop].reshape(-1)
-            for stop, size in zip(gain_stops, gain_sizes, strict=True)
-        ]
-        first_gain = [gains[0], gains[2]]
-        second_gain = [gains[1], gains[3]]
-        keyval_weight = [
-            shared[:, : keyval_rows_of[0]].reshape(-1, 2 * head_dim),
-            shared[:, keyval_rows_of[0] : gain_start].reshape(-1, 2 * head_dim),
-        ]
         query_weight = [
             [blocks[:, : query_depth[0]].reshape(-1, query_half) for blocks in query_blocks],
             [blocks[:, query_depth[0] :].reshape(-1, query_half) for blocks in query_blocks],
         ]
-        out_held = gather_blocks(
+        out_blocks = gather_blocks(
             jnp.concatenate([wo_prefix.T, wo_action.T], axis=0),
-            far,
+            wide_links,
             at,
             out_events,
             (query_events[1],),
         )
-        out_moved = hop(out_held.reshape(*(2 for unused in far), *out_held.shape[1:]), side)
+        out_weight = [
+            out_blocks[:, : query_depth[0]].reshape(-1, wo_prefix.shape[0]),
+            out_blocks[:, query_depth[0] :].reshape(-1, wo_action.shape[0]),
+        ]
         item_weight = mix_weight[0]
         dout = jnp.concatenate([cot_prefix, cot_action], axis=1).astype(wider) * item_weight
+        grad_events = []
+        grad_near = gather_all(dout.astype(low), grad_events, False, shared_events[-3])
+        copying = n_all * own <= 4096
+        if copying:
+            grad_near = jnp.concatenate(grad_near, axis=0)
+            grad_far = hop(grad_near, core)
+            grad_near, grad_far = ([(rows, i) for i in range(4)] for rows in (grad_near, grad_far))
+        else:
+            grad_far = [(hop(rows, core), 0) for rows in grad_near]
+            grad_near = [(rows, 0) for rows in grad_near]
+        def send_packets(few, packet_of, *earlier):
+            for k in few:
+                packets[k] = hop(packet_of(k), ("wide", k), *earlier)
+
+        def share(first, last):
+            return [k for k in distances if first * n_wide <= 8 * k < last * n_wide]
+
+        send_packets(share(4, 5), weight_packet, query_events[0])
+        send_packets(share(5, 6), weight_packet, shared_events[-2])
+        send_packets(share(0, 2), weight_packet, shared_events[-2])
 
         all_normed = [
             rms_norm(item_rows[stream].astype(wider), first_gain[stream]).astype(low)
@@ -576,19 +581,6 @@
         mixed_all = jnp.einsum("hqk,kd->qhd", attention, values, preferred_element_type=wider)
         mixed_all = mixed_all.astype(low).reshape(total_rows, -1)
         mixed_rows = [mixed_all[:prefix_len], mixed_all[prefix_len:]]
-        out_moved, mixed_all = join(out_moved, mixed_all)
-        mixed_rows = [mixed_all[:prefix_len], mixed_all[prefix_len:]]
-        out_held = out_held.reshape(out_moved.shape)
-        out_blocks = jnp.where(
-            (at["wide"] & 1) != 0,
-            jnp.stack([out_moved, out_held], len(far)),
-            jnp.stack([out_held, out_moved], len(far)),
-        )
-        out_blocks = out_blocks.reshape(-1, *out_blocks.shape[len(far) + 1 :])
-        out_weight = [
-            out_blocks[:, : query_depth[0]].reshape(-1, wo_prefix.shape[0]),
-            out_blocks[:, query_depth[0] :].reshape(-1, wo_action.shape[0]),
-        ]
         attended_all = (
             jnp.concatenate(
                 [
@@ -599,12 +591,8 @@
             )
         )
         attended_events = []
-        attended = scatter_rows(
-            attended_all,
-            [core, across],
-            attended_events,
-            [(), tuple(packets[k] for k in share(5, 6))],
-        )
+        attended_all = tie(attended_all, packets[n_wide // 2], *grad_events)
+        attended = scatter_rows(attended_all, [core, across], attended_events)
         send_packets(share(7, 8), weight_packet, attended_events[1])
         send_packets(share(3, 4), weight_packet, attended_events[1])
         inputs = [x_prefix.astype(wider), x_action.astype(wider)]
@@ -616,27 +604,15 @@
             axis=1,
         )
         token_events = []
-        near = gather_all(
-            normed2,
-            token_events,
-            True,
-            [tuple(packets[k] for k in share(0, 2))]
-            + [()] * (len(far) - 1)
-            + [
-                tuple(packets[k] for k in share(7, 8)),
-                tuple(packets[k] for k in share(3, 4)),
-            ],
-        )
-        send_packets(share(6, 7), weight_packet, token_events[-2])
-        send_packets(share(2, 3), weight_packet, token_events[-2])
-        grad_near = gather_all(
-            dout.astype(low),
-            [],
-            False,
-            [(shared_events[-3],)]
-            + [(shared_events[-1],)] * (len(far) - 1)
-            + [(attended_events[0],), (token_events[-2],)],
-        )
+        normed2 = tie(normed2, *(packets[k] for k in share(5, 6) + share(0, 2)))
+        near = gather_all(normed2, token_events, True)
+        if copying:
+            other_most = hop(jnp.concatenate(near[:3], axis=0), core)
+            token_far = [(other_most, i) for i in range(3)] + [(hop(near[3], core), 0)]
+        else:
+            token_far = [(hop(rows, core), 0) for rows in near]
+        send_packets(share(6, 7), weight_packet, token_events[-1])
+        send_packets(share(2, 3), weight_packet, token_events[-1])
         if aligned:
             feed_weights = copy_blocks(
                 packet_plan(
@@ -685,16 +661,6 @@
             total=n_all * own,
             n_copied=4 if copying else 0,
         )
-        if copying:
-            other_most = hop(jnp.concatenate(near[:3], axis=0), core)
-            token_far = [(other_most, i) for i in range(3)] + [(hop(near[3], core), 0)]
-            grad_near = jnp.concatenate(grad_near, axis=0)
-            grad_far = hop(grad_near, core)
-            grad_near, grad_far = ([(rows, i) for i in range(4)] for rows in (grad_near, grad_far))
-        else:
-            token_far = [(hop(rows, core), 0) for rows in near]
-            grad_far = [(hop(rows, core), 0) for rows in grad_near]
-            grad_near = [(rows, 0) for rows in grad_near]
         token_pieces = [(rows, 0) for rows in near] + [token_far[3], *token_far[:3]]
         grad_pieces = [*grad_near, grad_far[3], *grad_far[:3]]
         kept, back_most, out_most = feed(token_pieces[:3], grad_pieces[:3], kept=[], first=0)
@@ -703,25 +669,7 @@
         )
         kept, back_far, out_far = feed(token_pieces[5:], grad_pieces[5:], kept=kept, first=5)
         hidden_rows, both_rows = kept[-4::2], kept[-3::2]
-        def chip_far(rows, *earlier):
-            if copying:
-                return hop(rows, core, *earlier)
-            return [hop(rows[i * size : (i + 1) * size], core, *earlier) for i in range(3)]
-
-        back_events = []
-        dnormed2_packed = scatter_all(
-            back_most,
-            chip_far(back_far),
-            back_corner[:size],
-            back_corner[size:],
-            back_events,
-            True,
-        )
-        dnormed2 = streams(dnormed2_packed)
-        if copying:
-            gate_up_grad = [rows_contract(kept[i], both_rows[i]) for i in range(2)]
-            down_grad = [rows_contract(hidden_rows[i], kept[2 + i]) for i in range(2)]
-        else:
+        if not copying:
             gate_up_grad = [0.0, 0.0]
             down_grad = [0.0, 0.0]
             for i, ((token, token_at), (grad, grad_at)) in enumerate(
@@ -733,8 +681,27 @@
                 for j in range(2):
                     gate_up_grad[j] = gate_up_grad[j] + rows_contract(token[j], both_rows[j][rows])
                     down_grad[j] = down_grad[j] + rows_contract(hidden_rows[j][rows], grad[j])
-        gate_up_grad = [grad.astype(low) for grad in gate_up_grad]
-        down_grad = [grad.astype(low) for grad in down_grad]
+            gate_up_grad = [grad.astype(low) for grad in gate_up_grad]
+            down_grad = [grad.astype(low) for grad in down_grad]
+            back_corner, back_far, out_corner, out_far, *held = join(
+                back_corner, back_far, out_corner, out_far, *gate_up_grad, *down_grad
+            )
+            gate_up_grad, down_grad = held[:2], held[2:]
+        back_events = []
+        dnormed2_packed = scatter_all(
+            back_most, back_far, back_corner[:size], back_corner[size:], back_events, True
+        )
+        dnormed2 = streams(dnormed2_packed)
+        mlp_out = streams(
+            scatter_all(
+                out_most, out_far, out_corner[:size], out_corner[size:], [], False, back_events[-1]
+            )
+        )
+        if copying:
+            gate_up_grad = [rows_contract(kept[i], both_rows[i]) for i in range(2)]
+            down_grad = [rows_contract(hidden_rows[i], kept[2 + i]) for i in range(2)]
+            gate_up_grad = [grad.astype(low) for grad in gate_up_grad]
+            down_grad = [grad.astype(low) for grad in down_grad]
 
         def gradient_packet(k):
             peer = at["wide"] ^ k
@@ -769,6 +736,9 @@
         send_packets(share(4, 5), gradient_packet)
         send_packets(share(2, 3), gradient_packet)
         send_packets(share(6, 7), gradient_packet, back_events[1])
+        send_packets(share(0, 2), gradient_packet, back_events[-1])
+        send_packets(share(5, 6), gradient_packet, back_events[-1])
+        outputs = [(middle[stream] + mlp_out[stream]).astype(low) for stream in range(2)]
         dmiddle = []
         grad_second = []
         for stream, dout_part in enumerate(streams(dout)):
@@ -778,28 +748,27 @@
         att_events = []
         grad_att = streams(
             gather_rows(
-                jnp.concatenate([part.astype(low) for part in dmiddle], axis=1),
+                tie(
+                    jnp.concatenate([part.astype(low) for part in dmiddle], axis=1),
+                    *(packets[k] for k in share(4, 5) + share(2, 3)),
+                ),
                 narrow_links,
                 att_events,
             )
         )
-        send_packets(share(5, 6), gradient_packet, att_events[0])
-        send_packets(share(0, 2), gradient_packet, att_events[0])
-        return_events = []
-
-        def return_wide(parts, links, events=None, earlier=()):
+        send_packets(share(7, 8), gradient_packet, att_events[0])
+        send_packets(share(3, 4), gradient_packet, att_events[0])
+
+        def return_wide(parts, links):
             blocks = jnp.concatenate(
                 [part.astype(low).reshape(n_wide, -1, part.shape[1]) for part in parts], axis=1
             )
-            return scatter_blocks(blocks, links, at, events, earlier)
+            return scatter_blocks(blocks, links, at)
 
         out_grads = return_wide(
             [rows_contract(grad_att[stream], mixed_rows[stream]) for stream in range(2)],
             wide_links[::-1],
-            return_events,
-        )
-        send_packets(share(7, 8), gradient_packet, return_events[0])
-        send_packets(share(3, 4), gradient_packet, return_events[0])
+        )
         grad_out_w = [out_grads[: query_depth[0]].T, out_grads[query_depth[0] :].T]
         dmixed = jnp.concatenate(
             [product(grad_att[stream], out_weight[stream]) for stream in range(2)],
@@ -831,8 +800,6 @@
                         for stream in range(2)
                     ],
                     query_links[part],
-                    None,
-                    [(return_events[0],)],
                 )
                 for part in range(2)
             ],
@@ -873,7 +840,7 @@
             grad_first.append(jnp.sum(dnormed * unit_rows, axis=0))
             dnormed_parts.append(dnormed.astype(low))
         dnormed = streams(
-            scatter_rows(jnp.concatenate(dnormed_parts, axis=1), [core, across], [])
+            scatter_rows(jnp.concatenate(dnormed_parts, axis=1), [core, across])
         )
         grad_inputs = [
             dmiddle[stream] + norm_back(inputs[stream], first_gain[stream], dnormed[stream])[0]
@@ -909,24 +876,6 @@
             gain_grads[stop - size : stop]
             for stop, size in zip(gain_stops, gain_sizes, strict=True)
         ]
-        mlp_out = streams(
-            scatter_all(
-                out_most,
-                chip_far(out_far, back_events[-1]),
-                out_corner[:size],
-                out_corner[size:],
-                [],
-                False,
-                [
-                    (back_events[-1],),
-                    (att_events[0],),
-                    (att_events[1],),
-                    (return_events[0],),
-                    (return_events[1],),
-                ],
-            )
-        )
-        outputs = [(middle[stream] + mlp_out[stream]).astype(low) for stream in range(2)]
         weights = [
             (
                 grad_query_w[i],

time: 1030 us -> 974 us (0.946)
  waiting for transfers between devices: 588 us -> 500 us
  other arithmetic: 86.6 us -> 115 us
  local copies, waits for them, and re-layouts: 81.4 us -> 108 us
  starting transfers between devices: 126 us -> 112 us
    ppermute x79, waiting for transfers between devices: 588 us -> 500 us  [hop(): lax.ppermute(value, axis, [(i, i ^ mask) for i in range(sizes[axis])])]
    dynamic_update_slice x26, other arithmetic: 5.14 us -> 32.1 us  [local(): lax.dynamic_update_slice_in_dim(wide_mlp[i], parts[i].astype(wider), peer...]
    ppermute x79, starting transfers between devices: 126 us -> 112 us  [hop(): lax.ppermute(value, axis, [(i, i ^ mask) for i in range(sizes[axis])])]
    unnamed x386 -> x350, local copies, waits for them, and re-layouts: 33.5 us -> 46.9 us
    another operation x2, other arithmetic: 0.31 us -> 12.3 us
  transfers between devices with their start and end apart: 79 -> 79, of which waited for: 40 -> 39; matrix products, arithmetic and copies ran while one was open for 19% -> 23% of each run, Pallas kernels for 5% -> 5%
where the time goes in v2:
time: 974 us; the launch traced here: 965 us
  waiting for transfers between devices  500 us (51%)
  other arithmetic  115 us (12%)
  starting transfers between devices  112 us (11%)
  local copies, waits for them, and re-layouts  108 us (11%)
  Pallas kernels  76.3 us (8%)
  matrix products  49 us (5%)
    ppermute x79, waiting for transfers between devices, hop(): lax.ppermute(value, axis, [(i, i ^ mask) for i in range(sizes[axis])])  500 us
    ppermute x79, starting transfers between devices, hop(): lax.ppermute(value, axis, [(i, i ^ mask) for i in range(sizes[axis])])  112 us
    pallas_call x3, Pallas kernels, feed_forward(): pl.pallas_call(functools.partial(feed_kernel, count, half, len(kept), n_c...  67.4 us
    unnamed x350, local copies, waits for them, and re-layouts  46.9 us
    dynamic_update_slice x26, other arithmetic, local(): lax.dynamic_update_slice_in_dim(wide_mlp[i], parts[i].astype(wider), peer...  32.1 us
    dot_general x12, matrix products, rows_contract(): lax.dot_general(former, latter, (((0,), (0,)), ((), ())), preferred_eleme...  30.6 us
  transfers between devices with their start and end apart: 79, of which 39 were waited for; matrix products, arithmetic and copies ran while one was open for 23% of the time, Pallas kernels for 5%

profile of v2, /device:TPU:0, one launch (start us, length us, event | category | flops | bytes accessed | tf_op | source)
XLA Modules:
  0.0 965.0 jit_solution(2153696699743033921)
XLA Ops:
  3.9 3.0 collective-permute-start.10
  10.6 2.6 collective-permute-start.2
  28.8 3.4 pack_weights.1
  38.8 2.7 collective-permute-start.11
  49.5 8.2 collective-permute-done.11
  57.9 8.6 collective-permute-done.8
  68.0 14.3 %collective-permute-done.13 = bf16[384,512]{1,0:T(8,128)(2,1)S(1)} collective-permute-done((bf16[384,512]{1,0:T(8,128)(2,1)S(1)}, bf16[384,512]{1,0:T(8,128)(2,1)S(1)}, u32[]{:S(2)}, u32[]{:S(2)}) %collective-permute-start.13) | collective-permute-done | bytes 393248 | tf_op jit(solution)/shard_map/ppermute | solution.py:199
  82.5 3.8 collective-permute-start.14
  89.7 21.6 %collective-permute-done.14 = bf16[2,384,512]{2,1,0:T(8,128)(2,1)S(1)} collective-permute-done((bf16[2,384,512]{2,1,0:T(8,128)(2,1)S(1)}, bf16[2,384,512]{2,1,0:T(8,128)(2,1)S(1)}, u32[]{:S(2)}, u32[]{:S(2)}) %collective-permute-start.14) | collective-permute-done | bytes 786464 | tf_op jit(solution)/shard_map/ppermute | solution.py:199
  120.1 26.1 %collective-permute-done.15 = bf16[2,2,384,512]{3,2,0,1:T(8,128)(2,1)S(1)} collective-permute-done((bf16[2,2,384,512]{3,2,0,1:T(8,128)(2,1)S(1)}, bf16[2,2,384,512]{3,2,0,1:T(8,128)(2,1)S(1)}, u32[]{:S(2)}, u32[]{:S(2)}) %collective-permute-start.15) | collective-permute-done | bytes 1572896 | tf_op jit(solution)/shard_map/ppermute | solution.py:199
  157.9 2.4 fusion.37
  174.3 2.5 pad_maximum_fusion.3
  179.6 4.8 collective-permute-done.20
  188.6 27.8 %collective-permute-done.21.refs_5_ = bf16[896,512]{1,0:T(8,128)(2,1)S(1)} collective-permute-done((bf16[896,512]{1,0:T(8,128)(2,1)}, bf16[896,512]{1,0:T(8,128)(2,1)S(1)}, u32[]{:S(2)}, u32[]{:S(2)}) %collective-permute-start.21) | collective-permute-done | bytes 917536 | tf_op jit(solution)/shard_map/ppermute | solution.py:199
  219.0 30.3 %collective-permute-done.28 = bf16[256,3072]{1,0:T(8,128)(2,1)} collective-permute-done((bf16[256,3072]{1,0:T(8,128)(2,1)}, bf16[256,3072]{1,0:T(8,128)(2,1)}, u32[]{:S(2)}, u32[]{:S(2)}) %collective-permute-start.28) | collective-permute-done | bytes 1572896 | tf_op jit(solution)/shard_map/ppermute | solution.py:199
  250.7 2.7 constant_dynamic-update-slice_fusion.10
  254.9 2.8 constant_dynamic-update-slice_fusion.9
  259.3 13.0 %collective-permute-done.24 = bf16[128,3072]{1,0:T(8,128)(2,1)S(1)} collective-permute-done((bf16[128,3072]{1,0:T(8,128)(2,1)S(1)}, bf16[128,3072]{1,0:T(8,128)(2,1)S(1)}, u32[]{:S(2)}, u32[]{:S(2)}) %collective-permute-start.24) | collective-permute-done | bytes 786464 | tf_op jit(solution)/shard_map/ppermute | solution.py:199
  274.0 12.8 %collective-permute-done.29 = bf16[256,3072]{1,0:T(8,128)(2,1)S(1)} collective-permute-done((bf16[256,3072]{1,0:T(8,128)(2,1)}, bf16[256,3072]{1,0:T(8,128)(2,1)S(1)}, u32[]{:S(2)}, u32[]{:S(2)}) %collective-permute-start.29) | collective-permute-done | bytes 1572896 | tf_op jit(solution)/shard_map/ppermute | solution.py:199
  288.6 29.8 %collective-permute-done.25.refs_1_ = bf16[256,3072]{1,0:T(8,128)(2,1)S(1)} collective-permute-done((bf16[256,3072]{1,0:T(8,128)(2,1)S(1)}, bf16[256,3072]{1,0:T(8,128)(2,1)S(1)}, u32[]{:S(2)}, u32[]{:S(2)}) %collective-permute-start.25) | collective-permute-done | bytes 1572896 | tf_op jit(solution)/shard_map/ppermute | solution.py:199
  319.8 5.1 collective-permute-done.26.refs_2_
  330.8 19.2 %collective-permute-done.31.refs_3_ = bf16[896,512]{1,0:T(8,128)(2,1)S(1)} collective-permute-done((bf16[896,512]{1,0:T(8,128)(2,1)S(1)}, bf16[896,512]{1,0:T(8,128)(2,1)S(1)}, u32[]{:S(2)}, u32[]{:S(2)}) %collective-permute-start.31) | collective-permute-done | bytes 917536 | tf_op jit(solution)/shard_map/ppermute | solution.py:199
  350.1 2.5 collective-permute-start.33
  352.7 33.7 %collective-permute-done.37 = bf16[128,3072]{1,0:T(8,128)(2,1)S(1)} collective-permute-done((bf16[128,3072]{1,0:T(8,128)(2,1)S(1)}, bf16[128,3072]{1,0:T(8,128)(2,1)S(1)}, u32[]{:S(2)}, u32[]{:S(2)}) %collective-permute-start.37) | collective-permute-done | bytes 786464 | tf_op jit(solution)/shard_map/ppermute | solution.py:199
  390.0 4.9 collective-permute-done.30.refs_2_
  394.9 18.4 %collective-permute-done.32.refs_6_ = bf16[896,512]{1,0:T(8,128)(2,1)S(1)} collective-permute-done((bf16[896,512]{1,0:T(8,128)(2,1)S(1)}, bf16[896,512]{1,0:T(8,128)(2,1)S(1)}, u32[]{:S(2)}, u32[]{:S(2)}) %collective-permute-start.32) | collective-permute-done | bytes 917536 | tf_op jit(solution)/shard_map/ppermute | solution.py:199
  413.2 2.3 unpack_weights.1
  418.9 22.9 %feed_forward.3 = (bf16[2048,2048]{1,0:T(8,128)(2,1)}, bf16[2048,1024]{1,0:T(8,128)(2,1)}, bf16[2048,2048]{1,0:T(8,128)(2,1)}, bf16[2048,1024]{1,0:T(8,128)(2,1)...) custom-call(bf16[256,3072]{1,0:T(8,128)(2,1)} %copy-done.128, ...), custom_call_target="tpu_custom_call" | custom-call | flops 10871635968 | bytes 28311552 | tf_op jit(solution)/shard_map/feed_forward/pallas_call | solution.py:157
  441.8 2.6 copy-done.16
  444.4 18.6 %feed_forward.4 = (bf16[2048,2048]{1,0:T(8,128)(2,1)}, bf16[2048,1024]{1,0:T(8,128)(2,1)}, bf16[2048,2048]{1,0:T(8,128)(2,1)}, bf16[2048,1024]{1,0:T(8,128)(2,1)...) custom-call(bf16[256,3072]{1,0:T(8,128)(2,1)} %constant_dynamic-upda, ...), custom_call_target="tpu_custom_call", output_to_operand_aliasing={{0}: (8, {}), {1}: (9, {}), {2}: (10, {}), {3}: (11, {}), {... | custom-call | flops 7247757312 | bytes 18874368 | tf_op jit(solution)/shard_map/feed_forward/pallas_call | solution.py:157
  463.0 26.0 %feed_forward.5 = (bf16[2048,2048]{1,0:T(8,128)(2,1)}, bf16[2048,1024]{1,0:T(8,128)(2,1)}, bf16[2048,2048]{1,0:T(8,128)(2,1)}, bf16[2048,1024]{1,0:T(8,128)(2,1)...) custom-call(bf16[768,3072]{1,0:T(8,128)(2,1)} %collective-permute-do, ...), custom_call_target="tpu_custom_call", output_to_operand_aliasing={{0}: (10, {}), {1}: (11, {}), {2}: (12, {}), {3}: (13, {}),... | custom-call | flops 10871635968 | bytes 28311552 | tf_op jit(solution)/shard_map/feed_forward/pallas_call | solution.py:157
  489.7 9.1 collective-permute-done.40
  505.7 9.6 fusion.119
  515.4 5.3 collective-permute-done.41
  522.7 2.7 fusion.24
  528.5 32.8 %collective-permute-done.44 = bf16[256,3072]{1,0:T(8,128)(2,1)S(1)} collective-permute-done((bf16[256,3072]{1,0:T(8,128)(2,1)S(1)}, bf16[256,3072]{1,0:T(8,128)(2,1)S(1)}, u32[]{:S(2)}, u32[]{:S(2)}) %collective-permute-start.44) | collective-permute-done | bytes 1572896 | tf_op jit(solution)/shard_map/ppermute | solution.py:199
  562.6 2.6 fusion.5
  567.3 19.0 %collective-permute-start.45 = (bf16[128,3072]{1,0:T(8,128)(2,1)}, bf16[128,3072]{1,0:T(8,128)(2,1)}, u32[]{:S(2)}, u32[]{:S(2)}) collective-permute-start(bf16[128,3072]{1,0:T(8,128)(2,1)} %slice.714), channel_id=1, source_target_pairs={{0,8},{4,12},{8,0},{12,4},{16,24},{20,28},{24,16},{28,20},{1,9},{5... | collective-permute-start | bytes 2359304 | tf_op jit(solution)/shard_map/ppermute | solution.py:199
  590.5 2.5 copy.107
  593.6 2.7 slice.574
  596.2 6.4 collective-permute-done.45
  605.8 8.3 convolution_convert_fusion.3.refs_1_
  614.1 8.2 collective-permute-done.46
  623.1 9.6 convolution_convert_fusion.refs_0_
  636.3 3.1 pack_gradients.1
  651.6 2.7 collective-permute-start.77
  654.3 5.6 convert_add_fusion
  660.2 25.4 %collective-permute-done.50 = bf16[256,3072]{1,0:T(8,128)(2,1)S(1)} collective-permute-done((bf16[256,3072]{1,0:T(8,128)(2,1)}, bf16[256,3072]{1,0:T(8,128)(2,1)S(1)}, u32[]{:S(2)}, u32[]{:S(2)}) %collective-permute-start.50) | collective-permute-done | bytes 1572896 | tf_op jit(solution)/shard_map/ppermute | solution.py:199
  689.4 12.4 %collective-permute-done.55 = bf16[896,512]{1,0:T(8,128)(2,1)} collective-permute-done((bf16[896,512]{1,0:T(8,128)(2,1)S(1)}, bf16[896,512]{1,0:T(8,128)(2,1)}, u32[]{:S(2)}, u32[]{:S(2)}) %collective-permute-start.55) | collective-permute-done | bytes 917536 | tf_op jit(solution)/shard_map/ppermute | solution.py:199
  708.1 17.6 %collective-permute-start.76 = (bf16[896,512]{1,0:T(8,128)(2,1)S(1)}, bf16[896,512]{1,0:T(8,128)(2,1)}, u32[]{:S(2)}, u32[]{:S(2)}) collective-permute-start(bf16[896,512]{1,0:T(8,128)(2,1)S(1)} %get-tuple-element.158), channel_id=1, source_target_pairs={{0,20},{4,16},{8,28},{12,24},{16,4},{20,0},{24,12},{28,8},{1,21},{... | collective-permute-start | bytes 2752520 | tf_op jit(solution)/shard_map/ppermute | solution.py:199
  731.9 11.6 %collective-permute-done.74 = bf16[896,512]{1,0:T(8,128)(2,1)} collective-permute-done((bf16[896,512]{1,0:T(8,128)(2,1)}, bf16[896,512]{1,0:T(8,128)(2,1)}, u32[]{:S(2)}, u32[]{:S(2)}) %collective-permute-start.74) | collective-permute-done | bytes 917536 | tf_op jit(solution)/shard_map/ppermute | solution.py:199
  744.5 21.3 %collective-permute-done.76 = bf16[896,512]{1,0:T(8,128)(2,1)} collective-permute-done((bf16[896,512]{1,0:T(8,128)(2,1)S(1)}, bf16[896,512]{1,0:T(8,128)(2,1)}, u32[]{:S(2)}, u32[]{:S(2)}) %collective-permute-start.76) | collective-permute-done | bytes 917536 | tf_op jit(solution)/shard_map/ppermute | solution.py:199
  774.6 14.2 %collective-permute-done.53 = bf16[64,3072]{1,0:T(8,128)(2,1)S(1)} collective-permute-done((bf16[64,3072]{1,0:T(8,128)(2,1)S(1)}, bf16[64,3072]{1,0:T(8,128)(2,1)S(1)}, u32[]{:S(2)}, u32[]{:S(2)}) %collective-permute-start.53) | collective-permute-done | bytes 393248 | tf_op jit(solution)/shard_map/ppermute | solution.py:199
  796.9 5.0 collective-permute-done.56
  838.4 4.2 copy.122
  842.6 2.5 convolution_convert_fusion.7
  851.4 10.9 %collective-permute-done.78 = bf16[896,512]{1,0:T(8,128)(2,1)} collective-permute-done((bf16[896,512]{1,0:T(8,128)(2,1)S(1)}, bf16[896,512]{1,0:T(8,128)(2,1)}, u32[]{:S(2)}, u32[]{:S(2)}) %collective-permute-start.78) | collective-permute-done | bytes 917536 | tf_op jit(solution)/shard_map/ppermute | solution.py:199
  885.6 2.6 collective-permute-start.61
  893.7 8.9 collective-permute-done.61
  904.0 11.2 %collective-permute-done.64 = bf16[2,384,256]{2,1,0:T(8,128)(2,1)S(1)} collective-permute-done((bf16[2,384,256]{2,1,0:T(8,128)(2,1)S(1)}, bf16[2,384,256]{2,1,0:T(8,128)(2,1)S(1)}, u32[]{:S(2)}, u32[]{:S(2)}) %collective-permute-start.64) | collective-permute-done | bytes 393248 | tf_op jit(solution)/shard_map/ppermute | solution.py:199
  922.5 11.7 %collective-permute-done.72 = bf16[2,384,512]{1,2,0:T(8,128)(2,1)S(1)} collective-permute-done((bf16[2,384,512]{1,2,0:T(8,128)(2,1)S(1)}, bf16[2,384,512]{1,2,0:T(8,128)(2,1)S(1)}, u32[]{:S(2)}, u32[]{:S(2)}) %collective-permute-start.72) | collective-permute-done | bytes 786464 | tf_op jit(solution)/shard_map/ppermute | solution.py:199
  940.9 8.2 collective-permute-done.73
  950.2 5.2 collective-permute-done.69
  956.3 5.8 collective-permute-done.70
  (725 shorter events, 271.6 us)
Async XLA Ops:
  3.9 33.8 %collective-permute-start.10 = (bf16[384,256]{1,0:T(8,128)(2,1)}, bf16[384,256]{1,0:T(8,128)(2,1)}, u32[]{:S(2)}, u32[]{:S(2)}) collective-permute-start(bf16[384,256]{1,0:T(8,128)(2,1)} %get-tuple-element.276), channel_id=1, source_target_pairs={{0,4},{4,0},{8,12},{12,8},{16,20},{20,16},{24,28},{28,24},{1,5},{5... | collective-permute-start | bytes 589832 | tf_op jit(solution)/shard_map/ppermute | solution.py:199
  8.3 40.0 %collective-permute-start = (bf16[64,3072]{1,0:T(8,128)(2,1)}, bf16[64,3072]{1,0:T(8,128)(2,1)}, u32[]{:S(2)}, u32[]{:S(2)}) collective-permute-start(bf16[64,3072]{1,0:T(8,128)(2,1)} %constant_dynamic-update-slice_fusion), channel_id=1, source_target_pairs={{0,2},{1,3},{2,0},{3,1},{4,6},{5,7},{6,4},{7,5},{8,10},{9,11},{10,... | collective-permute-start | bytes 1179656 | tf_op jit(solution)/shard_map/ppermute | solution.py:199
  10.6 21.8 %collective-permute-start.2 = (bf16[112,512]{1,0:T(8,128)(2,1)}, bf16[112,512]{1,0:T(8,128)(2,1)}, u32[]{:S(2)}, u32[]{:S(2)}) collective-permute-start(bf16[112,512]{1,0:T(8,128)(2,1)} %fusion.94), channel_id=1, source_target_pairs={{0,16},{4,20},{8,24},{12,28},{16,0},{20,4},{24,8},{28,12},{1,17},{... | collective-permute-start | bytes 344072 | tf_op jit(solution)/shard_map/ppermute | solution.py:199
  13.1 30.5 %collective-permute-start.7 = (bf16[384,256]{1,0:T(8,128)(2,1)}, bf16[384,256]{1,0:T(8,128)(2,1)}, u32[]{:S(2)}, u32[]{:S(2)}) collective-permute-start(bf16[384,256]{1,0:T(8,128)(2,1)} %get-tuple-element.277), channel_id=1, source_target_pairs={{0,16},{4,20},{8,24},{12,28},{16,0},{20,4},{24,8},{28,12},{1,17},{... | collective-permute-start | bytes 589832 | tf_op jit(solution)/shard_map/ppermute | solution.py:199
  38.8 18.9 %collective-permute-start.11 = (bf16[2,384,256]{2,1,0:T(8,128)(2,1)S(1)}, bf16[2,384,256]{2,1,0:T(8,128)(2,1)S(1)}, u32[]{:S(2)}, u32[]{:S(2)}) collective-permute-start(bf16[2,384,256]{2,1,0:T(8,128)(2,1)S(1)} %maximum_select_fusion.16), channel_id=1, source_target_pairs={{0,16},{4,20},{8,24},{12,28},{16,0},{20,4},{24,8},{28,12},{1,17},{... | collective-permute-start | bytes 1179656 | tf_op jit(solution)/shard_map/ppermute | solution.py:199
  44.8 21.7 %collective-permute-start.8 = (bf16[2,384,256]{2,1,0:T(8,128)(2,1)S(1)}, bf16[2,384,256]{2,1,0:T(8,128)(2,1)S(1)}, u32[]{:S(2)}, u32[]{:S(2)}) collective-permute-start(bf16[2,384,256]{2,1,0:T(8,128)(2,1)S(1)} %maximum_select_fusion.15), channel_id=1, source_target_pairs={{0,8},{4,12},{8,0},{12,4},{16,24},{20,28},{24,16},{28,20},{1,9},{5... | collective-permute-start | bytes 1179656 | tf_op jit(solution)/shard_map/ppermute | solution.py:199
  47.6 19.5 %collective-permute-start.4 = (bf16[2,2,112,512]{3,2,1,0:T(8,128)(2,1)S(1)}, bf16[2,2,112,512]{3,2,1,0:T(8,128)(2,1)S(1)}, u32[]{:S(2)}, u32[]{:S(2)}) collective-permute-start(bf16[2,2,112,512]{3,2,1,0:T(8,128)(2,1)S(1)} %maximum_select_fusion.14), channel_id=1, source_target_pairs={{0,4},{4,0},{8,12},{12,8},{16,20},{20,16},{24,28},{28,24},{1,5},{5... | collective-permute-start | bytes 1376264 | tf_op jit(solution)/shard_map/ppermute | solution.py:199
  49.5 37.1 %collective-permute-start.1 = (bf16[128,3072]{1,0:T(8,128)(2,1)S(1)}, bf16[128,3072]{1,0:T(8,128)(2,1)S(1)}, u32[]{:S(2)}, u32[]{:S(2)}) collective-permute-start(bf16[128,3072]{1,0:T(8,128)(2,1)S(1)} %pad_maximum_fusion.9), channel_id=1, source_target_pairs={{0,1},{1,0},{2,3},{3,2},{4,5},{5,4},{6,7},{7,6},{8,9},{9,8},{10,11... | collective-permute-start | bytes 2359304 | tf_op jit(solution)/shard_map/ppermute | solution.py:199
  57.9 56.4 %collective-permute-start.12 = (bf16[2,2,384,256]{3,2,1,0:T(8,128)(2,1)S(1)}, bf16[2,2,384,256]{3,2,1,0:T(8,128)(2,1)S(1)}, u32[]{:S(2)}, u32[]{:S(2)}) collective-permute-start(bf16[2,2,384,256]{3,2,1,0:T(8,128)(2,1)S(1)} %maximum_select_fusion.11), channel_id=1, source_target_pairs={{0,8},{4,12},{8,0},{12,4},{16,24},{20,28},{24,16},{28,20},{1,9},{5... | collective-permute-start | bytes 2359304 | tf_op jit(solution)/shard_map/ppermute | solution.py:199
  66.6 50.9 %collective-permute-start.9 = (bf16[2,2,384,256]{3,2,0,1:T(8,128)(2,1)S(1)}, bf16[2,2,384,256]{3,2,0,1:T(8,128)(2,1)S(1)}, u32[]{:S(2)}, u32[]{:S(2)}) collective-permute-start(bf16[2,2,384,256]{3,2,0,1:T(8,128)(2,1)S(1)} %maximum_select_fusion.9), channel_id=1, source_target_pairs={{0,4},{4,0},{8,12},{12,8},{16,20},{20,16},{24,28},{28,24},{1,5},{5... | collective-permute-start | bytes 2359304 | tf_op jit(solution)/shard_map/ppermute | solution.py:199
  67.1 22.2 %collective-permute-start.5 = (bf16[2,2,2,112,512]{4,3,2,1,0:T(8,128)(2,1)S(1)}, bf16[2,2,2,112,512]{4,3,2,1,0:T(8,128)(2,1)S(1)}, u32[]{:S(2)}, u32[]{:S(2)}) collective-permute-start(bf16[2,2,2,112,512]{4,3,2,1,0:T(8,128)(2,1)S(1)} %maximum_select_fusion.8), channel_id=1, source_target_pairs={{0,2},{1,3},{2,0},{3,1},{4,6},{5,7},{6,4},{7,5},{8,10},{9,11},{10,... | collective-permute-start | bytes 2752520 | tf_op jit(solution)/shard_map/ppermute | solution.py:199
  82.5 28.9 %collective-permute-start.14 = (bf16[2,384,512]{2,1,0:T(8,128)(2,1)S(1)}, bf16[2,384,512]{2,1,0:T(8,128)(2,1)S(1)}, u32[]{:S(2)}, u32[]{:S(2)}) collective-permute-start(bf16[2,384,512]{2,1,0:T(8,128)(2,1)S(1)} %maximum_select_fusion.13), channel_id=1, source_target_pairs={{0,8},{4,12},{8,0},{12,4},{16,24},{20,28},{24,16},{28,20},{1,9},{5... | collective-permute-start | bytes 2359304 | tf_op jit(solution)/shard_map/ppermute | solution.py:199
  86.6 25.9 %collective-permute-start.17 = (bf16[64,3072]{1,0:T(8,128)(2,1)S(1)}, bf16[64,3072]{1,0:T(8,128)(2,1)S(1)}, u32[]{:S(2)}, u32[]{:S(2)}) collective-permute-start(bf16[64,3072]{1,0:T(8,128)(2,1)S(1)} %get-tuple-element.98), channel_id=1, source_target_pairs={{0,16},{4,20},{8,24},{12,28},{16,0},{20,4},{24,8},{28,12},{1,17},{... | collective-permute-start | bytes 1179656 | tf_op jit(solution)/shard_map/ppermute | solution.py:199
  89.6 59.1 %collective-permute-start.6 = (bf16[2,2,2,2,112,512]{5,4,2,1,0,3:T(8,128)(2,1)S(1)}, bf16[2,2,2,2,112,512]{5,4,2,1,0,3:T(8,128)(2,1)S(1)}, u32[]{:S(2)}, u32[]{:S(2)}) collective-permute-start(bf16[2,2,2,2,112,512]{5,4,2,1,0,3:T(8,128)(2,1)S(1)} %maximum_select_fusion.2), channel_id=1, source_target_pairs={{0,1},{1,0},{2,3},{3,2},{4,5},{5,4},{6,7},{7,6},{8,9},{9,8},{10,11... | collective-permute-start | bytes 5505032 | tf_op jit(solution)/shard_map/ppermute | solution.py:199
  111.6 34.7 %collective-permute-start.15 = (bf16[2,2,384,512]{3,2,0,1:T(8,128)(2,1)S(1)}, bf16[2,2,384,512]{3,2,0,1:T(8,128)(2,1)S(1)}, u32[]{:S(2)}, u32[]{:S(2)}) collective-permute-start(bf16[2,2,384,512]{3,2,0,1:T(8,128)(2,1)S(1)} %maximum_select_fusion.6), channel_id=1, source_target_pairs={{0,4},{4,0},{8,12},{12,8},{16,20},{20,16},{24,28},{28,24},{1,5},{5... | collective-permute-start | bytes 4718600 | tf_op jit(solution)/shard_map/ppermute | solution.py:199
  112.5 56.1 %collective-permute-start.16 = (bf16[896,512]{1,0:T(8,128)(2,1)}, bf16[896,512]{1,0:T(8,128)(2,1)S(1)}, u32[]{:S(2)}, u32[]{:S(2)}) collective-permute-start(bf16[896,512]{1,0:T(8,128)(2,1)} %get-tuple-element.97), channel_id=1, source_target_pairs={{0,16},{4,20},{8,24},{12,28},{16,0},{20,4},{24,8},{28,12},{1,17},{... | collective-permute-start | bytes 2752520 | tf_op jit(solution)/shard_map/ppermute | solution.py:199
  114.3 54.4 %collective-permute-start.18 = (bf16[128,3072]{1,0:T(8,128)(2,1)}, bf16[128,3072]{1,0:T(8,128)(2,1)}, u32[]{:S(2)}, u32[]{:S(2)}) collective-permute-start(bf16[128,3072]{1,0:T(8,128)(2,1)} %pad_maximum_fusion.10), channel_id=1, source_target_pairs={{0,8},{4,12},{8,0},{12,4},{16,24},{20,28},{24,16},{28,20},{1,9},{5... | collective-permute-start | bytes 2359304 | tf_op jit(solution)/shard_map/ppermute | solution.py:199
  173.4 42.9 %collective-permute-start.21 = (bf16[896,512]{1,0:T(8,128)(2,1)}, bf16[896,512]{1,0:T(8,128)(2,1)S(1)}, u32[]{:S(2)}, u32[]{:S(2)}) collective-permute-start(bf16[896,512]{1,0:T(8,128)(2,1)} %get-tuple-element.101), channel_id=1, source_target_pairs={{0,20},{4,16},{8,28},{12,24},{16,4},{20,0},{24,12},{28,8},{1,21},{... | collective-permute-start | bytes 2752520 | tf_op jit(solution)/shard_map/ppermute | solution.py:199
  173.4 43.2 %collective-permute-start.22 = (bf16[896,512]{1,0:T(8,128)(2,1)}, bf16[896,512]{1,0:T(8,128)(2,1)}, u32[]{:S(2)}, u32[]{:S(2)}) collective-permute-start(bf16[896,512]{1,0:T(8,128)(2,1)} %get-tuple-element.103), channel_id=1, source_target_pairs={{0,4},{4,0},{8,12},{12,8},{16,20},{20,16},{24,28},{28,24},{1,5},{5... | collective-permute-start | bytes 2752520 | tf_op jit(solution)/shard_map/ppermute | solution.py:199
  176.8 73.9 %collective-permute-start.27 = (bf16[256,3072]{1,0:T(8,128)(2,1)}, bf16[256,3072]{1,0:T(8,128)(2,1)}, u32[]{:S(2)}, u32[]{:S(2)}) collective-permute-start(bf16[256,3072]{1,0:T(8,128)(2,1)} %pad_maximum_fusion.3), channel_id=1, source_target_pairs={{0,2},{1,3},{2,0},{3,1},{4,6},{5,7},{6,4},{7,5},{8,10},{9,11},{10,... | collective-permute-start | bytes 4718600 | tf_op jit(solution)/shard_map/ppermute | solution.py:199
  178.3 70.9 %collective-permute-start.28 = (bf16[256,3072]{1,0:T(8,128)(2,1)}, bf16[256,3072]{1,0:T(8,128)(2,1)}, u32[]{:S(2)}, u32[]{:S(2)}) collective-permute-start(bf16[256,3072]{1,0:T(8,128)(2,1)} %pad_maximum_fusion.3), channel_id=1, source_target_pairs={{0,4},{4,0},{8,12},{12,8},{16,20},{20,16},{24,28},{28,24},{1,5},{5... | collective-permute-start | bytes 4718600 | tf_op jit(solution)/shard_map/ppermute | solution.py:199
  216.7 36.8 %collective-permute-start.23 = (bf16[64,3072]{1,0:T(8,128)(2,1)S(1)}, bf16[64,3072]{1,0:T(8,128)(2,1)S(1)}, u32[]{:S(2)}, u32[]{:S(2)}) collective-permute-start(bf16[64,3072]{1,0:T(8,128)(2,1)S(1)} %pad_maximum_fusion.18), channel_id=1, source_target_pairs={{0,16},{4,20},{8,24},{12,28},{16,0},{20,4},{24,8},{28,12},{1,17},{... | collective-permute-start | bytes 1179656 | tf_op jit(solution)/shard_map/ppermute | solution.py:199
  249.2 37.5 %collective-permute-start.29 = (bf16[256,3072]{1,0:T(8,128)(2,1)}, bf16[256,3072]{1,0:T(8,128)(2,1)S(1)}, u32[]{:S(2)}, u32[]{:S(2)}) collective-permute-start(bf16[256,3072]{1,0:T(8,128)(2,1)} %collective-permute-done.28), channel_id=1, source_target_pairs={{0,2},{1,3},{2,0},{3,1},{4,6},{5,7},{6,4},{7,5},{8,10},{9,11},{10,... | collective-permute-start | bytes 4718600 | tf_op jit(solution)/shard_map/ppermute | solution.py:199
  253.5 18.8 %collective-permute-start.24 = (bf16[128,3072]{1,0:T(8,128)(2,1)S(1)}, bf16[128,3072]{1,0:T(8,128)(2,1)S(1)}, u32[]{:S(2)}, u32[]{:S(2)}) collective-permute-start(bf16[128,3072]{1,0:T(8,128)(2,1)S(1)} %pad_maximum_fusion.11), channel_id=1, source_target_pairs={{0,8},{4,12},{8,0},{12,4},{16,24},{20,28},{24,16},{28,20},{1,9},{5... | collective-permute-start | bytes 2359304 | tf_op jit(solution)/shard_map/ppermute | solution.py:199
  273.4 45.0 %collective-permute-start.25 = (bf16[256,3072]{1,0:T(8,128)(2,1)S(1)}, bf16[256,3072]{1,0:T(8,128)(2,1)S(1)}, u32[]{:S(2)}, u32[]{:S(2)}) collective-permute-start(bf16[256,3072]{1,0:T(8,128)(2,1)S(1)} %get-tuple-element.256.refs_0_), channel_id=1, source_target_pairs={{0,2},{1,3},{2,0},{3,1},{4,6},{5,7},{6,4},{7,5},{8,10},{9,11},{10,... | collective-permute-start | bytes 4718600 | tf_op jit(solution)/shard_map/ppermute | solution.py:199
  288.1 153.7 %collective-permute-start.35 = (bf16[1024,3072]{1,0:T(8,128)(2,1)}, bf16[1024,3072]{1,0:T(8,128)(2,1)S(1)}, u32[]{:S(2)}, u32[]{:S(2)}) collective-permute-start(bf16[1024,3072]{1,0:T(8,128)(2,1)} %constant_dynamic-update-slice_fusion.8.refs_3_.refs_4_.refs_5_.refs_2_), channel_id=1, source_target_pairs={{0,1},{1,0},{2,3},{3,2},{4,5},{5,4},{6,7},{7,6},{8,9},{9,8},{10,11... | collective-permute-start | bytes 18874376 | tf_op jit(solution)/shard_map/ppermute | solution.py:199
  288.1 36.8 %collective-permute-start.26 = (bf16[256,3072]{1,0:T(8,128)(2,1)S(1)}, bf16[256,3072]{1,0:T(8,128)(2,1)S(1)}, u32[]{:S(2)}, u32[]{:S(2)}) collective-permute-start(bf16[256,3072]{1,0:T(8,128)(2,1)S(1)} %get-tuple-element.256.refs_0_), channel_id=1, source_target_pairs={{0,4},{4,0},{8,12},{12,8},{16,20},{20,16},{24,28},{28,24},{1,5},{5... | collective-permute-start | bytes 4718600 | tf_op jit(solution)/shard_map/ppermute | solution.py:199
  326.3 136.7 %collective-permute-start.34 = (bf16[768,3072]{1,0:T(8,128)(2,1)}, bf16[768,3072]{1,0:T(8,128)(2,1)}, u32[]{:S(2)}, u32[]{:S(2)}) collective-permute-start(bf16[768,3072]{1,0:T(8,128)(2,1)} %constant_dynamic-update-slice_fusion.14), channel_id=1, source_target_pairs={{0,1},{1,0},{2,3},{3,2},{4,5},{5,4},{6,7},{7,6},{8,9},{9,8},{10,11... | collective-permute-start | bytes 14155784 | tf_op jit(solution)/shard_map/ppermute | solution.py:199
  326.3 23.8 %collective-permute-start.31 = (bf16[896,512]{1,0:T(8,128)(2,1)S(1)}, bf16[896,512]{1,0:T(8,128)(2,1)S(1)}, u32[]{:S(2)}, u32[]{:S(2)}) collective-permute-start(bf16[896,512]{1,0:T(8,128)(2,1)S(1)} %copy-done.15), channel_id=1, source_target_pairs={{0,12},{4,8},{8,4},{12,0},{16,28},{20,24},{24,20},{28,16},{1,13},{... | collective-permute-start | bytes 2752520 | tf_op jit(solution)/shard_map/ppermute | solution.py:199
  327.6 24.9 %collective-permute-start.36 = (bf16[128,3072]{1,0:T(8,128)(2,1)S(1)}, bf16[128,3072]{1,0:T(8,128)(2,1)S(1)}, u32[]{:S(2)}, u32[]{:S(2)}) collective-permute-start(bf16[128,3072]{1,0:T(8,128)(2,1)S(1)} %slice.704), channel_id=1, source_target_pairs={{0,2},{1,3},{2,0},{3,1},{4,6},{5,7},{6,4},{7,5},{8,10},{9,11},{10,... | collective-permute-start | bytes 2359304 | tf_op jit(solution)/shard_map/ppermute | solution.py:199
  329.3 57.2 %collective-permute-start.37 = (bf16[128,3072]{1,0:T(8,128)(2,1)S(1)}, bf16[128,3072]{1,0:T(8,128)(2,1)S(1)}, u32[]{:S(2)}, u32[]{:S(2)}) collective-permute-start(bf16[128,3072]{1,0:T(8,128)(2,1)S(1)} %slice.705), channel_id=1, source_target_pairs={{0,4},{4,0},{8,12},{12,8},{16,20},{20,16},{24,28},{28,24},{1,5},{5... | collective-permute-start | bytes 2359304 | tf_op jit(solution)/shard_map/ppermute | solution.py:199
  350.1 39.9 %collective-permute-start.33 = (bf16[896,512]{1,0:T(8,128)(2,1)S(1)}, bf16[896,512]{1,0:T(8,128)(2,1)S(1)}, u32[]{:S(2)}, u32[]{:S(2)}) collective-permute-start(bf16[896,512]{1,0:T(8,128)(2,1)S(1)} %copy-done.13), channel_id=1, source_target_pairs={{0,28},{4,24},{8,20},{12,16},{16,12},{20,8},{24,4},{28,0},{1,29},{... | collective-permute-start | bytes 2752520 | tf_op jit(solution)/shard_map/ppermute | solution.py:199
  352.6 42.3 %collective-permute-start.30 = (bf16[896,512]{1,0:T(8,128)(2,1)S(1)}, bf16[896,512]{1,0:T(8,128)(2,1)S(1)}, u32[]{:S(2)}, u32[]{:S(2)}) collective-permute-start(bf16[896,512]{1,0:T(8,128)(2,1)S(1)} %copy-done.11), channel_id=1, source_target_pairs={{0,8},{4,12},{8,0},{12,4},{16,24},{20,28},{24,16},{28,20},{1,9},{5... | collective-permute-start | bytes 2752520 | tf_op jit(solution)/shard_map/ppermute | solution.py:199
  386.5 26.8 %collective-permute-start.32 = (bf16[896,512]{1,0:T(8,128)(2,1)S(1)}, bf16[896,512]{1,0:T(8,128)(2,1)S(1)}, u32[]{:S(2)}, u32[]{:S(2)}) collective-permute-start(bf16[896,512]{1,0:T(8,128)(2,1)S(1)} %copy-done.9), channel_id=1, source_target_pairs={{0,24},{4,28},{8,16},{12,20},{16,8},{20,12},{24,0},{28,4},{1,25},{... | collective-permute-start | bytes 2752520 | tf_op jit(solution)/shard_map/ppermute | solution.py:199
  389.9 51.8 %collective-permute-start.38 = (bf16[256,3072]{1,0:T(8,128)(2,1)}, bf16[256,3072]{1,0:T(8,128)(2,1)}, u32[]{:S(2)}, u32[]{:S(2)}) collective-permute-start(bf16[256,3072]{1,0:T(8,128)(2,1)} %constant_dynamic-update-slice_fusion.19.refs_0_), channel_id=1, source_target_pairs={{0,1},{1,0},{2,3},{3,2},{4,5},{5,4},{6,7},{7,6},{8,9},{9,8},{10,11... | collective-permute-start | bytes 4718600 | tf_op jit(solution)/shard_map/ppermute | solution.py:199
  500.7 20.0 %collective-permute-start.41 = (bf16[128,3072]{1,0:T(8,128)(2,1)}, bf16[128,3072]{1,0:T(8,128)(2,1)S(1)}, u32[]{:S(2)}, u32[]{:S(2)}) collective-permute-start(bf16[128,3072]{1,0:T(8,128)(2,1)} %get-tuple-element.197), channel_id=1, source_target_pairs={{0,4},{4,0},{8,12},{12,8},{16,20},{20,16},{24,28},{28,24},{1,5},{5... | collective-permute-start | bytes 2359304 | tf_op jit(solution)/shard_map/ppermute | solution.py:199
  502.1 19.7 %collective-permute-start.43 = (bf16[128,3072]{1,0:T(8,128)(2,1)}, bf16[128,3072]{1,0:T(8,128)(2,1)S(1)}, u32[]{:S(2)}, u32[]{:S(2)}) collective-permute-start(bf16[128,3072]{1,0:T(8,128)(2,1)} %get-tuple-element.198), channel_id=1, source_target_pairs={{0,2},{1,3},{2,0},{3,1},{4,6},{5,7},{6,4},{7,5},{8,10},{9,11},{10,... | collective-permute-start | bytes 2359304 | tf_op jit(solution)/shard_map/ppermute | solution.py:199
  525.6 35.7 %collective-permute-start.44 = (bf16[256,3072]{1,0:T(8,128)(2,1)S(1)}, bf16[256,3072]{1,0:T(8,128)(2,1)S(1)}, u32[]{:S(2)}, u32[]{:S(2)}) collective-permute-start(bf16[256,3072]{1,0:T(8,128)(2,1)S(1)} %pad_maximum_fusion.5), channel_id=1, source_target_pairs={{0,4},{4,0},{8,12},{12,8},{16,20},{20,16},{24,28},{28,24},{1,5},{5... | collective-permute-start | bytes 4718600 | tf_op jit(solution)/shard_map/ppermute | solution.py:199
  526.9 35.6 %collective-permute-start.42 = (bf16[256,3072]{1,0:T(8,128)(2,1)S(1)}, bf16[256,3072]{1,0:T(8,128)(2,1)S(1)}, u32[]{:S(2)}, u32[]{:S(2)}) collective-permute-start(bf16[256,3072]{1,0:T(8,128)(2,1)S(1)} %pad_maximum_fusion.4), channel_id=1, source_target_pairs={{0,2},{1,3},{2,0},{3,1},{4,6},{5,7},{6,4},{7,5},{8,10},{9,11},{10,... | collective-permute-start | bytes 4718600 | tf_op jit(solution)/shard_map/ppermute | solution.py:199
  567.3 35.4 %collective-permute-start.45 = (bf16[128,3072]{1,0:T(8,128)(2,1)}, bf16[128,3072]{1,0:T(8,128)(2,1)}, u32[]{:S(2)}, u32[]{:S(2)}) collective-permute-start(bf16[128,3072]{1,0:T(8,128)(2,1)} %slice.714), channel_id=1, source_target_pairs={{0,8},{4,12},{8,0},{12,4},{16,24},{20,28},{24,16},{28,20},{1,9},{5... | collective-permute-start | bytes 2359304 | tf_op jit(solution)/shard_map/ppermute | solution.py:199
  604.2 18.1 %collective-permute-start.46 = (bf16[64,3072]{1,0:T(8,128)(2,1)S(1)}, bf16[64,3072]{1,0:T(8,128)(2,1)S(1)}, u32[]{:S(2)}, u32[]{:S(2)}) collective-permute-start(bf16[64,3072]{1,0:T(8,128)(2,1)S(1)} %slice.715), channel_id=1, source_target_pairs={{0,16},{4,20},{8,24},{12,28},{16,0},{20,4},{24,8},{28,12},{1,17},{... | collective-permute-start | bytes 1179656 | tf_op jit(solution)/shard_map/ppermute | solution.py:199
  622.3 32.0 %collective-permute-start.47 = (bf16[768,3072]{1,0:T(8,128)(2,1)}, bf16[768,3072]{1,0:T(8,128)(2,1)}, u32[]{:S(2)}, u32[]{:S(2)}) collective-permute-start(bf16[768,3072]{1,0:T(8,128)(2,1)} %get-tuple-element.138), channel_id=1, source_target_pairs={{0,1},{1,0},{2,3},{3,2},{4,5},{5,4},{6,7},{7,6},{8,9},{9,8},{10,11... | collective-permute-start | bytes 14155784 | tf_op jit(solution)/shard_map/ppermute | solution.py:199
  639.4 64.0 %collective-permute-start.54 = (bf16[896,512]{1,0:T(8,128)(2,1)S(1)}, bf16[896,512]{1,0:T(8,128)(2,1)}, u32[]{:S(2)}, u32[]{:S(2)}) collective-permute-start(bf16[896,512]{1,0:T(8,128)(2,1)S(1)} %get-tuple-element.149), channel_id=1, source_target_pairs={{0,16},{4,20},{8,24},{12,28},{16,0},{20,4},{24,8},{28,12},{1,17},{... | collective-permute-start | bytes 2752520 | tf_op jit(solution)/shard_map/ppermute | solution.py:199
  639.5 62.2 %collective-permute-start.55 = (bf16[896,512]{1,0:T(8,128)(2,1)S(1)}, bf16[896,512]{1,0:T(8,128)(2,1)}, u32[]{:S(2)}, u32[]{:S(2)}) collective-permute-start(bf16[896,512]{1,0:T(8,128)(2,1)S(1)} %get-tuple-element.150), channel_id=1, source_target_pairs={{0,8},{4,12},{8,0},{12,4},{16,24},{20,28},{24,16},{28,20},{1,9},{5... | collective-permute-start | bytes 2752520 | tf_op jit(solution)/shard_map/ppermute | solution.py:199
  649.2 36.4 %collective-permute-start.50 = (bf16[256,3072]{1,0:T(8,128)(2,1)}, bf16[256,3072]{1,0:T(8,128)(2,1)S(1)}, u32[]{:S(2)}, u32[]{:S(2)}) collective-permute-start(bf16[256,3072]{1,0:T(8,128)(2,1)} %add_convert_fusion), channel_id=1, source_target_pairs={{0,2},{1,3},{2,0},{3,1},{4,6},{5,7},{6,4},{7,5},{8,10},{9,11},{10,... | collective-permute-start | bytes 4718600 | tf_op jit(solution)/shard_map/ppermute | solution.py:199
  651.6 53.5 %collective-permute-start.77 = (bf16[896,512]{1,0:T(8,128)(2,1)S(1)}, bf16[896,512]{1,0:T(8,128)(2,1)}, u32[]{:S(2)}, u32[]{:S(2)}) collective-permute-start(bf16[896,512]{1,0:T(8,128)(2,1)S(1)} %get-tuple-element.160), channel_id=1, source_target_pairs={{0,24},{4,28},{8,16},{12,20},{16,8},{20,12},{24,0},{28,4},{1,25},{... | collective-permute-start | bytes 2752520 | tf_op jit(solution)/shard_map/ppermute | solution.py:199
  686.1 40.5 %collective-permute-start.51 = (bf16[256,3072]{1,0:T(8,128)(2,1)S(1)}, bf16[256,3072]{1,0:T(8,128)(2,1)S(1)}, u32[]{:S(2)}, u32[]{:S(2)}) collective-permute-start(bf16[256,3072]{1,0:T(8,128)(2,1)S(1)} %fusion.1), channel_id=1, source_target_pairs={{0,4},{4,0},{8,12},{12,8},{16,20},{20,16},{24,28},{28,24},{1,5},{5... | collective-permute-start | bytes 4718600 | tf_op jit(solution)/shard_map/ppermute | solution.py:199
  687.9 38.8 %collective-permute-start.48 = (bf16[256,3072]{1,0:T(8,128)(2,1)S(1)}, bf16[256,3072]{1,0:T(8,128)(2,1)S(1)}, u32[]{:S(2)}, u32[]{:S(2)}) collective-permute-start(bf16[256,3072]{1,0:T(8,128)(2,1)S(1)} %slice.992), channel_id=1, source_target_pairs={{0,2},{1,3},{2,0},{3,1},{4,6},{5,7},{6,4},{7,5},{8,10},{9,11},{10,... | collective-permute-start | bytes 4718600 | tf_op jit(solution)/shard_map/ppermute | solution.py:199
  706.8 36.7 %collective-permute-start.74 = (bf16[896,512]{1,0:T(8,128)(2,1)}, bf16[896,512]{1,0:T(8,128)(2,1)}, u32[]{:S(2)}, u32[]{:S(2)}) collective-permute-start(bf16[896,512]{1,0:T(8,128)(2,1)} %get-tuple-element.154), channel_id=1, source_target_pairs={{0,4},{4,0},{8,12},{12,8},{16,20},{20,16},{24,28},{28,24},{1,5},{5... | collective-permute-start | bytes 2752520 | tf_op jit(solution)/shard_map/ppermute | solution.py:199
  708.1 57.7 %collective-permute-start.76 = (bf16[896,512]{1,0:T(8,128)(2,1)S(1)}, bf16[896,512]{1,0:T(8,128)(2,1)}, u32[]{:S(2)}, u32[]{:S(2)}) collective-permute-start(bf16[896,512]{1,0:T(8,128)(2,1)S(1)} %get-tuple-element.158), channel_id=1, source_target_pairs={{0,20},{4,16},{8,28},{12,24},{16,4},{20,0},{24,12},{28,8},{1,21},{... | collective-permute-start | bytes 2752520 | tf_op jit(solution)/shard_map/ppermute | solution.py:199
  728.4 39.0 %collective-permute-start.52 = (bf16[128,3072]{1,0:T(8,128)(2,1)}, bf16[128,3072]{1,0:T(8,128)(2,1)}, u32[]{:S(2)}, u32[]{:S(2)}) collective-permute-start(bf16[128,3072]{1,0:T(8,128)(2,1)} %slice.720), channel_id=1, source_target_pairs={{0,8},{4,12},{8,0},{12,4},{16,24},{20,28},{24,16},{28,20},{1,9},{5... | collective-permute-start | bytes 2359304 | tf_op jit(solution)/shard_map/ppermute | solution.py:199
  769.1 19.6 %collective-permute-start.53 = (bf16[64,3072]{1,0:T(8,128)(2,1)S(1)}, bf16[64,3072]{1,0:T(8,128)(2,1)S(1)}, u32[]{:S(2)}, u32[]{:S(2)}) collective-permute-start(bf16[64,3072]{1,0:T(8,128)(2,1)S(1)} %slice.722), channel_id=1, source_target_pairs={{0,16},{4,20},{8,24},{12,28},{16,0},{20,4},{24,8},{28,12},{1,17},{... | collective-permute-start | bytes 1179656 | tf_op jit(solution)/shard_map/ppermute | solution.py:199
  802.9 45.6 %collective-permute-start.75 = (bf16[896,512]{1,0:T(8,128)(2,1)S(1)}, bf16[896,512]{1,0:T(8,128)(2,1)}, u32[]{:S(2)}, u32[]{:S(2)}) collective-permute-start(bf16[896,512]{1,0:T(8,128)(2,1)S(1)} %get-tuple-element.156), channel_id=1, source_target_pairs={{0,12},{4,8},{8,4},{12,0},{16,28},{20,24},{24,20},{28,16},{1,13},{... | collective-permute-start | bytes 2752520 | tf_op jit(solution)/shard_map/ppermute | solution.py:199
  803.0 59.4 %collective-permute-start.78 = (bf16[896,512]{1,0:T(8,128)(2,1)S(1)}, bf16[896,512]{1,0:T(8,128)(2,1)}, u32[]{:S(2)}, u32[]{:S(2)}) collective-permute-start(bf16[896,512]{1,0:T(8,128)(2,1)S(1)} %get-tuple-element.162), channel_id=1, source_target_pairs={{0,28},{4,24},{8,20},{12,16},{16,12},{20,8},{24,4},{28,0},{1,29},{... | collective-permute-start | bytes 2752520 | tf_op jit(solution)/shard_map/ppermute | solution.py:199
  825.1 65.6 %collective-permute-start.58 = (bf16[128,3072]{1,0:T(8,128)(2,1)}, bf16[128,3072]{1,0:T(8,128)(2,1)}, u32[]{:S(2)}, u32[]{:S(2)}) collective-permute-start(bf16[128,3072]{1,0:T(8,128)(2,1)} %pad_maximum_fusion.8), channel_id=1, source_target_pairs={{0,1},{1,0},{2,3},{3,2},{4,5},{5,4},{6,7},{7,6},{8,9},{9,8},{10,11... | collective-permute-start | bytes 2359304 | tf_op jit(solution)/shard_map/ppermute | solution.py:199
  827.3 56.9 %collective-permute-start.60 = (bf16[2,2,384,256]{3,2,0,1:T(8,128)(2,1)}, bf16[2,2,384,256]{3,2,0,1:T(8,128)(2,1)}, u32[]{:S(2)}, u32[]{:S(2)}) collective-permute-start(bf16[2,2,384,256]{3,2,0,1:T(8,128)(2,1)} %bitcast.303), channel_id=1, source_target_pairs={{0,4},{4,0},{8,12},{12,8},{16,20},{20,16},{24,28},{28,24},{1,5},{5... | collective-permute-start | bytes 2359304 | tf_op jit(solution)/shard_map/ppermute | solution.py:199
  828.2 59.9 %collective-permute-start.63 = (bf16[2,2,384,256]{3,2,1,0:T(8,128)(2,1)}, bf16[2,2,384,256]{3,2,1,0:T(8,128)(2,1)}, u32[]{:S(2)}, u32[]{:S(2)}) collective-permute-start(bf16[2,2,384,256]{3,2,1,0:T(8,128)(2,1)} %fusion.54), channel_id=1, source_target_pairs={{0,8},{4,12},{8,0},{12,4},{16,24},{20,28},{24,16},{28,20},{1,9},{5... | collective-permute-start | bytes 2359304 | tf_op jit(solution)/shard_map/ppermute | solution.py:199
  848.8 69.7 %collective-permute-start.66 = (bf16[2,2,2,2,112,512]{5,4,0,1,2,3:T(8,128)(2,1)S(1)}, bf16[2,2,2,2,112,512]{5,4,0,1,2,3:T(8,128)(2,1)S(1)}, u32[]{:S(2)}, u32[]{:S(2)}) collective-permute-start(bf16[2,2,2,2,112,512]{5,4,0,1,2,3:T(8,128)(2,1)S(1)} %bitcast.364), channel_id=1, source_target_pairs={{0,1},{1,0},{2,3},{3,2},{4,5},{5,4},{6,7},{7,6},{8,9},{9,8},{10,11... | collective-permute-start | bytes 5505032 | tf_op jit(solution)/shard_map/ppermute | solution.py:199
  862.4 55.4 %collective-permute-start.71 = (bf16[2,2,384,512]{2,3,0,1:T(8,128)(2,1)S(1)}, bf16[2,2,384,512]{2,3,0,1:T(8,128)(2,1)S(1)}, u32[]{:S(2)}, u32[]{:S(2)}) collective-permute-start(bf16[2,2,384,512]{2,3,0,1:T(8,128)(2,1)S(1)} %fusion.20), channel_id=1, source_target_pairs={{0,4},{4,0},{8,12},{12,8},{16,20},{20,16},{24,28},{28,24},{1,5},{5... | collective-permute-start | bytes 4718600 | tf_op jit(solution)/shard_map/ppermute | solution.py:199
  885.6 17.0 %collective-permute-start.61 = (bf16[2,384,256]{2,1,0:T(8,128)(2,1)S(1)}, bf16[2,384,256]{2,1,0:T(8,128)(2,1)S(1)}, u32[]{:S(2)}, u32[]{:S(2)}) collective-permute-start(bf16[2,384,256]{2,1,0:T(8,128)(2,1)S(1)} %dynamic-slice_bitcast_fusion.5), channel_id=1, source_target_pairs={{0,8},{4,12},{8,0},{12,4},{16,24},{20,28},{24,16},{28,20},{1,9},{5... | collective-permute-start | bytes 1179656 | tf_op jit(solution)/shard_map/ppermute | solution.py:199
  889.5 25.6 %collective-permute-start.64 = (bf16[2,384,256]{2,1,0:T(8,128)(2,1)S(1)}, bf16[2,384,256]{2,1,0:T(8,128)(2,1)S(1)}, u32[]{:S(2)}, u32[]{:S(2)}) collective-permute-start(bf16[2,384,256]{2,1,0:T(8,128)(2,1)S(1)} %dynamic-slice_bitcast_fusion.4), channel_id=1, source_target_pairs={{0,16},{4,20},{8,24},{12,28},{16,0},{20,4},{24,8},{28,12},{1,17},{... | collective-permute-start | bytes 1179656 | tf_op jit(solution)/shard_map/ppermute | solution.py:199
  892.1 24.2 %collective-permute-start.59 = (bf16[64,3072]{1,0:T(8,128)(2,1)S(1)}, bf16[64,3072]{1,0:T(8,128)(2,1)S(1)}, u32[]{:S(2)}, u32[]{:S(2)}) collective-permute-start(bf16[64,3072]{1,0:T(8,128)(2,1)S(1)} %slice.743), channel_id=1, source_target_pairs={{0,2},{1,3},{2,0},{3,1},{4,6},{5,7},{6,4},{7,5},{8,10},{9,11},{10,... | collective-permute-start | bytes 1179656 | tf_op jit(solution)/shard_map/ppermute | solution.py:199
  902.8 19.6 %collective-permute-start.62 = (bf16[384,256]{1,0:T(8,128)(2,1)S(1)}, bf16[384,256]{1,0:T(8,128)(2,1)S(1)}, u32[]{:S(2)}, u32[]{:S(2)}) collective-permute-start(bf16[384,256]{1,0:T(8,128)(2,1)S(1)} %dynamic-slice_bitcast_fusion.8), channel_id=1, source_target_pairs={{0,16},{4,20},{8,24},{12,28},{16,0},{20,4},{24,8},{28,12},{1,17},{... | collective-permute-start | bytes 589832 | tf_op jit(solution)/shard_map/ppermute | solution.py:199
  920.0 17.2 %collective-permute-start.67 = (bf16[2,2,2,112,512]{4,3,0,1,2:T(8,128)(2,1)S(1)}, bf16[2,2,2,112,512]{4,3,0,1,2:T(8,128)(2,1)S(1)}, u32[]{:S(2)}, u32[]{:S(2)}) collective-permute-start(bf16[2,2,2,112,512]{4,3,0,1,2:T(8,128)(2,1)S(1)} %dynamic-slice_bitcast_fusion), channel_id=1, source_target_pairs={{0,2},{1,3},{2,0},{3,1},{4,6},{5,7},{6,4},{7,5},{8,10},{9,11},{10,... | collective-permute-start | bytes 2752520 | tf_op jit(solution)/shard_map/ppermute | solution.py:199
  (180 other events, 1927.0 us)

commit v3 on v2

--- a/solution.py
+++ b/solution.py
@@ -522,8 +522,8 @@
             return [k for k in distances if first * n_wide <= 8 * k < last * n_wide]
 
         send_packets(share(4, 5), weight_packet, query_events[0])
-        send_packets(share(5, 6), weight_packet, shared_events[-2])
-        send_packets(share(0, 2), weight_packet, shared_events[-2])
+        send_packets(share(6, 7), weight_packet, shared_events[-2])
+        send_packets(share(2, 3), weight_packet, shared_events[-2])
 
         all_normed = [
             rms_norm(item_rows[stream].astype(wider), first_gain[stream]).astype(low)
@@ -604,15 +604,15 @@
             axis=1,
         )
         token_events = []
-        normed2 = tie(normed2, *(packets[k] for k in share(5, 6) + share(0, 2)))
+        normed2 = tie(normed2, *(packets[k] for k in share(6, 7) + share(2, 3)))
         near = gather_all(normed2, token_events, True)
         if copying:
             other_most = hop(jnp.concatenate(near[:3], axis=0), core)
             token_far = [(other_most, i) for i in range(3)] + [(hop(near[3], core), 0)]
         else:
             token_far = [(hop(rows, core), 0) for rows in near]
-        send_packets(share(6, 7), weight_packet, token_events[-1])
-        send_packets(share(2, 3), weight_packet, token_events[-1])
+        send_packets(share(5, 6), weight_packet, token_events[-1])
+        send_packets(share(0, 2), weight_packet, token_events[-1])
         if aligned:
             feed_weights = copy_blocks(
                 packet_plan(

time: 974 us -> 949 us (0.974)
  starting transfers between devices: 112 us -> 87.9 us
    ppermute x79, starting transfers between devices: 112 us -> 87.9 us  [hop(): lax.ppermute(value, axis, [(i, i ^ mask) for i in range(sizes[axis])])]
  transfers between devices with their start and end apart: 79 -> 79, of which waited for: 39 -> 38; matrix products, arithmetic and copies ran while one was open for 23% -> 24% of each run, Pallas kernels for 5% -> 5%
where the time goes in v3:
time: 949 us; the launch traced here: 940 us
  waiting for transfers between devices  498 us (52%)
  other arithmetic  115 us (12%)
  local copies, waits for them, and re-layouts  109 us (11%)
  starting transfers between devices  87.9 us (9%)
  Pallas kernels  76.4 us (8%)
  matrix products  49 us (5%)
    ppermute x79, waiting for transfers between devices, hop(): lax.ppermute(value, axis, [(i, i ^ mask) for i in range(sizes[axis])])  498 us
    ppermute x79, starting transfers between devices, hop(): lax.ppermute(value, axis, [(i, i ^ mask) for i in range(sizes[axis])])  87.9 us
    pallas_call x3, Pallas kernels, feed_forward(): pl.pallas_call(functools.partial(feed_kernel, count, half, len(kept), n_c...  67.4 us
    unnamed x350, local copies, waits for them, and re-layouts  47.6 us
    dynamic_update_slice x26, other arithmetic, local(): lax.dynamic_update_slice_in_dim(wide_mlp[i], parts[i].astype(wider), peer...  32.1 us
    dot_general x12, matrix products, rows_contract(): lax.dot_general(former, latter, (((0,), (0,)), ((), ())), preferred_eleme...  30.6 us
  transfers between devices with their start and end apart: 79, of which 38 were waited for; matrix products, arithmetic and copies ran while one was open for 24% of the time, Pallas kernels for 5%

profile of v3, /device:TPU:0, one launch (start us, length us, event | category | flops | bytes accessed | tf_op | source)
XLA Modules:
  0.0 939.7 jit_solution(12457734800952673637)
XLA Ops:
  3.9 3.0 collective-permute-start.10
  10.6 2.6 collective-permute-start.2
  28.8 3.4 pack_weights.1
  38.8 2.7 collective-permute-start.11
  49.5 8.2 collective-permute-done.11
  57.9 8.6 collective-permute-done.8
  68.0 14.3 %collective-permute-done.13 = bf16[384,512]{1,0:T(8,128)(2,1)S(1)} collective-permute-done((bf16[384,512]{1,0:T(8,128)(2,1)S(1)}, bf16[384,512]{1,0:T(8,128)(2,1)S(1)}, u32[]{:S(2)}, u32[]{:S(2)}) %collective-permute-start.13) | collective-permute-done | bytes 393248 | tf_op jit(solution)/shard_map/ppermute | solution.py:199
  82.5 3.8 collective-permute-start.14
  89.7 21.6 %collective-permute-done.14 = bf16[2,384,512]{2,1,0:T(8,128)(2,1)S(1)} collective-permute-done((bf16[2,384,512]{2,1,0:T(8,128)(2,1)S(1)}, bf16[2,384,512]{2,1,0:T(8,128)(2,1)S(1)}, u32[]{:S(2)}, u32[]{:S(2)}) %collective-permute-start.14) | collective-permute-done | bytes 786464 | tf_op jit(solution)/shard_map/ppermute | solution.py:199
  120.1 26.1 %collective-permute-done.15 = bf16[2,2,384,512]{3,2,0,1:T(8,128)(2,1)S(1)} collective-permute-done((bf16[2,2,384,512]{3,2,0,1:T(8,128)(2,1)S(1)}, bf16[2,2,384,512]{3,2,0,1:T(8,128)(2,1)S(1)}, u32[]{:S(2)}, u32[]{:S(2)}) %collective-permute-start.15) | collective-permute-done | bytes 1572896 | tf_op jit(solution)/shard_map/ppermute | solution.py:199
  174.8 2.5 pad_maximum_fusion.3
  179.4 5.0 collective-permute-done.20
  188.6 10.1 %collective-permute-done.21.refs_6_ = bf16[896,512]{1,0:T(8,128)(2,1)S(1)} collective-permute-done((bf16[896,512]{1,0:T(8,128)(2,1)}, bf16[896,512]{1,0:T(8,128)(2,1)S(1)}, u32[]{:S(2)}, u32[]{:S(2)}) %collective-permute-start.21) | collective-permute-done | bytes 917536 | tf_op jit(solution)/shard_map/ppermute | solution.py:199
  198.7 17.9 %collective-permute-done.22.refs_2_ = bf16[896,512]{1,0:T(8,128)(2,1)} collective-permute-done((bf16[896,512]{1,0:T(8,128)(2,1)}, bf16[896,512]{1,0:T(8,128)(2,1)}, u32[]{:S(2)}, u32[]{:S(2)}) %collective-permute-start.22) | collective-permute-done | bytes 917536 | tf_op jit(solution)/shard_map/ppermute | solution.py:199
  221.5 2.7 constant_dynamic-update-slice_fusion.10
  224.2 11.8 %collective-permute-done.23 = bf16[64,3072]{1,0:T(8,128)(2,1)S(1)} collective-permute-done((bf16[64,3072]{1,0:T(8,128)(2,1)S(1)}, bf16[64,3072]{1,0:T(8,128)(2,1)S(1)}, u32[]{:S(2)}, u32[]{:S(2)}) %collective-permute-start.23) | collective-permute-done | bytes 393248 | tf_op jit(solution)/shard_map/ppermute | solution.py:199
  236.2 2.8 constant_dynamic-update-slice_fusion.9
  240.6 14.5 %collective-permute-done.24 = bf16[128,3072]{1,0:T(8,128)(2,1)S(1)} collective-permute-done((bf16[128,3072]{1,0:T(8,128)(2,1)S(1)}, bf16[128,3072]{1,0:T(8,128)(2,1)S(1)}, u32[]{:S(2)}, u32[]{:S(2)}) %collective-permute-start.24) | collective-permute-done | bytes 786464 | tf_op jit(solution)/shard_map/ppermute | solution.py:199
  259.5 31.6 %collective-permute-done.25.refs_1_ = bf16[256,3072]{1,0:T(8,128)(2,1)S(1)} collective-permute-done((bf16[256,3072]{1,0:T(8,128)(2,1)S(1)}, bf16[256,3072]{1,0:T(8,128)(2,1)S(1)}, u32[]{:S(2)}, u32[]{:S(2)}) %collective-permute-start.25) | collective-permute-done | bytes 1572896 | tf_op jit(solution)/shard_map/ppermute | solution.py:199
  292.5 3.3 collective-permute-done.26.refs_2_
  300.4 20.6 %collective-permute-done.31.refs_3_ = bf16[896,512]{1,0:T(8,128)(2,1)S(1)} collective-permute-done((bf16[896,512]{1,0:T(8,128)(2,1)S(1)}, bf16[896,512]{1,0:T(8,128)(2,1)S(1)}, u32[]{:S(2)}, u32[]{:S(2)}) %collective-permute-start.31) | collective-permute-done | bytes 917536 | tf_op jit(solution)/shard_map/ppermute | solution.py:199
  321.0 2.6 collective-permute-start.33
  325.2 32.4 %collective-permute-done.37 = bf16[128,3072]{1,0:T(8,128)(2,1)S(1)} collective-permute-done((bf16[128,3072]{1,0:T(8,128)(2,1)S(1)}, bf16[128,3072]{1,0:T(8,128)(2,1)S(1)}, u32[]{:S(2)}, u32[]{:S(2)}) %collective-permute-start.37) | collective-permute-done | bytes 786464 | tf_op jit(solution)/shard_map/ppermute | solution.py:199
  359.4 17.6 %collective-permute-done.30.refs_1_ = bf16[896,512]{1,0:T(8,128)(2,1)S(1)} collective-permute-done((bf16[896,512]{1,0:T(8,128)(2,1)S(1)}, bf16[896,512]{1,0:T(8,128)(2,1)S(1)}, u32[]{:S(2)}, u32[]{:S(2)}) %collective-permute-start.30) | collective-permute-done | bytes 917536 | tf_op jit(solution)/shard_map/ppermute | solution.py:199
  377.1 25.5 %collective-permute-done.32.refs_5_ = bf16[896,512]{1,0:T(8,128)(2,1)S(1)} collective-permute-done((bf16[896,512]{1,0:T(8,128)(2,1)S(1)}, bf16[896,512]{1,0:T(8,128)(2,1)S(1)}, u32[]{:S(2)}, u32[]{:S(2)}) %collective-permute-start.32) | collective-permute-done | bytes 917536 | tf_op jit(solution)/shard_map/ppermute | solution.py:199
  402.6 2.4 unpack_weights.1
  408.4 22.9 %feed_forward.3 = (bf16[2048,2048]{1,0:T(8,128)(2,1)}, bf16[2048,1024]{1,0:T(8,128)(2,1)}, bf16[2048,2048]{1,0:T(8,128)(2,1)}, bf16[2048,1024]{1,0:T(8,128)(2,1)...) custom-call(bf16[256,3072]{1,0:T(8,128)(2,1)} %copy-done.128, ...), custom_call_target="tpu_custom_call" | custom-call | flops 10871635968 | bytes 28311552 | tf_op jit(solution)/shard_map/feed_forward/pallas_call | solution.py:157
  431.2 2.6 copy-done.16
  433.8 18.6 %feed_forward.4 = (bf16[2048,2048]{1,0:T(8,128)(2,1)}, bf16[2048,1024]{1,0:T(8,128)(2,1)}, bf16[2048,2048]{1,0:T(8,128)(2,1)}, bf16[2048,1024]{1,0:T(8,128)(2,1)...) custom-call(bf16[256,3072]{1,0:T(8,128)(2,1)} %constant_dynamic-upda, ...), custom_call_target="tpu_custom_call", output_to_operand_aliasing={{0}: (8, {}), {1}: (9, {}), {2}: (10, {}), {3}: (11, {}), {... | custom-call | flops 7247757312 | bytes 18874368 | tf_op jit(solution)/shard_map/feed_forward/pallas_call | solution.py:157
  452.4 26.0 %feed_forward.5 = (bf16[2048,2048]{1,0:T(8,128)(2,1)}, bf16[2048,1024]{1,0:T(8,128)(2,1)}, bf16[2048,2048]{1,0:T(8,128)(2,1)}, bf16[2048,1024]{1,0:T(8,128)(2,1)...) custom-call(bf16[768,3072]{1,0:T(8,128)(2,1)} %collective-permute-do, ...), custom_call_target="tpu_custom_call", output_to_operand_aliasing={{0}: (10, {}), {1}: (11, {}), {2}: (12, {}), {3}: (13, {}),... | custom-call | flops 10871635968 | bytes 28311552 | tf_op jit(solution)/shard_map/feed_forward/pallas_call | solution.py:157
  479.2 9.1 collective-permute-done.40
  493.9 9.6 %fusion.119 = (bf16[768,3072]{1,0:T(8,128)(2,1)S(1)}, f32[768,3072]{1,0:T(8,128)}) fusion(bf16[768,3072]{1,0:T(8,128)(2,1)} %copy-done.41, bf16[768,3072]{1,0:T(8,128)(2,1)} %get-tuple-element.135), kind=kLoop, calls=%fused_computation.409 | loop fusion | flops 9437184 | bytes 23592960 | tf_op jit(solution)/shard_map/convert.33
  503.5 6.6 collective-permute-done.41
  511.9 2.7 fusion.24
  517.0 33.7 %collective-permute-done.44 = bf16[256,3072]{1,0:T(8,128)(2,1)S(1)} collective-permute-done((bf16[256,3072]{1,0:T(8,128)(2,1)S(1)}, bf16[256,3072]{1,0:T(8,128)(2,1)S(1)}, u32[]{:S(2)}, u32[]{:S(2)}) %collective-permute-start.44) | collective-permute-done | bytes 1572896 | tf_op jit(solution)/shard_map/ppermute | solution.py:199
  551.2 2.6 fusion.5
  560.2 2.5 copy.107
  563.3 2.7 slice.574
  566.0 7.8 collective-permute-done.45
  576.9 8.3 convolution_convert_fusion.3.refs_1_
  585.2 7.8 collective-permute-done.46
  593.8 9.6 %convolution_convert_fusion.refs_0_ = bf16[2048,1024]{1,0:T(8,128)(2,1)S(1)} fusion(bf16[2048,2048]{1,0:T(8,128)(2,1)S(1)} %bitcast.310, bf16[2048,1024]{1,0:T(8,128)(2,1)S(1)} %copy-done.24), kind=kOutput, calls=%fused_computation.6 | convolution fusion | flops 8592031744 | bytes 16777216 | tf_op jit(solution)/shard_map/dot_general | solution.py:33
  607.0 3.1 pack_gradients.1
  610.2 3.2 collective-permute-start.55
  624.8 5.6 convert_add_fusion
  630.7 27.1 %collective-permute-done.50 = bf16[256,3072]{1,0:T(8,128)(2,1)S(1)} collective-permute-done((bf16[256,3072]{1,0:T(8,128)(2,1)}, bf16[256,3072]{1,0:T(8,128)(2,1)S(1)}, u32[]{:S(2)}, u32[]{:S(2)}) %collective-permute-start.50) | collective-permute-done | bytes 1572896 | tf_op jit(solution)/shard_map/ppermute | solution.py:199
  660.7 12.8 %collective-permute-done.55 = bf16[896,512]{1,0:T(8,128)(2,1)} collective-permute-done((bf16[896,512]{1,0:T(8,128)(2,1)S(1)}, bf16[896,512]{1,0:T(8,128)(2,1)}, u32[]{:S(2)}, u32[]{:S(2)}) %collective-permute-start.55) | collective-permute-done | bytes 917536 | tf_op jit(solution)/shard_map/ppermute | solution.py:199
  678.6 17.8 %collective-permute-start.76 = (bf16[896,512]{1,0:T(8,128)(2,1)S(1)}, bf16[896,512]{1,0:T(8,128)(2,1)}, u32[]{:S(2)}, u32[]{:S(2)}) collective-permute-start(bf16[896,512]{1,0:T(8,128)(2,1)S(1)} %get-tuple-element.158), channel_id=1, source_target_pairs={{0,20},{4,16},{8,28},{12,24},{16,4},{20,0},{24,12},{28,8},{1,21},{... | collective-permute-start | bytes 2752520 | tf_op jit(solution)/shard_map/ppermute | solution.py:199
  703.2 14.0 %collective-permute-done.74 = bf16[896,512]{1,0:T(8,128)(2,1)} collective-permute-done((bf16[896,512]{1,0:T(8,128)(2,1)}, bf16[896,512]{1,0:T(8,128)(2,1)}, u32[]{:S(2)}, u32[]{:S(2)}) %collective-permute-start.74) | collective-permute-done | bytes 917536 | tf_op jit(solution)/shard_map/ppermute | solution.py:199
  718.2 18.4 %collective-permute-done.76 = bf16[896,512]{1,0:T(8,128)(2,1)} collective-permute-done((bf16[896,512]{1,0:T(8,128)(2,1)S(1)}, bf16[896,512]{1,0:T(8,128)(2,1)}, u32[]{:S(2)}, u32[]{:S(2)}) %collective-permute-start.76) | collective-permute-done | bytes 917536 | tf_op jit(solution)/shard_map/ppermute | solution.py:199
  745.3 14.3 %collective-permute-done.53 = bf16[64,3072]{1,0:T(8,128)(2,1)S(1)} collective-permute-done((bf16[64,3072]{1,0:T(8,128)(2,1)S(1)}, bf16[64,3072]{1,0:T(8,128)(2,1)S(1)}, u32[]{:S(2)}, u32[]{:S(2)}) %collective-permute-start.53) | collective-permute-done | bytes 393248 | tf_op jit(solution)/shard_map/ppermute | solution.py:199
  767.3 4.1 collective-permute-done.56
  772.4 2.4 collective-permute-start.75
  774.8 2.9 collective-permute-start.78
  810.8 4.2 copy.122
  815.0 2.5 convolution_convert_fusion.7
  823.9 10.9 %collective-permute-done.78 = bf16[896,512]{1,0:T(8,128)(2,1)} collective-permute-done((bf16[896,512]{1,0:T(8,128)(2,1)S(1)}, bf16[896,512]{1,0:T(8,128)(2,1)}, u32[]{:S(2)}, u32[]{:S(2)}) %collective-permute-start.78) | collective-permute-done | bytes 917536 | tf_op jit(solution)/shard_map/ppermute | solution.py:199
  858.1 2.4 collective-permute-start.61
  864.6 10.8 %collective-permute-done.61 = bf16[2,384,256]{2,1,0:T(8,128)(2,1)S(1)} collective-permute-done((bf16[2,384,256]{2,1,0:T(8,128)(2,1)S(1)}, bf16[2,384,256]{2,1,0:T(8,128)(2,1)S(1)}, u32[]{:S(2)}, u32[]{:S(2)}) %collective-permute-start.61) | collective-permute-done | bytes 393248 | tf_op jit(solution)/shard_map/ppermute | solution.py:199
  875.6 11.8 %collective-permute-done.64 = bf16[2,384,256]{2,1,0:T(8,128)(2,1)S(1)} collective-permute-done((bf16[2,384,256]{2,1,0:T(8,128)(2,1)S(1)}, bf16[2,384,256]{2,1,0:T(8,128)(2,1)S(1)}, u32[]{:S(2)}, u32[]{:S(2)}) %collective-permute-start.64) | collective-permute-done | bytes 393248 | tf_op jit(solution)/shard_map/ppermute | solution.py:199
  894.1 12.9 %collective-permute-done.72 = bf16[2,384,512]{1,2,0:T(8,128)(2,1)S(1)} collective-permute-done((bf16[2,384,512]{1,2,0:T(8,128)(2,1)S(1)}, bf16[2,384,512]{1,2,0:T(8,128)(2,1)S(1)}, u32[]{:S(2)}, u32[]{:S(2)}) %collective-permute-start.72) | collective-permute-done | bytes 786464 | tf_op jit(solution)/shard_map/ppermute | solution.py:199
  913.8 8.9 collective-permute-done.73
  923.8 6.0 collective-permute-done.69
  930.7 6.1 collective-permute-done.70
  (725 shorter events, 261.7 us)
Async XLA Ops:
  3.9 33.8 %collective-permute-start.10 = (bf16[384,256]{1,0:T(8,128)(2,1)}, bf16[384,256]{1,0:T(8,128)(2,1)}, u32[]{:S(2)}, u32[]{:S(2)}) collective-permute-start(bf16[384,256]{1,0:T(8,128)(2,1)} %get-tuple-element.276), channel_id=1, source_target_pairs={{0,4},{4,0},{8,12},{12,8},{16,20},{20,16},{24,28},{28,24},{1,5},{5... | collective-permute-start | bytes 589832 | tf_op jit(solution)/shard_map/ppermute | solution.py:199
  8.3 40.0 %collective-permute-start = (bf16[64,3072]{1,0:T(8,128)(2,1)}, bf16[64,3072]{1,0:T(8,128)(2,1)}, u32[]{:S(2)}, u32[]{:S(2)}) collective-permute-start(bf16[64,3072]{1,0:T(8,128)(2,1)} %constant_dynamic-update-slice_fusion), channel_id=1, source_target_pairs={{0,2},{1,3},{2,0},{3,1},{4,6},{5,7},{6,4},{7,5},{8,10},{9,11},{10,... | collective-permute-start | bytes 1179656 | tf_op jit(solution)/shard_map/ppermute | solution.py:199
  10.6 21.8 %collective-permute-start.2 = (bf16[112,512]{1,0:T(8,128)(2,1)}, bf16[112,512]{1,0:T(8,128)(2,1)}, u32[]{:S(2)}, u32[]{:S(2)}) collective-permute-start(bf16[112,512]{1,0:T(8,128)(2,1)} %fusion.94), channel_id=1, source_target_pairs={{0,16},{4,20},{8,24},{12,28},{16,0},{20,4},{24,8},{28,12},{1,17},{... | collective-permute-start | bytes 344072 | tf_op jit(solution)/shard_map/ppermute | solution.py:199
  13.1 30.5 %collective-permute-start.7 = (bf16[384,256]{1,0:T(8,128)(2,1)}, bf16[384,256]{1,0:T(8,128)(2,1)}, u32[]{:S(2)}, u32[]{:S(2)}) collective-permute-start(bf16[384,256]{1,0:T(8,128)(2,1)} %get-tuple-element.277), channel_id=1, source_target_pairs={{0,16},{4,20},{8,24},{12,28},{16,0},{20,4},{24,8},{28,12},{1,17},{... | collective-permute-start | bytes 589832 | tf_op jit(solution)/shard_map/ppermute | solution.py:199
  38.8 18.9 %collective-permute-start.11 = (bf16[2,384,256]{2,1,0:T(8,128)(2,1)S(1)}, bf16[2,384,256]{2,1,0:T(8,128)(2,1)S(1)}, u32[]{:S(2)}, u32[]{:S(2)}) collective-permute-start(bf16[2,384,256]{2,1,0:T(8,128)(2,1)S(1)} %maximum_select_fusion.16), channel_id=1, source_target_pairs={{0,16},{4,20},{8,24},{12,28},{16,0},{20,4},{24,8},{28,12},{1,17},{... | collective-permute-start | bytes 1179656 | tf_op jit(solution)/shard_map/ppermute | solution.py:199
  44.8 21.7 %collective-permute-start.8 = (bf16[2,384,256]{2,1,0:T(8,128)(2,1)S(1)}, bf16[2,384,256]{2,1,0:T(8,128)(2,1)S(1)}, u32[]{:S(2)}, u32[]{:S(2)}) collective-permute-start(bf16[2,384,256]{2,1,0:T(8,128)(2,1)S(1)} %maximum_select_fusion.15), channel_id=1, source_target_pairs={{0,8},{4,12},{8,0},{12,4},{16,24},{20,28},{24,16},{28,20},{1,9},{5... | collective-permute-start | bytes 1179656 | tf_op jit(solution)/shard_map/ppermute | solution.py:199
  47.6 19.5 %collective-permute-start.4 = (bf16[2,2,112,512]{3,2,1,0:T(8,128)(2,1)S(1)}, bf16[2,2,112,512]{3,2,1,0:T(8,128)(2,1)S(1)}, u32[]{:S(2)}, u32[]{:S(2)}) collective-permute-start(bf16[2,2,112,512]{3,2,1,0:T(8,128)(2,1)S(1)} %maximum_select_fusion.14), channel_id=1, source_target_pairs={{0,4},{4,0},{8,12},{12,8},{16,20},{20,16},{24,28},{28,24},{1,5},{5... | collective-permute-start | bytes 1376264 | tf_op jit(solution)/shard_map/ppermute | solution.py:199
  49.5 37.1 %collective-permute-start.1 = (bf16[128,3072]{1,0:T(8,128)(2,1)S(1)}, bf16[128,3072]{1,0:T(8,128)(2,1)S(1)}, u32[]{:S(2)}, u32[]{:S(2)}) collective-permute-start(bf16[128,3072]{1,0:T(8,128)(2,1)S(1)} %pad_maximum_fusion.9), channel_id=1, source_target_pairs={{0,1},{1,0},{2,3},{3,2},{4,5},{5,4},{6,7},{7,6},{8,9},{9,8},{10,11... | collective-permute-start | bytes 2359304 | tf_op jit(solution)/shard_map/ppermute | solution.py:199
  57.9 56.4 %collective-permute-start.12 = (bf16[2,2,384,256]{3,2,1,0:T(8,128)(2,1)S(1)}, bf16[2,2,384,256]{3,2,1,0:T(8,128)(2,1)S(1)}, u32[]{:S(2)}, u32[]{:S(2)}) collective-permute-start(bf16[2,2,384,256]{3,2,1,0:T(8,128)(2,1)S(1)} %maximum_select_fusion.11), channel_id=1, source_target_pairs={{0,8},{4,12},{8,0},{12,4},{16,24},{20,28},{24,16},{28,20},{1,9},{5... | collective-permute-start | bytes 2359304 | tf_op jit(solution)/shard_map/ppermute | solution.py:199
  66.6 50.9 %collective-permute-start.9 = (bf16[2,2,384,256]{3,2,0,1:T(8,128)(2,1)S(1)}, bf16[2,2,384,256]{3,2,0,1:T(8,128)(2,1)S(1)}, u32[]{:S(2)}, u32[]{:S(2)}) collective-permute-start(bf16[2,2,384,256]{3,2,0,1:T(8,128)(2,1)S(1)} %maximum_select_fusion.9), channel_id=1, source_target_pairs={{0,4},{4,0},{8,12},{12,8},{16,20},{20,16},{24,28},{28,24},{1,5},{5... | collective-permute-start | bytes 2359304 | tf_op jit(solution)/shard_map/ppermute | solution.py:199
  67.1 22.2 %collective-permute-start.5 = (bf16[2,2,2,112,512]{4,3,2,1,0:T(8,128)(2,1)S(1)}, bf16[2,2,2,112,512]{4,3,2,1,0:T(8,128)(2,1)S(1)}, u32[]{:S(2)}, u32[]{:S(2)}) collective-permute-start(bf16[2,2,2,112,512]{4,3,2,1,0:T(8,128)(2,1)S(1)} %maximum_select_fusion.8), channel_id=1, source_target_pairs={{0,2},{1,3},{2,0},{3,1},{4,6},{5,7},{6,4},{7,5},{8,10},{9,11},{10,... | collective-permute-start | bytes 2752520 | tf_op jit(solution)/shard_map/ppermute | solution.py:199
  82.5 28.9 %collective-permute-start.14 = (bf16[2,384,512]{2,1,0:T(8,128)(2,1)S(1)}, bf16[2,384,512]{2,1,0:T(8,128)(2,1)S(1)}, u32[]{:S(2)}, u32[]{:S(2)}) collective-permute-start(bf16[2,384,512]{2,1,0:T(8,128)(2,1)S(1)} %maximum_select_fusion.13), channel_id=1, source_target_pairs={{0,8},{4,12},{8,0},{12,4},{16,24},{20,28},{24,16},{28,20},{1,9},{5... | collective-permute-start | bytes 2359304 | tf_op jit(solution)/shard_map/ppermute | solution.py:199
  86.6 25.9 %collective-permute-start.17 = (bf16[64,3072]{1,0:T(8,128)(2,1)S(1)}, bf16[64,3072]{1,0:T(8,128)(2,1)S(1)}, u32[]{:S(2)}, u32[]{:S(2)}) collective-permute-start(bf16[64,3072]{1,0:T(8,128)(2,1)S(1)} %get-tuple-element.98), channel_id=1, source_target_pairs={{0,16},{4,20},{8,24},{12,28},{16,0},{20,4},{24,8},{28,12},{1,17},{... | collective-permute-start | bytes 1179656 | tf_op jit(solution)/shard_map/ppermute | solution.py:199
  89.6 59.1 %collective-permute-start.6 = (bf16[2,2,2,2,112,512]{5,4,2,1,0,3:T(8,128)(2,1)S(1)}, bf16[2,2,2,2,112,512]{5,4,2,1,0,3:T(8,128)(2,1)S(1)}, u32[]{:S(2)}, u32[]{:S(2)}) collective-permute-start(bf16[2,2,2,2,112,512]{5,4,2,1,0,3:T(8,128)(2,1)S(1)} %maximum_select_fusion.2), channel_id=1, source_target_pairs={{0,1},{1,0},{2,3},{3,2},{4,5},{5,4},{6,7},{7,6},{8,9},{9,8},{10,11... | collective-permute-start | bytes 5505032 | tf_op jit(solution)/shard_map/ppermute | solution.py:199
  111.6 34.7 %collective-permute-start.15 = (bf16[2,2,384,512]{3,2,0,1:T(8,128)(2,1)S(1)}, bf16[2,2,384,512]{3,2,0,1:T(8,128)(2,1)S(1)}, u32[]{:S(2)}, u32[]{:S(2)}) collective-permute-start(bf16[2,2,384,512]{3,2,0,1:T(8,128)(2,1)S(1)} %maximum_select_fusion.6), channel_id=1, source_target_pairs={{0,4},{4,0},{8,12},{12,8},{16,20},{20,16},{24,28},{28,24},{1,5},{5... | collective-permute-start | bytes 4718600 | tf_op jit(solution)/shard_map/ppermute | solution.py:199
  112.5 56.1 %collective-permute-start.16 = (bf16[896,512]{1,0:T(8,128)(2,1)}, bf16[896,512]{1,0:T(8,128)(2,1)S(1)}, u32[]{:S(2)}, u32[]{:S(2)}) collective-permute-start(bf16[896,512]{1,0:T(8,128)(2,1)} %get-tuple-element.97), channel_id=1, source_target_pairs={{0,16},{4,20},{8,24},{12,28},{16,0},{20,4},{24,8},{28,12},{1,17},{... | collective-permute-start | bytes 2752520 | tf_op jit(solution)/shard_map/ppermute | solution.py:199
  114.3 54.4 %collective-permute-start.18 = (bf16[128,3072]{1,0:T(8,128)(2,1)}, bf16[128,3072]{1,0:T(8,128)(2,1)}, u32[]{:S(2)}, u32[]{:S(2)}) collective-permute-start(bf16[128,3072]{1,0:T(8,128)(2,1)} %pad_maximum_fusion.10), channel_id=1, source_target_pairs={{0,8},{4,12},{8,0},{12,4},{16,24},{20,28},{24,16},{28,20},{1,9},{5... | collective-permute-start | bytes 2359304 | tf_op jit(solution)/shard_map/ppermute | solution.py:199
  173.5 25.2 %collective-permute-start.21 = (bf16[896,512]{1,0:T(8,128)(2,1)}, bf16[896,512]{1,0:T(8,128)(2,1)S(1)}, u32[]{:S(2)}, u32[]{:S(2)}) collective-permute-start(bf16[896,512]{1,0:T(8,128)(2,1)} %get-tuple-element.101), channel_id=1, source_target_pairs={{0,24},{4,28},{8,16},{12,20},{16,8},{20,12},{24,0},{28,4},{1,25},{... | collective-permute-start | bytes 2752520 | tf_op jit(solution)/shard_map/ppermute | solution.py:199
  174.8 41.8 %collective-permute-start.22 = (bf16[896,512]{1,0:T(8,128)(2,1)}, bf16[896,512]{1,0:T(8,128)(2,1)}, u32[]{:S(2)}, u32[]{:S(2)}) collective-permute-start(bf16[896,512]{1,0:T(8,128)(2,1)} %get-tuple-element.103), channel_id=1, source_target_pairs={{0,8},{4,12},{8,0},{12,4},{16,24},{20,28},{24,16},{28,20},{1,9},{5... | collective-permute-start | bytes 2752520 | tf_op jit(solution)/shard_map/ppermute | solution.py:199
  177.3 44.3 %collective-permute-start.27 = (bf16[256,3072]{1,0:T(8,128)(2,1)}, bf16[256,3072]{1,0:T(8,128)(2,1)}, u32[]{:S(2)}, u32[]{:S(2)}) collective-permute-start(bf16[256,3072]{1,0:T(8,128)(2,1)} %pad_maximum_fusion.3), channel_id=1, source_target_pairs={{0,2},{1,3},{2,0},{3,1},{4,6},{5,7},{6,4},{7,5},{8,10},{9,11},{10,... | collective-permute-start | bytes 4718600 | tf_op jit(solution)/shard_map/ppermute | solution.py:199
  178.8 41.3 %collective-permute-start.28 = (bf16[256,3072]{1,0:T(8,128)(2,1)}, bf16[256,3072]{1,0:T(8,128)(2,1)}, u32[]{:S(2)}, u32[]{:S(2)}) collective-permute-start(bf16[256,3072]{1,0:T(8,128)(2,1)} %pad_maximum_fusion.3), channel_id=1, source_target_pairs={{0,4},{4,0},{8,12},{12,8},{16,20},{20,16},{24,28},{28,24},{1,5},{5... | collective-permute-start | bytes 4718600 | tf_op jit(solution)/shard_map/ppermute | solution.py:199
  216.6 19.5 %collective-permute-start.23 = (bf16[64,3072]{1,0:T(8,128)(2,1)S(1)}, bf16[64,3072]{1,0:T(8,128)(2,1)S(1)}, u32[]{:S(2)}, u32[]{:S(2)}) collective-permute-start(bf16[64,3072]{1,0:T(8,128)(2,1)S(1)} %pad_maximum_fusion.18), channel_id=1, source_target_pairs={{0,16},{4,20},{8,24},{12,28},{16,0},{20,4},{24,8},{28,12},{1,17},{... | collective-permute-start | bytes 1179656 | tf_op jit(solution)/shard_map/ppermute | solution.py:199
  220.0 37.7 %collective-permute-start.29 = (bf16[256,3072]{1,0:T(8,128)(2,1)}, bf16[256,3072]{1,0:T(8,128)(2,1)S(1)}, u32[]{:S(2)}, u32[]{:S(2)}) collective-permute-start(bf16[256,3072]{1,0:T(8,128)(2,1)} %collective-permute-done.28), channel_id=1, source_target_pairs={{0,2},{1,3},{2,0},{3,1},{4,6},{5,7},{6,4},{7,5},{8,10},{9,11},{10,... | collective-permute-start | bytes 4718600 | tf_op jit(solution)/shard_map/ppermute | solution.py:199
  236.1 19.0 %collective-permute-start.24 = (bf16[128,3072]{1,0:T(8,128)(2,1)S(1)}, bf16[128,3072]{1,0:T(8,128)(2,1)S(1)}, u32[]{:S(2)}, u32[]{:S(2)}) collective-permute-start(bf16[128,3072]{1,0:T(8,128)(2,1)S(1)} %pad_maximum_fusion.11), channel_id=1, source_target_pairs={{0,8},{4,12},{8,0},{12,4},{16,24},{20,28},{24,16},{28,20},{1,9},{5... | collective-permute-start | bytes 2359304 | tf_op jit(solution)/shard_map/ppermute | solution.py:199
  256.3 34.9 %collective-permute-start.25 = (bf16[256,3072]{1,0:T(8,128)(2,1)S(1)}, bf16[256,3072]{1,0:T(8,128)(2,1)S(1)}, u32[]{:S(2)}, u32[]{:S(2)}) collective-permute-start(bf16[256,3072]{1,0:T(8,128)(2,1)S(1)} %get-tuple-element.256.refs_0_), channel_id=1, source_target_pairs={{0,2},{1,3},{2,0},{3,1},{4,6},{5,7},{6,4},{7,5},{8,10},{9,11},{10,... | collective-permute-start | bytes 4718600 | tf_op jit(solution)/shard_map/ppermute | solution.py:199
  259.0 172.2 %collective-permute-start.35 = (bf16[1024,3072]{1,0:T(8,128)(2,1)}, bf16[1024,3072]{1,0:T(8,128)(2,1)S(1)}, u32[]{:S(2)}, u32[]{:S(2)}) collective-permute-start(bf16[1024,3072]{1,0:T(8,128)(2,1)} %constant_dynamic-update-slice_fusion.8.refs_3_.refs_4_.refs_5_.refs_2_), channel_id=1, source_target_pairs={{0,1},{1,0},{2,3},{3,2},{4,5},{5,4},{6,7},{7,6},{8,9},{9,8},{10,11... | collective-permute-start | bytes 18874376 | tf_op jit(solution)/shard_map/ppermute | solution.py:199
  259.0 36.8 %collective-permute-start.26 = (bf16[256,3072]{1,0:T(8,128)(2,1)S(1)}, bf16[256,3072]{1,0:T(8,128)(2,1)S(1)}, u32[]{:S(2)}, u32[]{:S(2)}) collective-permute-start(bf16[256,3072]{1,0:T(8,128)(2,1)S(1)} %get-tuple-element.256.refs_0_), channel_id=1, source_target_pairs={{0,4},{4,0},{8,12},{12,8},{16,20},{20,16},{24,28},{28,24},{1,5},{5... | collective-permute-start | bytes 4718600 | tf_op jit(solution)/shard_map/ppermute | solution.py:199
  297.2 155.2 %collective-permute-start.34 = (bf16[768,3072]{1,0:T(8,128)(2,1)}, bf16[768,3072]{1,0:T(8,128)(2,1)}, u32[]{:S(2)}, u32[]{:S(2)}) collective-permute-start(bf16[768,3072]{1,0:T(8,128)(2,1)} %constant_dynamic-update-slice_fusion.14), channel_id=1, source_target_pairs={{0,1},{1,0},{2,3},{3,2},{4,5},{5,4},{6,7},{7,6},{8,9},{9,8},{10,11... | collective-permute-start | bytes 14155784 | tf_op jit(solution)/shard_map/ppermute | solution.py:199
  297.3 23.8 %collective-permute-start.31 = (bf16[896,512]{1,0:T(8,128)(2,1)S(1)}, bf16[896,512]{1,0:T(8,128)(2,1)S(1)}, u32[]{:S(2)}, u32[]{:S(2)}) collective-permute-start(bf16[896,512]{1,0:T(8,128)(2,1)S(1)} %copy-done.15), channel_id=1, source_target_pairs={{0,12},{4,8},{8,4},{12,0},{16,28},{20,24},{24,20},{28,16},{1,13},{... | collective-permute-start | bytes 2752520 | tf_op jit(solution)/shard_map/ppermute | solution.py:199
  297.6 26.0 %collective-permute-start.36 = (bf16[128,3072]{1,0:T(8,128)(2,1)S(1)}, bf16[128,3072]{1,0:T(8,128)(2,1)S(1)}, u32[]{:S(2)}, u32[]{:S(2)}) collective-permute-start(bf16[128,3072]{1,0:T(8,128)(2,1)S(1)} %slice.704), channel_id=1, source_target_pairs={{0,2},{1,3},{2,0},{3,1},{4,6},{5,7},{6,4},{7,5},{8,10},{9,11},{10,... | collective-permute-start | bytes 2359304 | tf_op jit(solution)/shard_map/ppermute | solution.py:199
  298.8 58.7 %collective-permute-start.37 = (bf16[128,3072]{1,0:T(8,128)(2,1)S(1)}, bf16[128,3072]{1,0:T(8,128)(2,1)S(1)}, u32[]{:S(2)}, u32[]{:S(2)}) collective-permute-start(bf16[128,3072]{1,0:T(8,128)(2,1)S(1)} %slice.705), channel_id=1, source_target_pairs={{0,4},{4,0},{8,12},{12,8},{16,20},{20,16},{24,28},{28,24},{1,5},{5... | collective-permute-start | bytes 2359304 | tf_op jit(solution)/shard_map/ppermute | solution.py:199
  321.0 38.4 %collective-permute-start.33 = (bf16[896,512]{1,0:T(8,128)(2,1)S(1)}, bf16[896,512]{1,0:T(8,128)(2,1)S(1)}, u32[]{:S(2)}, u32[]{:S(2)}) collective-permute-start(bf16[896,512]{1,0:T(8,128)(2,1)S(1)} %copy-done.13), channel_id=1, source_target_pairs={{0,28},{4,24},{8,20},{12,16},{16,12},{20,8},{24,4},{28,0},{1,29},{... | collective-permute-start | bytes 2752520 | tf_op jit(solution)/shard_map/ppermute | solution.py:199
  323.6 53.5 %collective-permute-start.30 = (bf16[896,512]{1,0:T(8,128)(2,1)S(1)}, bf16[896,512]{1,0:T(8,128)(2,1)S(1)}, u32[]{:S(2)}, u32[]{:S(2)}) collective-permute-start(bf16[896,512]{1,0:T(8,128)(2,1)S(1)} %copy-done.11), channel_id=1, source_target_pairs={{0,4},{4,0},{8,12},{12,8},{16,20},{20,16},{24,28},{28,24},{1,5},{5... | collective-permute-start | bytes 2752520 | tf_op jit(solution)/shard_map/ppermute | solution.py:199
  357.5 45.0 %collective-permute-start.32 = (bf16[896,512]{1,0:T(8,128)(2,1)S(1)}, bf16[896,512]{1,0:T(8,128)(2,1)S(1)}, u32[]{:S(2)}, u32[]{:S(2)}) collective-permute-start(bf16[896,512]{1,0:T(8,128)(2,1)S(1)} %copy-done.9), channel_id=1, source_target_pairs={{0,20},{4,16},{8,28},{12,24},{16,4},{20,0},{24,12},{28,8},{1,21},{... | collective-permute-start | bytes 2752520 | tf_op jit(solution)/shard_map/ppermute | solution.py:199
  359.4 71.8 %collective-permute-start.38 = (bf16[256,3072]{1,0:T(8,128)(2,1)}, bf16[256,3072]{1,0:T(8,128)(2,1)}, u32[]{:S(2)}, u32[]{:S(2)}) collective-permute-start(bf16[256,3072]{1,0:T(8,128)(2,1)} %constant_dynamic-update-slice_fusion.19.refs_0_), channel_id=1, source_target_pairs={{0,1},{1,0},{2,3},{3,2},{4,5},{5,4},{6,7},{7,6},{8,9},{9,8},{10,11... | collective-permute-start | bytes 4718600 | tf_op jit(solution)/shard_map/ppermute | solution.py:199
  490.1 20.0 %collective-permute-start.41 = (bf16[128,3072]{1,0:T(8,128)(2,1)}, bf16[128,3072]{1,0:T(8,128)(2,1)S(1)}, u32[]{:S(2)}, u32[]{:S(2)}) collective-permute-start(bf16[128,3072]{1,0:T(8,128)(2,1)} %get-tuple-element.197), channel_id=1, source_target_pairs={{0,4},{4,0},{8,12},{12,8},{16,20},{20,16},{24,28},{28,24},{1,5},{5... | collective-permute-start | bytes 2359304 | tf_op jit(solution)/shard_map/ppermute | solution.py:199
  490.7 19.7 %collective-permute-start.43 = (bf16[128,3072]{1,0:T(8,128)(2,1)}, bf16[128,3072]{1,0:T(8,128)(2,1)S(1)}, u32[]{:S(2)}, u32[]{:S(2)}) collective-permute-start(bf16[128,3072]{1,0:T(8,128)(2,1)} %get-tuple-element.198), channel_id=1, source_target_pairs={{0,2},{1,3},{2,0},{3,1},{4,6},{5,7},{6,4},{7,5},{8,10},{9,11},{10,... | collective-permute-start | bytes 2359304 | tf_op jit(solution)/shard_map/ppermute | solution.py:199
  514.8 35.9 %collective-permute-start.44 = (bf16[256,3072]{1,0:T(8,128)(2,1)S(1)}, bf16[256,3072]{1,0:T(8,128)(2,1)S(1)}, u32[]{:S(2)}, u32[]{:S(2)}) collective-permute-start(bf16[256,3072]{1,0:T(8,128)(2,1)S(1)} %pad_maximum_fusion.5), channel_id=1, source_target_pairs={{0,4},{4,0},{8,12},{12,8},{16,20},{20,16},{24,28},{28,24},{1,5},{5... | collective-permute-start | bytes 4718600 | tf_op jit(solution)/shard_map/ppermute | solution.py:199
  515.8 35.4 %collective-permute-start.42 = (bf16[256,3072]{1,0:T(8,128)(2,1)S(1)}, bf16[256,3072]{1,0:T(8,128)(2,1)S(1)}, u32[]{:S(2)}, u32[]{:S(2)}) collective-permute-start(bf16[256,3072]{1,0:T(8,128)(2,1)S(1)} %pad_maximum_fusion.4), channel_id=1, source_target_pairs={{0,2},{1,3},{2,0},{3,1},{4,6},{5,7},{6,4},{7,5},{8,10},{9,11},{10,... | collective-permute-start | bytes 4718600 | tf_op jit(solution)/shard_map/ppermute | solution.py:199
  555.9 17.9 %collective-permute-start.45 = (bf16[128,3072]{1,0:T(8,128)(2,1)}, bf16[128,3072]{1,0:T(8,128)(2,1)}, u32[]{:S(2)}, u32[]{:S(2)}) collective-permute-start(bf16[128,3072]{1,0:T(8,128)(2,1)} %slice.714), channel_id=1, source_target_pairs={{0,8},{4,12},{8,0},{12,4},{16,24},{20,28},{24,16},{28,20},{1,9},{5... | collective-permute-start | bytes 2359304 | tf_op jit(solution)/shard_map/ppermute | solution.py:199
  575.3 17.7 %collective-permute-start.46 = (bf16[64,3072]{1,0:T(8,128)(2,1)S(1)}, bf16[64,3072]{1,0:T(8,128)(2,1)S(1)}, u32[]{:S(2)}, u32[]{:S(2)}) collective-permute-start(bf16[64,3072]{1,0:T(8,128)(2,1)S(1)} %slice.715), channel_id=1, source_target_pairs={{0,16},{4,20},{8,24},{12,28},{16,0},{20,4},{24,8},{28,12},{1,17},{... | collective-permute-start | bytes 1179656 | tf_op jit(solution)/shard_map/ppermute | solution.py:199
  593.0 31.7 %collective-permute-start.47 = (bf16[768,3072]{1,0:T(8,128)(2,1)}, bf16[768,3072]{1,0:T(8,128)(2,1)}, u32[]{:S(2)}, u32[]{:S(2)}) collective-permute-start(bf16[768,3072]{1,0:T(8,128)(2,1)} %get-tuple-element.138), channel_id=1, source_target_pairs={{0,1},{1,0},{2,3},{3,2},{4,5},{5,4},{6,7},{7,6},{8,9},{9,8},{10,11... | collective-permute-start | bytes 14155784 | tf_op jit(solution)/shard_map/ppermute | solution.py:199
  610.1 65.1 %collective-permute-start.54 = (bf16[896,512]{1,0:T(8,128)(2,1)S(1)}, bf16[896,512]{1,0:T(8,128)(2,1)}, u32[]{:S(2)}, u32[]{:S(2)}) collective-permute-start(bf16[896,512]{1,0:T(8,128)(2,1)S(1)} %get-tuple-element.149), channel_id=1, source_target_pairs={{0,16},{4,20},{8,24},{12,28},{16,0},{20,4},{24,8},{28,12},{1,17},{... | collective-permute-start | bytes 2752520 | tf_op jit(solution)/shard_map/ppermute | solution.py:199
  610.2 63.3 %collective-permute-start.55 = (bf16[896,512]{1,0:T(8,128)(2,1)S(1)}, bf16[896,512]{1,0:T(8,128)(2,1)}, u32[]{:S(2)}, u32[]{:S(2)}) collective-permute-start(bf16[896,512]{1,0:T(8,128)(2,1)S(1)} %get-tuple-element.150), channel_id=1, source_target_pairs={{0,8},{4,12},{8,0},{12,4},{16,24},{20,28},{24,16},{28,20},{1,9},{5... | collective-permute-start | bytes 2752520 | tf_op jit(solution)/shard_map/ppermute | solution.py:199
  621.3 36.4 %collective-permute-start.50 = (bf16[256,3072]{1,0:T(8,128)(2,1)}, bf16[256,3072]{1,0:T(8,128)(2,1)S(1)}, u32[]{:S(2)}, u32[]{:S(2)}) collective-permute-start(bf16[256,3072]{1,0:T(8,128)(2,1)} %add_convert_fusion), channel_id=1, source_target_pairs={{0,2},{1,3},{2,0},{3,1},{4,6},{5,7},{6,4},{7,5},{8,10},{9,11},{10,... | collective-permute-start | bytes 4718600 | tf_op jit(solution)/shard_map/ppermute | solution.py:199
  622.8 54.1 %collective-permute-start.77 = (bf16[896,512]{1,0:T(8,128)(2,1)S(1)}, bf16[896,512]{1,0:T(8,128)(2,1)}, u32[]{:S(2)}, u32[]{:S(2)}) collective-permute-start(bf16[896,512]{1,0:T(8,128)(2,1)S(1)} %get-tuple-element.160), channel_id=1, source_target_pairs={{0,24},{4,28},{8,16},{12,20},{16,8},{20,12},{24,0},{28,4},{1,25},{... | collective-permute-start | bytes 2752520 | tf_op jit(solution)/shard_map/ppermute | solution.py:199
  658.2 39.1 %collective-permute-start.51 = (bf16[256,3072]{1,0:T(8,128)(2,1)S(1)}, bf16[256,3072]{1,0:T(8,128)(2,1)S(1)}, u32[]{:S(2)}, u32[]{:S(2)}) collective-permute-start(bf16[256,3072]{1,0:T(8,128)(2,1)S(1)} %fusion.1), channel_id=1, source_target_pairs={{0,4},{4,0},{8,12},{12,8},{16,20},{20,16},{24,28},{28,24},{1,5},{5... | collective-permute-start | bytes 4718600 | tf_op jit(solution)/shard_map/ppermute | solution.py:199
  660.1 37.2 %collective-permute-start.48 = (bf16[256,3072]{1,0:T(8,128)(2,1)S(1)}, bf16[256,3072]{1,0:T(8,128)(2,1)S(1)}, u32[]{:S(2)}, u32[]{:S(2)}) collective-permute-start(bf16[256,3072]{1,0:T(8,128)(2,1)S(1)} %slice.992), channel_id=1, source_target_pairs={{0,2},{1,3},{2,0},{3,1},{4,6},{5,7},{6,4},{7,5},{8,10},{9,11},{10,... | collective-permute-start | bytes 4718600 | tf_op jit(solution)/shard_map/ppermute | solution.py:199
  678.6 38.6 %collective-permute-start.74 = (bf16[896,512]{1,0:T(8,128)(2,1)}, bf16[896,512]{1,0:T(8,128)(2,1)}, u32[]{:S(2)}, u32[]{:S(2)}) collective-permute-start(bf16[896,512]{1,0:T(8,128)(2,1)} %get-tuple-element.154), channel_id=1, source_target_pairs={{0,4},{4,0},{8,12},{12,8},{16,20},{20,16},{24,28},{28,24},{1,5},{5... | collective-permute-start | bytes 2752520 | tf_op jit(solution)/shard_map/ppermute | solution.py:199
  678.6 58.0 %collective-permute-start.76 = (bf16[896,512]{1,0:T(8,128)(2,1)S(1)}, bf16[896,512]{1,0:T(8,128)(2,1)}, u32[]{:S(2)}, u32[]{:S(2)}) collective-permute-start(bf16[896,512]{1,0:T(8,128)(2,1)S(1)} %get-tuple-element.158), channel_id=1, source_target_pairs={{0,20},{4,16},{8,28},{12,24},{16,4},{20,0},{24,12},{28,8},{1,21},{... | collective-permute-start | bytes 2752520 | tf_op jit(solution)/shard_map/ppermute | solution.py:199
  699.1 39.1 %collective-permute-start.52 = (bf16[128,3072]{1,0:T(8,128)(2,1)}, bf16[128,3072]{1,0:T(8,128)(2,1)}, u32[]{:S(2)}, u32[]{:S(2)}) collective-permute-start(bf16[128,3072]{1,0:T(8,128)(2,1)} %slice.720), channel_id=1, source_target_pairs={{0,8},{4,12},{8,0},{12,4},{16,24},{20,28},{24,16},{28,20},{1,9},{5... | collective-permute-start | bytes 2359304 | tf_op jit(solution)/shard_map/ppermute | solution.py:199
  739.9 19.7 %collective-permute-start.53 = (bf16[64,3072]{1,0:T(8,128)(2,1)S(1)}, bf16[64,3072]{1,0:T(8,128)(2,1)S(1)}, u32[]{:S(2)}, u32[]{:S(2)}) collective-permute-start(bf16[64,3072]{1,0:T(8,128)(2,1)S(1)} %slice.722), channel_id=1, source_target_pairs={{0,16},{4,20},{8,24},{12,28},{16,0},{20,4},{24,8},{28,12},{1,17},{... | collective-permute-start | bytes 1179656 | tf_op jit(solution)/shard_map/ppermute | solution.py:199
  772.4 48.6 %collective-permute-start.75 = (bf16[896,512]{1,0:T(8,128)(2,1)S(1)}, bf16[896,512]{1,0:T(8,128)(2,1)}, u32[]{:S(2)}, u32[]{:S(2)}) collective-permute-start(bf16[896,512]{1,0:T(8,128)(2,1)S(1)} %get-tuple-element.156), channel_id=1, source_target_pairs={{0,12},{4,8},{8,4},{12,0},{16,28},{20,24},{24,20},{28,16},{1,13},{... | collective-permute-start | bytes 2752520 | tf_op jit(solution)/shard_map/ppermute | solution.py:199
  774.8 60.0 %collective-permute-start.78 = (bf16[896,512]{1,0:T(8,128)(2,1)S(1)}, bf16[896,512]{1,0:T(8,128)(2,1)}, u32[]{:S(2)}, u32[]{:S(2)}) collective-permute-start(bf16[896,512]{1,0:T(8,128)(2,1)S(1)} %get-tuple-element.162), channel_id=1, source_target_pairs={{0,28},{4,24},{8,20},{12,16},{16,12},{20,8},{24,4},{28,0},{1,29},{... | collective-permute-start | bytes 2752520 | tf_op jit(solution)/shard_map/ppermute | solution.py:199
  797.5 65.3 %collective-permute-start.58 = (bf16[128,3072]{1,0:T(8,128)(2,1)}, bf16[128,3072]{1,0:T(8,128)(2,1)}, u32[]{:S(2)}, u32[]{:S(2)}) collective-permute-start(bf16[128,3072]{1,0:T(8,128)(2,1)} %pad_maximum_fusion.8), channel_id=1, source_target_pairs={{0,1},{1,0},{2,3},{3,2},{4,5},{5,4},{6,7},{7,6},{8,9},{9,8},{10,11... | collective-permute-start | bytes 2359304 | tf_op jit(solution)/shard_map/ppermute | solution.py:199
  799.7 57.0 %collective-permute-start.60 = (bf16[2,2,384,256]{3,2,0,1:T(8,128)(2,1)}, bf16[2,2,384,256]{3,2,0,1:T(8,128)(2,1)}, u32[]{:S(2)}, u32[]{:S(2)}) collective-permute-start(bf16[2,2,384,256]{3,2,0,1:T(8,128)(2,1)} %bitcast.303), channel_id=1, source_target_pairs={{0,4},{4,0},{8,12},{12,8},{16,20},{20,16},{24,28},{28,24},{1,5},{5... | collective-permute-start | bytes 2359304 | tf_op jit(solution)/shard_map/ppermute | solution.py:199
  800.7 59.7 %collective-permute-start.63 = (bf16[2,2,384,256]{3,2,1,0:T(8,128)(2,1)}, bf16[2,2,384,256]{3,2,1,0:T(8,128)(2,1)}, u32[]{:S(2)}, u32[]{:S(2)}) collective-permute-start(bf16[2,2,384,256]{3,2,1,0:T(8,128)(2,1)} %fusion.54), channel_id=1, source_target_pairs={{0,8},{4,12},{8,0},{12,4},{16,24},{20,28},{24,16},{28,20},{1,9},{5... | collective-permute-start | bytes 2359304 | tf_op jit(solution)/shard_map/ppermute | solution.py:199
  821.2 69.4 %collective-permute-start.66 = (bf16[2,2,2,2,112,512]{5,4,0,1,2,3:T(8,128)(2,1)S(1)}, bf16[2,2,2,2,112,512]{5,4,0,1,2,3:T(8,128)(2,1)S(1)}, u32[]{:S(2)}, u32[]{:S(2)}) collective-permute-start(bf16[2,2,2,2,112,512]{5,4,0,1,2,3:T(8,128)(2,1)S(1)} %bitcast.364), channel_id=1, source_target_pairs={{0,1},{1,0},{2,3},{3,2},{4,5},{5,4},{6,7},{7,6},{8,9},{9,8},{10,11... | collective-permute-start | bytes 5505032 | tf_op jit(solution)/shard_map/ppermute | solution.py:199
  834.8 55.1 %collective-permute-start.71 = (bf16[2,2,384,512]{2,3,0,1:T(8,128)(2,1)S(1)}, bf16[2,2,384,512]{2,3,0,1:T(8,128)(2,1)S(1)}, u32[]{:S(2)}, u32[]{:S(2)}) collective-permute-start(bf16[2,2,384,512]{2,3,0,1:T(8,128)(2,1)S(1)} %fusion.20), channel_id=1, source_target_pairs={{0,4},{4,0},{8,12},{12,8},{16,20},{20,16},{24,28},{28,24},{1,5},{5... | collective-permute-start | bytes 4718600 | tf_op jit(solution)/shard_map/ppermute | solution.py:199
  858.1 17.3 %collective-permute-start.61 = (bf16[2,384,256]{2,1,0:T(8,128)(2,1)S(1)}, bf16[2,384,256]{2,1,0:T(8,128)(2,1)S(1)}, u32[]{:S(2)}, u32[]{:S(2)}) collective-permute-start(bf16[2,384,256]{2,1,0:T(8,128)(2,1)S(1)} %dynamic-slice_bitcast_fusion.5), channel_id=1, source_target_pairs={{0,8},{4,12},{8,0},{12,4},{16,24},{20,28},{24,16},{28,20},{1,9},{5... | collective-permute-start | bytes 1179656 | tf_op jit(solution)/shard_map/ppermute | solution.py:199
  861.8 25.7 %collective-permute-start.64 = (bf16[2,384,256]{2,1,0:T(8,128)(2,1)S(1)}, bf16[2,384,256]{2,1,0:T(8,128)(2,1)S(1)}, u32[]{:S(2)}, u32[]{:S(2)}) collective-permute-start(bf16[2,384,256]{2,1,0:T(8,128)(2,1)S(1)} %dynamic-slice_bitcast_fusion.4), channel_id=1, source_target_pairs={{0,16},{4,20},{8,24},{12,28},{16,0},{20,4},{24,8},{28,12},{1,17},{... | collective-permute-start | bytes 1179656 | tf_op jit(solution)/shard_map/ppermute | solution.py:199
  864.2 24.2 %collective-permute-start.59 = (bf16[64,3072]{1,0:T(8,128)(2,1)S(1)}, bf16[64,3072]{1,0:T(8,128)(2,1)S(1)}, u32[]{:S(2)}, u32[]{:S(2)}) collective-permute-start(bf16[64,3072]{1,0:T(8,128)(2,1)S(1)} %slice.743), channel_id=1, source_target_pairs={{0,2},{1,3},{2,0},{3,1},{4,6},{5,7},{6,4},{7,5},{8,10},{9,11},{10,... | collective-permute-start | bytes 1179656 | tf_op jit(solution)/shard_map/ppermute | solution.py:199
  875.5 18.5 %collective-permute-start.62 = (bf16[384,256]{1,0:T(8,128)(2,1)S(1)}, bf16[384,256]{1,0:T(8,128)(2,1)S(1)}, u32[]{:S(2)}, u32[]{:S(2)}) collective-permute-start(bf16[384,256]{1,0:T(8,128)(2,1)S(1)} %dynamic-slice_bitcast_fusion.8), channel_id=1, source_target_pairs={{0,16},{4,20},{8,24},{12,28},{16,0},{20,4},{24,8},{28,12},{1,17},{... | collective-permute-start | bytes 589832 | tf_op jit(solution)/shard_map/ppermute | solution.py:199
  892.1 18.0 %collective-permute-start.67 = (bf16[2,2,2,112,512]{4,3,0,1,2:T(8,128)(2,1)S(1)}, bf16[2,2,2,112,512]{4,3,0,1,2:T(8,128)(2,1)S(1)}, u32[]{:S(2)}, u32[]{:S(2)}) collective-permute-start(bf16[2,2,2,112,512]{4,3,0,1,2:T(8,128)(2,1)S(1)} %dynamic-slice_bitcast_fusion), channel_id=1, source_target_pairs={{0,2},{1,3},{2,0},{3,1},{4,6},{5,7},{6,4},{7,5},{8,10},{9,11},{10,... | collective-permute-start | bytes 2752520 | tf_op jit(solution)/shard_map/ppermute | solution.py:199
  (180 other events, 1860.9 us)

commit v4 on v3

--- a/solution.py
+++ b/solution.py
@@ -694,7 +694,7 @@
         dnormed2 = streams(dnormed2_packed)
         mlp_out = streams(
             scatter_all(
-                out_most, out_far, out_corner[:size], out_corner[size:], [], False, back_events[-1]
+                out_most, out_far, out_corner[:size], out_corner[size:], [], False, back_events[1]
             )
         )
         if copying:

time: 949 us -> 940 us (level)
  waiting for transfers between devices: 498 us -> 483 us
    ppermute x79, waiting for transfers between devices: 498 us -> 483 us  [hop(): lax.ppermute(value, axis, [(i, i ^ mask) for i in range(sizes[axis])])]
    add x1 -> x2, other arithmetic: 5.62 us -> 16.9 us  [scatter_all(): most = most.astype(wider) + hop(other_most, core, *earlier).astype(wider)]
    unnamed x350 -> x326, local copies, waits for them, and re-layouts: 47.6 us -> 45.1 us
  transfers between devices with their start and end apart: 79 -> 79, of which waited for: 38 -> 36; matrix products, arithmetic and copies ran while one was open for 24% -> 25% of each run, Pallas kernels for 5% -> 5%
where the time goes in v4:
time: 940 us; the launch traced here: 931 us
  waiting for transfers between devices  483 us (51%)
  other arithmetic  114 us (12%)
  local copies, waits for them, and re-layouts  109 us (12%)
  starting transfers between devices  94.9 us (10%)
  Pallas kernels  75.8 us (8%)
  matrix products  48.3 us (5%)
    ppermute x79, waiting for transfers between devices, hop(): lax.ppermute(value, axis, [(i, i ^ mask) for i in range(sizes[axis])])  483 us
    ppermute x79, starting transfers between devices, hop(): lax.ppermute(value, axis, [(i, i ^ mask) for i in range(sizes[axis])])  94.9 us
    pallas_call x3, Pallas kernels, feed_forward(): pl.pallas_call(functools.partial(feed_kernel, count, half, len(kept), n_c...  66.9 us
    unnamed x326, local copies, waits for them, and re-layouts  45.1 us
    dynamic_update_slice x26, other arithmetic, local(): lax.dynamic_update_slice_in_dim(wide_mlp[i], parts[i].astype(wider), peer...  29.7 us
    dot_general x12, matrix products, rows_contract(): lax.dot_general(former, latter, (((0,), (0,)), ((), ())), preferred_eleme...  29.2 us
  transfers between devices with their start and end apart: 79, of which 36 were waited for; matrix products, arithmetic and copies ran while one was open for 25% of the time, Pallas kernels for 5%

profile of v4, /device:TPU:0, one launch (start us, length us, event | category | flops | bytes accessed | tf_op | source)
XLA Modules:
  0.0 930.6 jit_solution(9116043961061880164)
XLA Ops:
  3.9 3.0 collective-permute-start.10
  10.6 2.6 collective-permute-start.2
  28.8 3.4 pack_weights.1
  38.8 2.7 collective-permute-start.11
  49.5 8.2 collective-permute-done.11
  57.9 8.6 collective-permute-done.8
  68.0 14.3 %collective-permute-done.13 = bf16[384,512]{1,0:T(8,128)(2,1)S(1)} collective-permute-done((bf16[384,512]{1,0:T(8,128)(2,1)S(1)}, bf16[384,512]{1,0:T(8,128)(2,1)S(1)}, u32[]{:S(2)}, u32[]{:S(2)}) %collective-permute-start.13) | collective-permute-done | bytes 393248 | tf_op jit(solution)/shard_map/ppermute | solution.py:199
  82.5 3.8 collective-permute-start.14
  89.7 21.6 %collective-permute-done.14 = bf16[2,384,512]{2,1,0:T(8,128)(2,1)S(1)} collective-permute-done((bf16[2,384,512]{2,1,0:T(8,128)(2,1)S(1)}, bf16[2,384,512]{2,1,0:T(8,128)(2,1)S(1)}, u32[]{:S(2)}, u32[]{:S(2)}) %collective-permute-start.14) | collective-permute-done | bytes 786464 | tf_op jit(solution)/shard_map/ppermute | solution.py:199
  120.6 25.6 %collective-permute-done.15 = bf16[2,2,384,512]{3,2,0,1:T(8,128)(2,1)S(1)} collective-permute-done((bf16[2,2,384,512]{3,2,0,1:T(8,128)(2,1)S(1)}, bf16[2,2,384,512]{3,2,0,1:T(8,128)(2,1)S(1)}, u32[]{:S(2)}, u32[]{:S(2)}) %collective-permute-start.15) | collective-permute-done | bytes 1572896 | tf_op jit(solution)/shard_map/ppermute | solution.py:199
  175.0 2.5 pad_maximum_fusion.3
  181.1 3.5 collective-permute-done.20
  187.3 11.6 %collective-permute-done.21.refs_6_ = bf16[896,512]{1,0:T(8,128)(2,1)S(1)} collective-permute-done((bf16[896,512]{1,0:T(8,128)(2,1)}, bf16[896,512]{1,0:T(8,128)(2,1)S(1)}, u32[]{:S(2)}, u32[]{:S(2)}) %collective-permute-start.21) | collective-permute-done | bytes 917536 | tf_op jit(solution)/shard_map/ppermute | solution.py:199
  198.9 17.9 %collective-permute-done.22.refs_2_ = bf16[896,512]{1,0:T(8,128)(2,1)} collective-permute-done((bf16[896,512]{1,0:T(8,128)(2,1)}, bf16[896,512]{1,0:T(8,128)(2,1)}, u32[]{:S(2)}, u32[]{:S(2)}) %collective-permute-start.22) | collective-permute-done | bytes 917536 | tf_op jit(solution)/shard_map/ppermute | solution.py:199
  221.8 2.7 constant_dynamic-update-slice_fusion.10
  224.4 11.8 %collective-permute-done.23 = bf16[64,3072]{1,0:T(8,128)(2,1)S(1)} collective-permute-done((bf16[64,3072]{1,0:T(8,128)(2,1)S(1)}, bf16[64,3072]{1,0:T(8,128)(2,1)S(1)}, u32[]{:S(2)}, u32[]{:S(2)}) %collective-permute-start.23) | collective-permute-done | bytes 393248 | tf_op jit(solution)/shard_map/ppermute | solution.py:199
  236.4 2.7 constant_dynamic-update-slice_fusion.9
  240.8 14.6 %collective-permute-done.24 = bf16[128,3072]{1,0:T(8,128)(2,1)S(1)} collective-permute-done((bf16[128,3072]{1,0:T(8,128)(2,1)S(1)}, bf16[128,3072]{1,0:T(8,128)(2,1)S(1)}, u32[]{:S(2)}, u32[]{:S(2)}) %collective-permute-start.24) | collective-permute-done | bytes 786464 | tf_op jit(solution)/shard_map/ppermute | solution.py:199
  259.8 31.6 %collective-permute-done.25.refs_1_ = bf16[256,3072]{1,0:T(8,128)(2,1)S(1)} collective-permute-done((bf16[256,3072]{1,0:T(8,128)(2,1)S(1)}, bf16[256,3072]{1,0:T(8,128)(2,1)S(1)}, u32[]{:S(2)}, u32[]{:S(2)}) %collective-permute-start.25) | collective-permute-done | bytes 1572896 | tf_op jit(solution)/shard_map/ppermute | solution.py:199
  292.7 3.3 collective-permute-done.26.refs_2_
  300.7 20.6 %collective-permute-done.31.refs_3_ = bf16[896,512]{1,0:T(8,128)(2,1)S(1)} collective-permute-done((bf16[896,512]{1,0:T(8,128)(2,1)S(1)}, bf16[896,512]{1,0:T(8,128)(2,1)S(1)}, u32[]{:S(2)}, u32[]{:S(2)}) %collective-permute-start.31) | collective-permute-done | bytes 917536 | tf_op jit(solution)/shard_map/ppermute | solution.py:199
  321.2 2.6 collective-permute-start.33
  325.4 32.4 %collective-permute-done.37 = bf16[128,3072]{1,0:T(8,128)(2,1)S(1)} collective-permute-done((bf16[128,3072]{1,0:T(8,128)(2,1)S(1)}, bf16[128,3072]{1,0:T(8,128)(2,1)S(1)}, u32[]{:S(2)}, u32[]{:S(2)}) %collective-permute-start.37) | collective-permute-done | bytes 786464 | tf_op jit(solution)/shard_map/ppermute | solution.py:199
  359.7 17.7 %collective-permute-done.30.refs_1_ = bf16[896,512]{1,0:T(8,128)(2,1)S(1)} collective-permute-done((bf16[896,512]{1,0:T(8,128)(2,1)S(1)}, bf16[896,512]{1,0:T(8,128)(2,1)S(1)}, u32[]{:S(2)}, u32[]{:S(2)}) %collective-permute-start.30) | collective-permute-done | bytes 917536 | tf_op jit(solution)/shard_map/ppermute | solution.py:199
  377.3 25.5 %collective-permute-done.32.refs_5_ = bf16[896,512]{1,0:T(8,128)(2,1)S(1)} collective-permute-done((bf16[896,512]{1,0:T(8,128)(2,1)S(1)}, bf16[896,512]{1,0:T(8,128)(2,1)S(1)}, u32[]{:S(2)}, u32[]{:S(2)}) %collective-permute-start.32) | collective-permute-done | bytes 917536 | tf_op jit(solution)/shard_map/ppermute | solution.py:199
  402.8 2.4 unpack_weights.1
  408.5 22.8 %feed_forward.3 = (bf16[2048,2048]{1,0:T(8,128)(2,1)}, bf16[2048,1024]{1,0:T(8,128)(2,1)}, bf16[2048,2048]{1,0:T(8,128)(2,1)}, bf16[2048,1024]{1,0:T(8,128)(2,1)...) custom-call(bf16[256,3072]{1,0:T(8,128)(2,1)} %copy-done.128, ...), custom_call_target="tpu_custom_call" | custom-call | flops 10871635968 | bytes 28311552 | tf_op jit(solution)/shard_map/feed_forward/pallas_call | solution.py:157
  431.4 2.6 copy-done.16
  434.0 18.6 %feed_forward.4 = (bf16[2048,2048]{1,0:T(8,128)(2,1)}, bf16[2048,1024]{1,0:T(8,128)(2,1)}, bf16[2048,2048]{1,0:T(8,128)(2,1)}, bf16[2048,1024]{1,0:T(8,128)(2,1)...) custom-call(bf16[256,3072]{1,0:T(8,128)(2,1)} %constant_dynamic-upda, ...), custom_call_target="tpu_custom_call", output_to_operand_aliasing={{0}: (8, {}), {1}: (9, {}), {2}: (10, {}), {3}: (11, {}), {... | custom-call | flops 7247757312 | bytes 18874368 | tf_op jit(solution)/shard_map/feed_forward/pallas_call | solution.py:157
  452.6 25.5 %feed_forward.5 = (bf16[2048,2048]{1,0:T(8,128)(2,1)}, bf16[2048,1024]{1,0:T(8,128)(2,1)}, bf16[2048,2048]{1,0:T(8,128)(2,1)}, bf16[2048,1024]{1,0:T(8,128)(2,1)...) custom-call(bf16[768,3072]{1,0:T(8,128)(2,1)} %collective-permute-do, ...), custom_call_target="tpu_custom_call", output_to_operand_aliasing={{0}: (10, {}), {1}: (11, {}), {2}: (12, {}), {3}: (13, {}),... | custom-call | flops 10871635968 | bytes 28311552 | tf_op jit(solution)/shard_map/feed_forward/pallas_call | solution.py:157
  482.0 2.7 copy.108
  484.7 2.5 copy.107
  487.3 2.7 slice.567
  490.0 3.1 convolution_convert_fusion.19.refs_3_
  500.1 11.2 %convert_add_fusion.1 = (f32[768,3072]{1,0:T(8,128)}, bf16[768,3072]{1,0:T(8,128)(2,1)}) fusion(bf16[768,3072]{1,0:T(8,128)(2,1)} %collective-permute-done.39, bf16[768,3072]{1,0:T(8,128)(2,1)} %get-tuple-element.135), kind=kLoop, calls=%fused_computation.3 | loop fusion | flops 9437184 | bytes 23592960 | tf_op jit(solution)/shard_map/add | solution.py:272
  513.7 4.6 collective-permute-done.50
  518.6 3.7 fusion.23
  523.9 9.5 %convolution_convert_fusion.refs_0_ = bf16[2048,1024]{1,0:T(8,128)(2,1)S(1)} fusion(bf16[2048,2048]{1,0:T(8,128)(2,1)S(1)} %bitcast.310, bf16[2048,1024]{1,0:T(8,128)(2,1)S(1)} %copy-done.23), kind=kOutput, calls=%fused_computation.6 | convolution fusion | flops 8592031744 | bytes 16777216 | tf_op jit(solution)/shard_map/dot_general | solution.py:33
  533.4 24.2 %collective-permute-done.42 = bf16[256,3072]{1,0:T(8,128)(2,1)S(1)} collective-permute-done((bf16[256,3072]{1,0:T(8,128)(2,1)S(1)}, bf16[256,3072]{1,0:T(8,128)(2,1)S(1)}, u32[]{:S(2)}, u32[]{:S(2)}) %collective-permute-start.42) | collective-permute-done | bytes 1572896 | tf_op jit(solution)/shard_map/ppermute | solution.py:199
  558.8 4.7 convolution_convert_fusion.3.refs_1_
  563.6 3.1 pack_gradients.1
  566.8 3.2 collective-permute-start.55
  576.7 33.6 %collective-permute-done.55 = bf16[896,512]{1,0:T(8,128)(2,1)S(1)} collective-permute-done((bf16[896,512]{1,0:T(8,128)(2,1)S(1)}, bf16[896,512]{1,0:T(8,128)(2,1)S(1)}, u32[]{:S(2)}, u32[]{:S(2)}) %collective-permute-start.55) | collective-permute-done | bytes 917536 | tf_op jit(solution)/shard_map/ppermute | solution.py:199
  613.5 2.6 fusion.2
  621.0 5.6 convert_add_fusion
  626.6 19.4 %collective-permute-done.46 = bf16[256,3072]{1,0:T(8,128)(2,1)S(1)} collective-permute-done((bf16[256,3072]{1,0:T(8,128)(2,1)}, bf16[256,3072]{1,0:T(8,128)(2,1)S(1)}, u32[]{:S(2)}, u32[]{:S(2)}) %collective-permute-start.46) | collective-permute-done | bytes 1572896 | tf_op jit(solution)/shard_map/ppermute | solution.py:199
  650.7 3.1 collective-permute-start.53
  658.6 16.5 %collective-permute-done.53 = bf16[64,3072]{1,0:T(8,128)(2,1)S(1)} collective-permute-done((bf16[64,3072]{1,0:T(8,128)(2,1)S(1)}, bf16[64,3072]{1,0:T(8,128)(2,1)S(1)}, u32[]{:S(2)}, u32[]{:S(2)}) %collective-permute-start.53) | collective-permute-done | bytes 393248 | tf_op jit(solution)/shard_map/ppermute | solution.py:199
  676.9 5.4 collective-permute-done.47
  684.1 24.0 %collective-permute-start.48 = (bf16[128,3072]{1,0:T(8,128)(2,1)}, bf16[128,3072]{1,0:T(8,128)(2,1)}, u32[]{:S(2)}, u32[]{:S(2)}) collective-permute-start(bf16[128,3072]{1,0:T(8,128)(2,1)} %slice.713), channel_id=1, source_target_pairs={{0,8},{4,12},{8,0},{12,4},{16,24},{20,28},{24,16},{28,20},{1,9},{5... | collective-permute-start | bytes 2359304 | tf_op jit(solution)/shard_map/ppermute | solution.py:199
  709.6 8.8 collective-permute-done.74
  721.1 12.7 %collective-permute-done.48 = bf16[128,3072]{1,0:T(8,128)(2,1)} collective-permute-done((bf16[128,3072]{1,0:T(8,128)(2,1)}, bf16[128,3072]{1,0:T(8,128)(2,1)}, u32[]{:S(2)}, u32[]{:S(2)}) %collective-permute-start.48) | collective-permute-done | bytes 786464 | tf_op jit(solution)/shard_map/ppermute | solution.py:199
  739.2 15.6 %collective-permute-done.49 = bf16[64,3072]{1,0:T(8,128)(2,1)S(1)} collective-permute-done((bf16[64,3072]{1,0:T(8,128)(2,1)S(1)}, bf16[64,3072]{1,0:T(8,128)(2,1)S(1)}, u32[]{:S(2)}, u32[]{:S(2)}) %collective-permute-start.49) | collective-permute-done | bytes 393248 | tf_op jit(solution)/shard_map/ppermute | solution.py:199
  761.1 6.9 collective-permute-done.56
  769.1 2.4 collective-permute-start.78
  806.5 4.2 copy.122
  810.7 2.5 convolution_convert_fusion.7
  819.6 9.1 collective-permute-done.78
  860.5 9.6 %collective-permute-done.61 = bf16[2,384,256]{2,1,0:T(8,128)(2,1)S(1)} collective-permute-done((bf16[2,384,256]{2,1,0:T(8,128)(2,1)S(1)}, bf16[2,384,256]{2,1,0:T(8,128)(2,1)S(1)}, u32[]{:S(2)}, u32[]{:S(2)}) %collective-permute-start.61) | collective-permute-done | bytes 393248 | tf_op jit(solution)/shard_map/ppermute | solution.py:199
  870.4 12.1 %collective-permute-done.64 = bf16[2,384,256]{2,1,0:T(8,128)(2,1)S(1)} collective-permute-done((bf16[2,384,256]{2,1,0:T(8,128)(2,1)S(1)}, bf16[2,384,256]{2,1,0:T(8,128)(2,1)S(1)}, u32[]{:S(2)}, u32[]{:S(2)}) %collective-permute-start.64) | collective-permute-done | bytes 393248 | tf_op jit(solution)/shard_map/ppermute | solution.py:199
  889.6 11.2 %collective-permute-done.72 = bf16[2,384,512]{1,2,0:T(8,128)(2,1)S(1)} collective-permute-done((bf16[2,384,512]{1,2,0:T(8,128)(2,1)S(1)}, bf16[2,384,512]{1,2,0:T(8,128)(2,1)S(1)}, u32[]{:S(2)}, u32[]{:S(2)}) %collective-permute-start.72) | collective-permute-done | bytes 786464 | tf_op jit(solution)/shard_map/ppermute | solution.py:199
  904.1 9.6 %collective-permute-done.73 = bf16[384,512]{0,1:T(8,128)(2,1)S(1)} collective-permute-done((bf16[384,512]{0,1:T(8,128)(2,1)S(1)}, bf16[384,512]{0,1:T(8,128)(2,1)S(1)}, u32[]{:S(2)}, u32[]{:S(2)}) %collective-permute-start.73) | collective-permute-done | bytes 393248 | tf_op jit(solution)/shard_map/ppermute | solution.py:199
  914.9 5.7 collective-permute-done.69
  922.4 5.2 collective-permute-done.70
  (702 shorter events, 257.5 us)
Async XLA Ops:
  3.9 33.8 %collective-permute-start.10 = (bf16[384,256]{1,0:T(8,128)(2,1)}, bf16[384,256]{1,0:T(8,128)(2,1)}, u32[]{:S(2)}, u32[]{:S(2)}) collective-permute-start(bf16[384,256]{1,0:T(8,128)(2,1)} %get-tuple-element.276), channel_id=1, source_target_pairs={{0,4},{4,0},{8,12},{12,8},{16,20},{20,16},{24,28},{28,24},{1,5},{5... | collective-permute-start | bytes 589832 | tf_op jit(solution)/shard_map/ppermute | solution.py:199
  8.3 40.0 %collective-permute-start = (bf16[64,3072]{1,0:T(8,128)(2,1)}, bf16[64,3072]{1,0:T(8,128)(2,1)}, u32[]{:S(2)}, u32[]{:S(2)}) collective-permute-start(bf16[64,3072]{1,0:T(8,128)(2,1)} %constant_dynamic-update-slice_fusion), channel_id=1, source_target_pairs={{0,2},{1,3},{2,0},{3,1},{4,6},{5,7},{6,4},{7,5},{8,10},{9,11},{10,... | collective-permute-start | bytes 1179656 | tf_op jit(solution)/shard_map/ppermute | solution.py:199
  10.6 21.8 %collective-permute-start.2 = (bf16[112,512]{1,0:T(8,128)(2,1)}, bf16[112,512]{1,0:T(8,128)(2,1)}, u32[]{:S(2)}, u32[]{:S(2)}) collective-permute-start(bf16[112,512]{1,0:T(8,128)(2,1)} %fusion.94), channel_id=1, source_target_pairs={{0,16},{4,20},{8,24},{12,28},{16,0},{20,4},{24,8},{28,12},{1,17},{... | collective-permute-start | bytes 344072 | tf_op jit(solution)/shard_map/ppermute | solution.py:199
  13.1 30.5 %collective-permute-start.7 = (bf16[384,256]{1,0:T(8,128)(2,1)}, bf16[384,256]{1,0:T(8,128)(2,1)}, u32[]{:S(2)}, u32[]{:S(2)}) collective-permute-start(bf16[384,256]{1,0:T(8,128)(2,1)} %get-tuple-element.277), channel_id=1, source_target_pairs={{0,16},{4,20},{8,24},{12,28},{16,0},{20,4},{24,8},{28,12},{1,17},{... | collective-permute-start | bytes 589832 | tf_op jit(solution)/shard_map/ppermute | solution.py:199
  38.8 18.9 %collective-permute-start.11 = (bf16[2,384,256]{2,1,0:T(8,128)(2,1)S(1)}, bf16[2,384,256]{2,1,0:T(8,128)(2,1)S(1)}, u32[]{:S(2)}, u32[]{:S(2)}) collective-permute-start(bf16[2,384,256]{2,1,0:T(8,128)(2,1)S(1)} %maximum_select_fusion.16), channel_id=1, source_target_pairs={{0,16},{4,20},{8,24},{12,28},{16,0},{20,4},{24,8},{28,12},{1,17},{... | collective-permute-start | bytes 1179656 | tf_op jit(solution)/shard_map/ppermute | solution.py:199
  44.8 21.7 %collective-permute-start.8 = (bf16[2,384,256]{2,1,0:T(8,128)(2,1)S(1)}, bf16[2,384,256]{2,1,0:T(8,128)(2,1)S(1)}, u32[]{:S(2)}, u32[]{:S(2)}) collective-permute-start(bf16[2,384,256]{2,1,0:T(8,128)(2,1)S(1)} %maximum_select_fusion.15), channel_id=1, source_target_pairs={{0,8},{4,12},{8,0},{12,4},{16,24},{20,28},{24,16},{28,20},{1,9},{5... | collective-permute-start | bytes 1179656 | tf_op jit(solution)/shard_map/ppermute | solution.py:199
  47.6 19.5 %collective-permute-start.4 = (bf16[2,2,112,512]{3,2,1,0:T(8,128)(2,1)S(1)}, bf16[2,2,112,512]{3,2,1,0:T(8,128)(2,1)S(1)}, u32[]{:S(2)}, u32[]{:S(2)}) collective-permute-start(bf16[2,2,112,512]{3,2,1,0:T(8,128)(2,1)S(1)} %maximum_select_fusion.14), channel_id=1, source_target_pairs={{0,4},{4,0},{8,12},{12,8},{16,20},{20,16},{24,28},{28,24},{1,5},{5... | collective-permute-start | bytes 1376264 | tf_op jit(solution)/shard_map/ppermute | solution.py:199
  49.4 37.1 %collective-permute-start.1 = (bf16[128,3072]{1,0:T(8,128)(2,1)S(1)}, bf16[128,3072]{1,0:T(8,128)(2,1)S(1)}, u32[]{:S(2)}, u32[]{:S(2)}) collective-permute-start(bf16[128,3072]{1,0:T(8,128)(2,1)S(1)} %pad_maximum_fusion.9), channel_id=1, source_target_pairs={{0,1},{1,0},{2,3},{3,2},{4,5},{5,4},{6,7},{7,6},{8,9},{9,8},{10,11... | collective-permute-start | bytes 2359304 | tf_op jit(solution)/shard_map/ppermute | solution.py:199
  57.8 56.4 %collective-permute-start.12 = (bf16[2,2,384,256]{3,2,1,0:T(8,128)(2,1)S(1)}, bf16[2,2,384,256]{3,2,1,0:T(8,128)(2,1)S(1)}, u32[]{:S(2)}, u32[]{:S(2)}) collective-permute-start(bf16[2,2,384,256]{3,2,1,0:T(8,128)(2,1)S(1)} %maximum_select_fusion.11), channel_id=1, source_target_pairs={{0,8},{4,12},{8,0},{12,4},{16,24},{20,28},{24,16},{28,20},{1,9},{5... | collective-permute-start | bytes 2359304 | tf_op jit(solution)/shard_map/ppermute | solution.py:199
  66.6 51.3 %collective-permute-start.9 = (bf16[2,2,384,256]{3,2,0,1:T(8,128)(2,1)S(1)}, bf16[2,2,384,256]{3,2,0,1:T(8,128)(2,1)S(1)}, u32[]{:S(2)}, u32[]{:S(2)}) collective-permute-start(bf16[2,2,384,256]{3,2,0,1:T(8,128)(2,1)S(1)} %maximum_select_fusion.9), channel_id=1, source_target_pairs={{0,4},{4,0},{8,12},{12,8},{16,20},{20,16},{24,28},{28,24},{1,5},{5... | collective-permute-start | bytes 2359304 | tf_op jit(solution)/shard_map/ppermute | solution.py:199
  67.1 22.2 %collective-permute-start.5 = (bf16[2,2,2,112,512]{4,3,2,1,0:T(8,128)(2,1)S(1)}, bf16[2,2,2,112,512]{4,3,2,1,0:T(8,128)(2,1)S(1)}, u32[]{:S(2)}, u32[]{:S(2)}) collective-permute-start(bf16[2,2,2,112,512]{4,3,2,1,0:T(8,128)(2,1)S(1)} %maximum_select_fusion.8), channel_id=1, source_target_pairs={{0,2},{1,3},{2,0},{3,1},{4,6},{5,7},{6,4},{7,5},{8,10},{9,11},{10,... | collective-permute-start | bytes 2752520 | tf_op jit(solution)/shard_map/ppermute | solution.py:199
  82.5 28.9 %collective-permute-start.14 = (bf16[2,384,512]{2,1,0:T(8,128)(2,1)S(1)}, bf16[2,384,512]{2,1,0:T(8,128)(2,1)S(1)}, u32[]{:S(2)}, u32[]{:S(2)}) collective-permute-start(bf16[2,384,512]{2,1,0:T(8,128)(2,1)S(1)} %maximum_select_fusion.13), channel_id=1, source_target_pairs={{0,8},{4,12},{8,0},{12,4},{16,24},{20,28},{24,16},{28,20},{1,9},{5... | collective-permute-start | bytes 2359304 | tf_op jit(solution)/shard_map/ppermute | solution.py:199
  86.6 26.5 %collective-permute-start.17 = (bf16[64,3072]{1,0:T(8,128)(2,1)S(1)}, bf16[64,3072]{1,0:T(8,128)(2,1)S(1)}, u32[]{:S(2)}, u32[]{:S(2)}) collective-permute-start(bf16[64,3072]{1,0:T(8,128)(2,1)S(1)} %get-tuple-element.98), channel_id=1, source_target_pairs={{0,16},{4,20},{8,24},{12,28},{16,0},{20,4},{24,8},{28,12},{1,17},{... | collective-permute-start | bytes 1179656 | tf_op jit(solution)/shard_map/ppermute | solution.py:199
  89.6 59.1 %collective-permute-start.6 = (bf16[2,2,2,2,112,512]{5,4,2,1,0,3:T(8,128)(2,1)S(1)}, bf16[2,2,2,2,112,512]{5,4,2,1,0,3:T(8,128)(2,1)S(1)}, u32[]{:S(2)}, u32[]{:S(2)}) collective-permute-start(bf16[2,2,2,2,112,512]{5,4,2,1,0,3:T(8,128)(2,1)S(1)} %maximum_select_fusion.2), channel_id=1, source_target_pairs={{0,1},{1,0},{2,3},{3,2},{4,5},{5,4},{6,7},{7,6},{8,9},{9,8},{10,11... | collective-permute-start | bytes 5505032 | tf_op jit(solution)/shard_map/ppermute | solution.py:199
  111.6 34.7 %collective-permute-start.15 = (bf16[2,2,384,512]{3,2,0,1:T(8,128)(2,1)S(1)}, bf16[2,2,384,512]{3,2,0,1:T(8,128)(2,1)S(1)}, u32[]{:S(2)}, u32[]{:S(2)}) collective-permute-start(bf16[2,2,384,512]{3,2,0,1:T(8,128)(2,1)S(1)} %maximum_select_fusion.6), channel_id=1, source_target_pairs={{0,4},{4,0},{8,12},{12,8},{16,20},{20,16},{24,28},{28,24},{1,5},{5... | collective-permute-start | bytes 4718600 | tf_op jit(solution)/shard_map/ppermute | solution.py:199
  113.1 55.9 %collective-permute-start.16 = (bf16[896,512]{1,0:T(8,128)(2,1)}, bf16[896,512]{1,0:T(8,128)(2,1)S(1)}, u32[]{:S(2)}, u32[]{:S(2)}) collective-permute-start(bf16[896,512]{1,0:T(8,128)(2,1)} %get-tuple-element.97), channel_id=1, source_target_pairs={{0,16},{4,20},{8,24},{12,28},{16,0},{20,4},{24,8},{28,12},{1,17},{... | collective-permute-start | bytes 2752520 | tf_op jit(solution)/shard_map/ppermute | solution.py:199
  114.3 54.7 %collective-permute-start.18 = (bf16[128,3072]{1,0:T(8,128)(2,1)}, bf16[128,3072]{1,0:T(8,128)(2,1)}, u32[]{:S(2)}, u32[]{:S(2)}) collective-permute-start(bf16[128,3072]{1,0:T(8,128)(2,1)} %pad_maximum_fusion.10), channel_id=1, source_target_pairs={{0,8},{4,12},{8,0},{12,4},{16,24},{20,28},{24,16},{28,20},{1,9},{5... | collective-permute-start | bytes 2359304 | tf_op jit(solution)/shard_map/ppermute | solution.py:199
  173.7 25.2 %collective-permute-start.21 = (bf16[896,512]{1,0:T(8,128)(2,1)}, bf16[896,512]{1,0:T(8,128)(2,1)S(1)}, u32[]{:S(2)}, u32[]{:S(2)}) collective-permute-start(bf16[896,512]{1,0:T(8,128)(2,1)} %get-tuple-element.101), channel_id=1, source_target_pairs={{0,24},{4,28},{8,16},{12,20},{16,8},{20,12},{24,0},{28,4},{1,25},{... | collective-permute-start | bytes 2752520 | tf_op jit(solution)/shard_map/ppermute | solution.py:199
  175.0 41.8 %collective-permute-start.22 = (bf16[896,512]{1,0:T(8,128)(2,1)}, bf16[896,512]{1,0:T(8,128)(2,1)}, u32[]{:S(2)}, u32[]{:S(2)}) collective-permute-start(bf16[896,512]{1,0:T(8,128)(2,1)} %get-tuple-element.103), channel_id=1, source_target_pairs={{0,8},{4,12},{8,0},{12,4},{16,24},{20,28},{24,16},{28,20},{1,9},{5... | collective-permute-start | bytes 2752520 | tf_op jit(solution)/shard_map/ppermute | solution.py:199
  177.5 44.3 %collective-permute-start.27 = (bf16[256,3072]{1,0:T(8,128)(2,1)}, bf16[256,3072]{1,0:T(8,128)(2,1)}, u32[]{:S(2)}, u32[]{:S(2)}) collective-permute-start(bf16[256,3072]{1,0:T(8,128)(2,1)} %pad_maximum_fusion.3), channel_id=1, source_target_pairs={{0,2},{1,3},{2,0},{3,1},{4,6},{5,7},{6,4},{7,5},{8,10},{9,11},{10,... | collective-permute-start | bytes 4718600 | tf_op jit(solution)/shard_map/ppermute | solution.py:199
  179.0 41.3 %collective-permute-start.28 = (bf16[256,3072]{1,0:T(8,128)(2,1)}, bf16[256,3072]{1,0:T(8,128)(2,1)}, u32[]{:S(2)}, u32[]{:S(2)}) collective-permute-start(bf16[256,3072]{1,0:T(8,128)(2,1)} %pad_maximum_fusion.3), channel_id=1, source_target_pairs={{0,4},{4,0},{8,12},{12,8},{16,20},{20,16},{24,28},{28,24},{1,5},{5... | collective-permute-start | bytes 4718600 | tf_op jit(solution)/shard_map/ppermute | solution.py:199
  216.8 19.5 %collective-permute-start.23 = (bf16[64,3072]{1,0:T(8,128)(2,1)S(1)}, bf16[64,3072]{1,0:T(8,128)(2,1)S(1)}, u32[]{:S(2)}, u32[]{:S(2)}) collective-permute-start(bf16[64,3072]{1,0:T(8,128)(2,1)S(1)} %pad_maximum_fusion.18), channel_id=1, source_target_pairs={{0,16},{4,20},{8,24},{12,28},{16,0},{20,4},{24,8},{28,12},{1,17},{... | collective-permute-start | bytes 1179656 | tf_op jit(solution)/shard_map/ppermute | solution.py:199
  220.3 37.7 %collective-permute-start.29 = (bf16[256,3072]{1,0:T(8,128)(2,1)}, bf16[256,3072]{1,0:T(8,128)(2,1)S(1)}, u32[]{:S(2)}, u32[]{:S(2)}) collective-permute-start(bf16[256,3072]{1,0:T(8,128)(2,1)} %collective-permute-done.28), channel_id=1, source_target_pairs={{0,2},{1,3},{2,0},{3,1},{4,6},{5,7},{6,4},{7,5},{8,10},{9,11},{10,... | collective-permute-start | bytes 4718600 | tf_op jit(solution)/shard_map/ppermute | solution.py:199
  236.3 19.0 %collective-permute-start.24 = (bf16[128,3072]{1,0:T(8,128)(2,1)S(1)}, bf16[128,3072]{1,0:T(8,128)(2,1)S(1)}, u32[]{:S(2)}, u32[]{:S(2)}) collective-permute-start(bf16[128,3072]{1,0:T(8,128)(2,1)S(1)} %pad_maximum_fusion.11), channel_id=1, source_target_pairs={{0,8},{4,12},{8,0},{12,4},{16,24},{20,28},{24,16},{28,20},{1,9},{5... | collective-permute-start | bytes 2359304 | tf_op jit(solution)/shard_map/ppermute | solution.py:199
  256.5 34.9 %collective-permute-start.25 = (bf16[256,3072]{1,0:T(8,128)(2,1)S(1)}, bf16[256,3072]{1,0:T(8,128)(2,1)S(1)}, u32[]{:S(2)}, u32[]{:S(2)}) collective-permute-start(bf16[256,3072]{1,0:T(8,128)(2,1)S(1)} %get-tuple-element.256.refs_0_), channel_id=1, source_target_pairs={{0,2},{1,3},{2,0},{3,1},{4,6},{5,7},{6,4},{7,5},{8,10},{9,11},{10,... | collective-permute-start | bytes 4718600 | tf_op jit(solution)/shard_map/ppermute | solution.py:199
  259.3 172.1 %collective-permute-start.35 = (bf16[1024,3072]{1,0:T(8,128)(2,1)}, bf16[1024,3072]{1,0:T(8,128)(2,1)S(1)}, u32[]{:S(2)}, u32[]{:S(2)}) collective-permute-start(bf16[1024,3072]{1,0:T(8,128)(2,1)} %constant_dynamic-update-slice_fusion.8.refs_3_.refs_4_.refs_5_.refs_2_), channel_id=1, source_target_pairs={{0,1},{1,0},{2,3},{3,2},{4,5},{5,4},{6,7},{7,6},{8,9},{9,8},{10,11... | collective-permute-start | bytes 18874376 | tf_op jit(solution)/shard_map/ppermute | solution.py:199
  259.3 36.8 %collective-permute-start.26 = (bf16[256,3072]{1,0:T(8,128)(2,1)S(1)}, bf16[256,3072]{1,0:T(8,128)(2,1)S(1)}, u32[]{:S(2)}, u32[]{:S(2)}) collective-permute-start(bf16[256,3072]{1,0:T(8,128)(2,1)S(1)} %get-tuple-element.256.refs_0_), channel_id=1, source_target_pairs={{0,4},{4,0},{8,12},{12,8},{16,20},{20,16},{24,28},{28,24},{1,5},{5... | collective-permute-start | bytes 4718600 | tf_op jit(solution)/shard_map/ppermute | solution.py:199
  297.4 155.2 %collective-permute-start.34 = (bf16[768,3072]{1,0:T(8,128)(2,1)}, bf16[768,3072]{1,0:T(8,128)(2,1)}, u32[]{:S(2)}, u32[]{:S(2)}) collective-permute-start(bf16[768,3072]{1,0:T(8,128)(2,1)} %constant_dynamic-update-slice_fusion.14), channel_id=1, source_target_pairs={{0,1},{1,0},{2,3},{3,2},{4,5},{5,4},{6,7},{7,6},{8,9},{9,8},{10,11... | collective-permute-start | bytes 14155784 | tf_op jit(solution)/shard_map/ppermute | solution.py:199
  297.5 23.8 %collective-permute-start.31 = (bf16[896,512]{1,0:T(8,128)(2,1)S(1)}, bf16[896,512]{1,0:T(8,128)(2,1)S(1)}, u32[]{:S(2)}, u32[]{:S(2)}) collective-permute-start(bf16[896,512]{1,0:T(8,128)(2,1)S(1)} %copy-done.15), channel_id=1, source_target_pairs={{0,12},{4,8},{8,4},{12,0},{16,28},{20,24},{24,20},{28,16},{1,13},{... | collective-permute-start | bytes 2752520 | tf_op jit(solution)/shard_map/ppermute | solution.py:199
  297.8 26.0 %collective-permute-start.36 = (bf16[128,3072]{1,0:T(8,128)(2,1)S(1)}, bf16[128,3072]{1,0:T(8,128)(2,1)S(1)}, u32[]{:S(2)}, u32[]{:S(2)}) collective-permute-start(bf16[128,3072]{1,0:T(8,128)(2,1)S(1)} %slice.704), channel_id=1, source_target_pairs={{0,2},{1,3},{2,0},{3,1},{4,6},{5,7},{6,4},{7,5},{8,10},{9,11},{10,... | collective-permute-start | bytes 2359304 | tf_op jit(solution)/shard_map/ppermute | solution.py:199
  299.1 58.6 %collective-permute-start.37 = (bf16[128,3072]{1,0:T(8,128)(2,1)S(1)}, bf16[128,3072]{1,0:T(8,128)(2,1)S(1)}, u32[]{:S(2)}, u32[]{:S(2)}) collective-permute-start(bf16[128,3072]{1,0:T(8,128)(2,1)S(1)} %slice.705), channel_id=1, source_target_pairs={{0,4},{4,0},{8,12},{12,8},{16,20},{20,16},{24,28},{28,24},{1,5},{5... | collective-permute-start | bytes 2359304 | tf_op jit(solution)/shard_map/ppermute | solution.py:199
  321.2 38.4 %collective-permute-start.33 = (bf16[896,512]{1,0:T(8,128)(2,1)S(1)}, bf16[896,512]{1,0:T(8,128)(2,1)S(1)}, u32[]{:S(2)}, u32[]{:S(2)}) collective-permute-start(bf16[896,512]{1,0:T(8,128)(2,1)S(1)} %copy-done.13), channel_id=1, source_target_pairs={{0,28},{4,24},{8,20},{12,16},{16,12},{20,8},{24,4},{28,0},{1,29},{... | collective-permute-start | bytes 2752520 | tf_op jit(solution)/shard_map/ppermute | solution.py:199
  323.9 53.5 %collective-permute-start.30 = (bf16[896,512]{1,0:T(8,128)(2,1)S(1)}, bf16[896,512]{1,0:T(8,128)(2,1)S(1)}, u32[]{:S(2)}, u32[]{:S(2)}) collective-permute-start(bf16[896,512]{1,0:T(8,128)(2,1)S(1)} %copy-done.11), channel_id=1, source_target_pairs={{0,4},{4,0},{8,12},{12,8},{16,20},{20,16},{24,28},{28,24},{1,5},{5... | collective-permute-start | bytes 2752520 | tf_op jit(solution)/shard_map/ppermute | solution.py:199
  357.7 45.0 %collective-permute-start.32 = (bf16[896,512]{1,0:T(8,128)(2,1)S(1)}, bf16[896,512]{1,0:T(8,128)(2,1)S(1)}, u32[]{:S(2)}, u32[]{:S(2)}) collective-permute-start(bf16[896,512]{1,0:T(8,128)(2,1)S(1)} %copy-done.9), channel_id=1, source_target_pairs={{0,20},{4,16},{8,28},{12,24},{16,4},{20,0},{24,12},{28,8},{1,21},{... | collective-permute-start | bytes 2752520 | tf_op jit(solution)/shard_map/ppermute | solution.py:199
  359.6 71.7 %collective-permute-start.38 = (bf16[256,3072]{1,0:T(8,128)(2,1)}, bf16[256,3072]{1,0:T(8,128)(2,1)}, u32[]{:S(2)}, u32[]{:S(2)}) collective-permute-start(bf16[256,3072]{1,0:T(8,128)(2,1)} %constant_dynamic-update-slice_fusion.19.refs_0_), channel_id=1, source_target_pairs={{0,1},{1,0},{2,3},{3,2},{4,5},{5,4},{6,7},{7,6},{8,9},{9,8},{10,11... | collective-permute-start | bytes 4718600 | tf_op jit(solution)/shard_map/ppermute | solution.py:199
  478.1 22.0 %collective-permute-start.39 = (bf16[768,3072]{1,0:T(8,128)(2,1)}, bf16[768,3072]{1,0:T(8,128)(2,1)}, u32[]{:S(2)}, u32[]{:S(2)}) collective-permute-start(bf16[768,3072]{1,0:T(8,128)(2,1)} %get-tuple-element.136), channel_id=1, source_target_pairs={{0,1},{1,0},{2,3},{3,2},{4,5},{5,4},{6,7},{7,6},{8,9},{9,8},{10,11... | collective-permute-start | bytes 14155784 | tf_op jit(solution)/shard_map/ppermute | solution.py:199
  498.4 19.8 %collective-permute-start.50 = (bf16[128,3072]{1,0:T(8,128)(2,1)}, bf16[128,3072]{1,0:T(8,128)(2,1)}, u32[]{:S(2)}, u32[]{:S(2)}) collective-permute-start(bf16[128,3072]{1,0:T(8,128)(2,1)} %get-tuple-element.197), channel_id=1, source_target_pairs={{0,4},{4,0},{8,12},{12,8},{16,20},{20,16},{24,28},{28,24},{1,5},{5... | collective-permute-start | bytes 2359304 | tf_op jit(solution)/shard_map/ppermute | solution.py:199
  499.0 19.5 %collective-permute-start.41 = (bf16[128,3072]{1,0:T(8,128)(2,1)}, bf16[128,3072]{1,0:T(8,128)(2,1)}, u32[]{:S(2)}, u32[]{:S(2)}) collective-permute-start(bf16[128,3072]{1,0:T(8,128)(2,1)} %get-tuple-element.198), channel_id=1, source_target_pairs={{0,2},{1,3},{2,0},{3,1},{4,6},{5,7},{6,4},{7,5},{8,10},{9,11},{10,... | collective-permute-start | bytes 2359304 | tf_op jit(solution)/shard_map/ppermute | solution.py:199
  522.4 35.2 %collective-permute-start.42 = (bf16[256,3072]{1,0:T(8,128)(2,1)S(1)}, bf16[256,3072]{1,0:T(8,128)(2,1)S(1)}, u32[]{:S(2)}, u32[]{:S(2)}) collective-permute-start(bf16[256,3072]{1,0:T(8,128)(2,1)S(1)} %pad_maximum_fusion.4), channel_id=1, source_target_pairs={{0,4},{4,0},{8,12},{12,8},{16,20},{20,16},{24,28},{28,24},{1,5},{5... | collective-permute-start | bytes 4718600 | tf_op jit(solution)/shard_map/ppermute | solution.py:199
  558.8 60.0 %collective-permute-start.43 = (bf16[768,3072]{1,0:T(8,128)(2,1)}, bf16[768,3072]{1,0:T(8,128)(2,1)S(1)}, u32[]{:S(2)}, u32[]{:S(2)}) collective-permute-start(bf16[768,3072]{1,0:T(8,128)(2,1)} %get-tuple-element.138), channel_id=1, source_target_pairs={{0,1},{1,0},{2,3},{3,2},{4,5},{5,4},{6,7},{7,6},{8,9},{9,8},{10,11... | collective-permute-start | bytes 14155784 | tf_op jit(solution)/shard_map/ppermute | solution.py:199
  566.8 87.1 %collective-permute-start.54 = (bf16[896,512]{1,0:T(8,128)(2,1)S(1)}, bf16[896,512]{1,0:T(8,128)(2,1)}, u32[]{:S(2)}, u32[]{:S(2)}) collective-permute-start(bf16[896,512]{1,0:T(8,128)(2,1)S(1)} %get-tuple-element.149), channel_id=1, source_target_pairs={{0,16},{4,20},{8,24},{12,28},{16,0},{20,4},{24,8},{28,12},{1,17},{... | collective-permute-start | bytes 2752520 | tf_op jit(solution)/shard_map/ppermute | solution.py:199
  566.8 43.5 %collective-permute-start.55 = (bf16[896,512]{1,0:T(8,128)(2,1)S(1)}, bf16[896,512]{1,0:T(8,128)(2,1)S(1)}, u32[]{:S(2)}, u32[]{:S(2)}) collective-permute-start(bf16[896,512]{1,0:T(8,128)(2,1)S(1)} %get-tuple-element.150), channel_id=1, source_target_pairs={{0,8},{4,12},{8,0},{12,4},{16,24},{20,28},{24,16},{28,20},{1,9},{5... | collective-permute-start | bytes 2752520 | tf_op jit(solution)/shard_map/ppermute | solution.py:199
  570.2 40.9 %collective-permute-start.45 = (bf16[256,3072]{1,0:T(8,128)(2,1)S(1)}, bf16[256,3072]{1,0:T(8,128)(2,1)S(1)}, u32[]{:S(2)}, u32[]{:S(2)}) collective-permute-start(bf16[256,3072]{1,0:T(8,128)(2,1)S(1)} %copy-done.91), channel_id=1, source_target_pairs={{0,1},{1,0},{2,3},{3,2},{4,5},{5,4},{6,7},{7,6},{8,9},{9,8},{10,11... | collective-permute-start | bytes 4718600 | tf_op jit(solution)/shard_map/ppermute | solution.py:199
  571.5 42.1 %collective-permute-start.51 = (bf16[256,3072]{1,0:T(8,128)(2,1)S(1)}, bf16[256,3072]{1,0:T(8,128)(2,1)S(1)}, u32[]{:S(2)}, u32[]{:S(2)}) collective-permute-start(bf16[256,3072]{1,0:T(8,128)(2,1)S(1)} %pad_maximum_fusion.5), channel_id=1, source_target_pairs={{0,2},{1,3},{2,0},{3,1},{4,6},{5,7},{6,4},{7,5},{8,10},{9,11},{10,... | collective-permute-start | bytes 4718600 | tf_op jit(solution)/shard_map/ppermute | solution.py:199
  612.9 33.2 %collective-permute-start.46 = (bf16[256,3072]{1,0:T(8,128)(2,1)}, bf16[256,3072]{1,0:T(8,128)(2,1)S(1)}, u32[]{:S(2)}, u32[]{:S(2)}) collective-permute-start(bf16[256,3072]{1,0:T(8,128)(2,1)} %add_convert_fusion), channel_id=1, source_target_pairs={{0,2},{1,3},{2,0},{3,1},{4,6},{5,7},{6,4},{7,5},{8,10},{9,11},{10,... | collective-permute-start | bytes 4718600 | tf_op jit(solution)/shard_map/ppermute | solution.py:199
  617.1 32.3 %collective-permute-start.52 = (bf16[128,3072]{1,0:T(8,128)(2,1)}, bf16[128,3072]{1,0:T(8,128)(2,1)}, u32[]{:S(2)}, u32[]{:S(2)}) collective-permute-start(bf16[128,3072]{1,0:T(8,128)(2,1)} %slice.724), channel_id=1, source_target_pairs={{0,8},{4,12},{8,0},{12,4},{16,24},{20,28},{24,16},{28,20},{1,9},{5... | collective-permute-start | bytes 2359304 | tf_op jit(solution)/shard_map/ppermute | solution.py:199
  617.1 39.9 %collective-permute-start.77 = (bf16[896,512]{1,0:T(8,128)(2,1)S(1)}, bf16[896,512]{1,0:T(8,128)(2,1)}, u32[]{:S(2)}, u32[]{:S(2)}) collective-permute-start(bf16[896,512]{1,0:T(8,128)(2,1)S(1)} %get-tuple-element.160), channel_id=1, source_target_pairs={{0,24},{4,28},{8,16},{12,20},{16,8},{20,12},{24,0},{28,4},{1,25},{... | collective-permute-start | bytes 2752520 | tf_op jit(solution)/shard_map/ppermute | solution.py:199
  646.7 35.5 %collective-permute-start.47 = (bf16[256,3072]{1,0:T(8,128)(2,1)S(1)}, bf16[256,3072]{1,0:T(8,128)(2,1)S(1)}, u32[]{:S(2)}, u32[]{:S(2)}) collective-permute-start(bf16[256,3072]{1,0:T(8,128)(2,1)S(1)} %fusion.3), channel_id=1, source_target_pairs={{0,4},{4,0},{8,12},{12,8},{16,20},{20,16},{24,28},{28,24},{1,5},{5... | collective-permute-start | bytes 4718600 | tf_op jit(solution)/shard_map/ppermute | solution.py:199
  648.6 33.6 %collective-permute-start.44 = (bf16[256,3072]{1,0:T(8,128)(2,1)S(1)}, bf16[256,3072]{1,0:T(8,128)(2,1)S(1)}, u32[]{:S(2)}, u32[]{:S(2)}) collective-permute-start(bf16[256,3072]{1,0:T(8,128)(2,1)S(1)} %slice.992), channel_id=1, source_target_pairs={{0,2},{1,3},{2,0},{3,1},{4,6},{5,7},{6,4},{7,5},{8,10},{9,11},{10,... | collective-permute-start | bytes 4718600 | tf_op jit(solution)/shard_map/ppermute | solution.py:199
  650.7 24.4 %collective-permute-start.53 = (bf16[64,3072]{1,0:T(8,128)(2,1)S(1)}, bf16[64,3072]{1,0:T(8,128)(2,1)S(1)}, u32[]{:S(2)}, u32[]{:S(2)}) collective-permute-start(bf16[64,3072]{1,0:T(8,128)(2,1)S(1)} %slice.726), channel_id=1, source_target_pairs={{0,16},{4,20},{8,24},{12,28},{16,0},{20,4},{24,8},{28,12},{1,17},{... | collective-permute-start | bytes 1179656 | tf_op jit(solution)/shard_map/ppermute | solution.py:199
  675.1 43.3 %collective-permute-start.74 = (bf16[896,512]{1,0:T(8,128)(2,1)}, bf16[896,512]{1,0:T(8,128)(2,1)}, u32[]{:S(2)}, u32[]{:S(2)}) collective-permute-start(bf16[896,512]{1,0:T(8,128)(2,1)} %get-tuple-element.154), channel_id=1, source_target_pairs={{0,4},{4,0},{8,12},{12,8},{16,20},{20,16},{24,28},{28,24},{1,5},{5... | collective-permute-start | bytes 2752520 | tf_op jit(solution)/shard_map/ppermute | solution.py:199
  676.5 42.9 %collective-permute-start.76 = (bf16[896,512]{1,0:T(8,128)(2,1)S(1)}, bf16[896,512]{1,0:T(8,128)(2,1)}, u32[]{:S(2)}, u32[]{:S(2)}) collective-permute-start(bf16[896,512]{1,0:T(8,128)(2,1)S(1)} %get-tuple-element.158), channel_id=1, source_target_pairs={{0,20},{4,16},{8,28},{12,24},{16,4},{20,0},{24,12},{28,8},{1,21},{... | collective-permute-start | bytes 2752520 | tf_op jit(solution)/shard_map/ppermute | solution.py:199
  684.1 49.8 %collective-permute-start.48 = (bf16[128,3072]{1,0:T(8,128)(2,1)}, bf16[128,3072]{1,0:T(8,128)(2,1)}, u32[]{:S(2)}, u32[]{:S(2)}) collective-permute-start(bf16[128,3072]{1,0:T(8,128)(2,1)} %slice.713), channel_id=1, source_target_pairs={{0,8},{4,12},{8,0},{12,4},{16,24},{20,28},{24,16},{28,20},{1,9},{5... | collective-permute-start | bytes 2359304 | tf_op jit(solution)/shard_map/ppermute | solution.py:199
  735.4 19.4 %collective-permute-start.49 = (bf16[64,3072]{1,0:T(8,128)(2,1)S(1)}, bf16[64,3072]{1,0:T(8,128)(2,1)S(1)}, u32[]{:S(2)}, u32[]{:S(2)}) collective-permute-start(bf16[64,3072]{1,0:T(8,128)(2,1)S(1)} %slice.715), channel_id=1, source_target_pairs={{0,16},{4,20},{8,24},{12,28},{16,0},{20,4},{24,8},{28,12},{1,17},{... | collective-permute-start | bytes 1179656 | tf_op jit(solution)/shard_map/ppermute | solution.py:199
  769.0 47.6 %collective-permute-start.75 = (bf16[896,512]{1,0:T(8,128)(2,1)S(1)}, bf16[896,512]{1,0:T(8,128)(2,1)}, u32[]{:S(2)}, u32[]{:S(2)}) collective-permute-start(bf16[896,512]{1,0:T(8,128)(2,1)S(1)} %get-tuple-element.156), channel_id=1, source_target_pairs={{0,12},{4,8},{8,4},{12,0},{16,28},{20,24},{24,20},{28,16},{1,13},{... | collective-permute-start | bytes 2752520 | tf_op jit(solution)/shard_map/ppermute | solution.py:199
  769.1 59.5 %collective-permute-start.78 = (bf16[896,512]{1,0:T(8,128)(2,1)S(1)}, bf16[896,512]{1,0:T(8,128)(2,1)}, u32[]{:S(2)}, u32[]{:S(2)}) collective-permute-start(bf16[896,512]{1,0:T(8,128)(2,1)S(1)} %get-tuple-element.162), channel_id=1, source_target_pairs={{0,28},{4,24},{8,20},{12,16},{16,12},{20,8},{24,4},{28,0},{1,29},{... | collective-permute-start | bytes 2752520 | tf_op jit(solution)/shard_map/ppermute | solution.py:199
  791.9 65.6 %collective-permute-start.58 = (bf16[128,3072]{1,0:T(8,128)(2,1)}, bf16[128,3072]{1,0:T(8,128)(2,1)}, u32[]{:S(2)}, u32[]{:S(2)}) collective-permute-start(bf16[128,3072]{1,0:T(8,128)(2,1)} %pad_maximum_fusion.8), channel_id=1, source_target_pairs={{0,1},{1,0},{2,3},{3,2},{4,5},{5,4},{6,7},{7,6},{8,9},{9,8},{10,11... | collective-permute-start | bytes 2359304 | tf_op jit(solution)/shard_map/ppermute | solution.py:199
  794.0 57.7 %collective-permute-start.60 = (bf16[2,2,384,256]{3,2,0,1:T(8,128)(2,1)}, bf16[2,2,384,256]{3,2,0,1:T(8,128)(2,1)}, u32[]{:S(2)}, u32[]{:S(2)}) collective-permute-start(bf16[2,2,384,256]{3,2,0,1:T(8,128)(2,1)} %bitcast.303), channel_id=1, source_target_pairs={{0,4},{4,0},{8,12},{12,8},{16,20},{20,16},{24,28},{28,24},{1,5},{5... | collective-permute-start | bytes 2359304 | tf_op jit(solution)/shard_map/ppermute | solution.py:199
  796.3 59.2 %collective-permute-start.63 = (bf16[2,2,384,256]{3,2,1,0:T(8,128)(2,1)}, bf16[2,2,384,256]{3,2,1,0:T(8,128)(2,1)}, u32[]{:S(2)}, u32[]{:S(2)}) collective-permute-start(bf16[2,2,384,256]{3,2,1,0:T(8,128)(2,1)} %fusion.54), channel_id=1, source_target_pairs={{0,8},{4,12},{8,0},{12,4},{16,24},{20,28},{24,16},{28,20},{1,9},{5... | collective-permute-start | bytes 2359304 | tf_op jit(solution)/shard_map/ppermute | solution.py:199
  816.9 68.9 %collective-permute-start.66 = (bf16[2,2,2,2,112,512]{5,4,0,1,2,3:T(8,128)(2,1)S(1)}, bf16[2,2,2,2,112,512]{5,4,0,1,2,3:T(8,128)(2,1)S(1)}, u32[]{:S(2)}, u32[]{:S(2)}) collective-permute-start(bf16[2,2,2,2,112,512]{5,4,0,1,2,3:T(8,128)(2,1)S(1)} %bitcast.366), channel_id=1, source_target_pairs={{0,1},{1,0},{2,3},{3,2},{4,5},{5,4},{6,7},{7,6},{8,9},{9,8},{10,11... | collective-permute-start | bytes 5505032 | tf_op jit(solution)/shard_map/ppermute | solution.py:199
  828.7 56.5 %collective-permute-start.71 = (bf16[2,2,384,512]{2,3,0,1:T(8,128)(2,1)S(1)}, bf16[2,2,384,512]{2,3,0,1:T(8,128)(2,1)S(1)}, u32[]{:S(2)}, u32[]{:S(2)}) collective-permute-start(bf16[2,2,384,512]{2,3,0,1:T(8,128)(2,1)S(1)} %fusion.20), channel_id=1, source_target_pairs={{0,4},{4,0},{8,12},{12,8},{16,20},{20,16},{24,28},{28,24},{1,5},{5... | collective-permute-start | bytes 4718600 | tf_op jit(solution)/shard_map/ppermute | solution.py:199
  856.9 25.6 %collective-permute-start.64 = (bf16[2,384,256]{2,1,0:T(8,128)(2,1)S(1)}, bf16[2,384,256]{2,1,0:T(8,128)(2,1)S(1)}, u32[]{:S(2)}, u32[]{:S(2)}) collective-permute-start(bf16[2,384,256]{2,1,0:T(8,128)(2,1)S(1)} %dynamic-slice_bitcast_fusion.4), channel_id=1, source_target_pairs={{0,16},{4,20},{8,24},{12,28},{16,0},{20,4},{24,8},{28,12},{1,17},{... | collective-permute-start | bytes 1179656 | tf_op jit(solution)/shard_map/ppermute | solution.py:199
  858.9 24.8 %collective-permute-start.59 = (bf16[64,3072]{1,0:T(8,128)(2,1)S(1)}, bf16[64,3072]{1,0:T(8,128)(2,1)S(1)}, u32[]{:S(2)}, u32[]{:S(2)}) collective-permute-start(bf16[64,3072]{1,0:T(8,128)(2,1)S(1)} %slice.743), channel_id=1, source_target_pairs={{0,2},{1,3},{2,0},{3,1},{4,6},{5,7},{6,4},{7,5},{8,10},{9,11},{10,... | collective-permute-start | bytes 1179656 | tf_op jit(solution)/shard_map/ppermute | solution.py:199
  870.3 19.2 %collective-permute-start.62 = (bf16[384,256]{1,0:T(8,128)(2,1)S(1)}, bf16[384,256]{1,0:T(8,128)(2,1)S(1)}, u32[]{:S(2)}, u32[]{:S(2)}) collective-permute-start(bf16[384,256]{1,0:T(8,128)(2,1)S(1)} %dynamic-slice_bitcast_fusion.8), channel_id=1, source_target_pairs={{0,16},{4,20},{8,24},{12,28},{16,0},{20,4},{24,8},{28,12},{1,17},{... | collective-permute-start | bytes 589832 | tf_op jit(solution)/shard_map/ppermute | solution.py:199
  (168 other events, 1659.8 us)
